TPU v7x, 128 devices: a whole 4x4x4 slice. The times are simulated.
128 devices in a mesh: seq: 8 (over x, core), head: 16 (over y, z).
Axes of the slice: x: 4, y: 4, z: 4, core: 2. Of those that a mesh axis runs over, the one named last changes fastest.
Arguments:
- tokens: bfloat16 [2048, 4096], P('seq', 'head'), may hold values from -6 to 6
- w_query: bfloat16 [4096, 2048], P(None, 'head'), may hold values from -0.09375 to 0.09375
- w_key: bfloat16 [4096, 2048], P(None, 'head'), may hold values from -0.09375 to 0.09375
- w_value: bfloat16 [4096, 2048], P(None, 'head'), may hold values from -0.09375 to 0.09375
- w_out: bfloat16 [2048, 4096], P('head'), may hold values from -0.125 to 0.125
- grad_out: bfloat16 [2048, 4096], P('seq', 'head'), may hold values from -6 to 6
- state_in: float32 [16, 128, 128], P('head'), may hold values from -384 to 384
Outputs:
- result: bfloat16 [2048, 4096], P('seq', 'head')
- grad_tokens: float32 [2048, 4096], P('seq', 'head')
- grad_wq: float32 [4096, 2048], P('seq', 'head')
- grad_wk: float32 [4096, 2048], P('seq', 'head')
- grad_wv: float32 [4096, 2048], P('seq', 'head')
- grad_wo: float32 [2048, 4096], P('head', 'seq')
- grad_state_in: float32 [16, 128, 128], P('head')
All inputs are finite; a program needn't handle non-finite values.
Results may differ from a plain program's by a relative error of at most 0.018.
Values may be sent and summed in bfloat16 or wider, within the bound.
No kernel may reach another device: no remote copies, remote signals or barrier semaphores. Data moves between devices by JAX's collectives and lax.ppermute only.
A program may use at most 64 MiB of HBM per device.

v0:
```python
import jax
import jax.numpy as jnp
from jax import lax
from jax.sharding import Mesh
from jax.sharding import PartitionSpec as P

DH = 128
BLOCK = 256
HEAD = ("head_0", "head_1")


EPSILON = 1e-06
WIDE_TYPE = jnp.float32
HALF_TYPE = jnp.bfloat16


def laid_out(tiles, dim):
    shape = list(tiles.shape[1:])
    shape[dim] *= tiles.shape[0]
    return jnp.moveaxis(tiles, 0, dim).reshape(shape)


def sent_to_all(shard, axis):
    size = lax.axis_size(axis)
    return lax.all_to_all(
        jnp.broadcast_to(shard[None], (size, *shard.shape)), axis, 0, 0, tiled=True
    )


def collect(shard, axis, dim):
    return laid_out(sent_to_all(shard, axis), dim)


def combined_pairwise(pieces, combine):
    while len(jax.tree.leaves(pieces)[0]) > 1:
        pieces = jax.vmap(combine)(*(pieces[side::2] for side in (0, 1)))
    return pieces[0]


def carried_in(shard, axis, combine, identity, reverse):
    size, index = (lax.axis_size(axis), lax.axis_index(axis))
    passed = jnp.arange(size) > index if reverse else jnp.arange(size) < index

    def kept(part, zero, own):
        part = jnp.where(
            passed.reshape(-1, *(1 for _ in own.shape)),
            part.astype(own.dtype),
            jnp.asarray(zero, own.dtype),
        )
        return part[::-1] if reverse else part

    pieces = sent_to_all(shard.astype(jnp.bfloat16), axis)
    return combined_pairwise(kept(pieces, identity, shard), combine)


def sum_by_axis(shard, axes, dim):
    for axis in axes:
        shard = lax.psum_scatter(shard, axis, scatter_dimension=dim, tiled=True)
    return shard


def over_copies(shard, axis):
    return sent_to_all(shard, axis).astype(jnp.float32).sum(axis=0)


def split_up(shard, dim, size):
    before, after = (shard.shape[:dim], shard.shape[dim + 1 :])
    return jnp.moveaxis(shard.reshape(*before, size, -1, *after), dim, 0)


def sent_and_summed(shard, axis, dim):
    size = lax.axis_size(axis)
    tiles = lax.all_to_all(split_up(shard, dim, size), axis, 0, 0, tiled=True)
    return jnp.sum(tiles.astype(jnp.float32), axis=0)


def side_by_side(arrays, axis, dim, along):
    ends, at = ([], 0)
    for a in arrays[:-1]:
        at += a.shape[along]
        ends.append(at)
    both = jnp.concatenate(arrays, axis=along)
    return tuple(
        jnp.split(lax.psum_scatter(both, axis, scatter_dimension=dim, tiled=True), ends, axis=along)
    )


def causal_mask(width):
    return jnp.tril(jnp.ones((width, width), WIDE_TYPE)) > 0.5


def excl_prefix(states):
    running = jnp.cumsum(states, axis=0)
    return jnp.concatenate([jnp.zeros_like(states), running[:-1]], axis=0)


def excl_suffix(states):
    return jnp.flip(excl_prefix(jnp.flip(states, 0)), 0)


def on_device(tokens, w_query, w_key, w_value, w_out, grad_out, state_in):
    gathered = collect(tokens, HEAD, 1)
    row_count = gathered.shape[0]
    columns = w_query.shape[1]
    heads_here = columns // DH
    blocks = row_count // BLOCK
    block_shape = (blocks, BLOCK, heads_here, DH)
    query = (
        jnp.dot(gathered, w_query, preferred_element_type=WIDE_TYPE)
        .astype(HALF_TYPE)
        .reshape(block_shape)
    )
    keys = (
        jnp.dot(gathered, w_key, preferred_element_type=WIDE_TYPE)
        .astype(HALF_TYPE)
        .reshape(block_shape)
    )
    values = (
        jnp.dot(gathered, w_value, preferred_element_type=WIDE_TYPE)
        .astype(HALF_TYPE)
        .reshape(block_shape)
    )
    block_states = jnp.einsum("cshd,cshe->chde", keys, values, preferred_element_type=WIDE_TYPE)
    own_state = jnp.sum(block_states, axis=0)
    before_dev = carried_in(own_state, "seq", jnp.add, jnp.zeros_like(own_state), False)
    prior_bf = (state_in[None] + before_dev[None] + excl_prefix(block_states)).astype(HALF_TYPE)
    allowed = causal_mask(BLOCK)[None, None]
    scores = jnp.einsum("cthd,cshd->chts", query, keys, preferred_element_type=WIDE_TYPE)
    scores_bf = jnp.where(allowed, scores, 0.0).astype(HALF_TYPE)
    mixed = jnp.einsum("chts,cshd->cthd", scores_bf, values, preferred_element_type=WIDE_TYPE)
    mixed = mixed + jnp.einsum("cthd,chde->cthe", query, prior_bf, preferred_element_type=WIDE_TYPE)
    inv_norm = lax.rsqrt(jnp.mean(mixed * mixed, axis=-1, keepdims=True) + EPSILON)
    normed = (mixed * inv_norm).astype(HALF_TYPE).reshape(row_count, columns)
    out_terms = jnp.dot(normed, w_out, preferred_element_type=WIDE_TYPE)
    result = (
        sum_by_axis(out_terms.astype(jnp.bfloat16), HEAD, 1).astype(jnp.float32).astype(HALF_TYPE)
    )
    grad_full = collect(grad_out, HEAD, 1)
    contract_last = (((1,), (1,)), ((), ()))
    grad_normed = lax.dot_general(
        grad_full, w_out, contract_last, preferred_element_type=WIDE_TYPE
    ).reshape(block_shape)
    grad_mixed = inv_norm * (
        grad_normed
        - mixed * inv_norm * inv_norm * jnp.mean(grad_normed * mixed, axis=-1, keepdims=True)
    )
    grad_mixed = grad_mixed.astype(HALF_TYPE)
    back_states = jnp.einsum("cthd,cthe->chde", query, grad_mixed, preferred_element_type=WIDE_TYPE)
    own_back = jnp.sum(back_states, axis=0)
    after_dev = carried_in(own_back, "seq", jnp.add, jnp.zeros_like(own_back), True)
    grad_state_in = over_copies(own_back.astype(jnp.bfloat16), "seq").astype(jnp.float32)
    later_bf = (after_dev[None] + excl_suffix(back_states)).astype(HALF_TYPE)
    grad_scores = jnp.einsum(
        "cthd,cshd->chts", grad_mixed, values, preferred_element_type=WIDE_TYPE
    )
    grad_scores = jnp.where(allowed, grad_scores, 0.0).astype(HALF_TYPE)
    grad_query = jnp.einsum("chts,cshd->cthd", grad_scores, keys, preferred_element_type=WIDE_TYPE)
    grad_query = grad_query + jnp.einsum(
        "cthe,chde->cthd", grad_mixed, prior_bf, preferred_element_type=WIDE_TYPE
    )
    grad_keys = jnp.einsum("chts,cthd->cshd", grad_scores, query, preferred_element_type=WIDE_TYPE)
    grad_keys = grad_keys + jnp.einsum(
        "cshe,chde->cshd", values, later_bf, preferred_element_type=WIDE_TYPE
    )
    grad_value = jnp.einsum(
        "chts,cthe->cshe", scores_bf, grad_mixed, preferred_element_type=WIDE_TYPE
    )
    grad_value = grad_value + jnp.einsum(
        "cshd,chde->cshe", keys, later_bf, preferred_element_type=WIDE_TYPE
    )
    grad_query = grad_query.astype(HALF_TYPE).reshape(row_count, columns)
    grad_keys = grad_keys.astype(HALF_TYPE).reshape(row_count, columns)
    grad_value = grad_value.astype(HALF_TYPE).reshape(row_count, columns)
    input_terms = lax.dot_general(
        grad_query, w_query, contract_last, preferred_element_type=WIDE_TYPE
    )
    input_terms = input_terms + lax.dot_general(
        grad_keys, w_key, contract_last, preferred_element_type=WIDE_TYPE
    )
    input_terms = input_terms + lax.dot_general(
        grad_value, w_value, contract_last, preferred_element_type=WIDE_TYPE
    )
    grad_tokens = sent_and_summed(input_terms.astype(jnp.bfloat16), HEAD, 1)
    contract_first = (((0,), (0,)), ((), ()))
    term_wq = lax.dot_general(
        gathered, grad_query, contract_first, preferred_element_type=WIDE_TYPE
    )
    term_wk = lax.dot_general(gathered, grad_keys, contract_first, preferred_element_type=WIDE_TYPE)
    term_wv = lax.dot_general(
        gathered, grad_value, contract_first, preferred_element_type=WIDE_TYPE
    )
    grad_wq, grad_wk, grad_wv = tuple(
        (
            part.astype(jnp.float32)
            for part in side_by_side(
                (
                    term_wq.astype(jnp.bfloat16),
                    term_wk.astype(jnp.bfloat16),
                    term_wv.astype(jnp.bfloat16),
                ),
                "seq",
                0,
                1,
            )
        )
    )
    term_wo = lax.dot_general(normed, grad_full, contract_first, preferred_element_type=WIDE_TYPE)
    grad_wo = sent_and_summed(term_wo.astype(jnp.bfloat16), "seq", 1)
    return (result, grad_tokens, grad_wq, grad_wk, grad_wv, grad_wo, grad_state_in)


def solution(mesh):
    torus = Mesh(mesh.devices.reshape(mesh.shape["seq"], 4, 4), ("seq", "head_0", "head_1"))
    placed = (
        P("seq", HEAD),
        P(None, HEAD),
        P(None, HEAD),
        P(None, HEAD),
        P(HEAD, None),
        P("seq", HEAD),
        P(HEAD, None, None),
    )
    return jax.shard_map(
        on_device,
        mesh=torus,
        in_specs=placed,
        out_specs=(
            P("seq", HEAD),
            P("seq", HEAD),
            P("seq", HEAD),
            P("seq", HEAD),
            P("seq", HEAD),
            P(HEAD, "seq"),
            P(HEAD, None, None),
        ),
        check_vma=False,
    )
```

profile of v0, /device:TPU:0, one launch (start us, length us, event | category | flops | bytes accessed | tf_op | source)
XLA Modules:
  0.0 196.5 jit_solution(810155403460694228)
XLA Ops:
  8.5 36.3 %all_to_all.31 = bf16[16,256,256]{1,2,0:T(8,128)(2,1)S(1)} all-to-all(bf16[16,256,256]{1,2,0:T(8,128)(2,1)S(1)} %broadcast_in_dim.37), channel_id=1, replica_groups=mesh['seq'=8,'head_0'=4,'head_1'=4] {'head_0','head_1'}, dimensions={0} | all-to-all | bytes 4194304 | tf_op jit(solution)/shard_map/all_to_all | solution.py:25
  47.7 4.3 %all-to-all-start.1 = ((bf16[8,1,128,128]{3,2,1,0:T(8,128)(2,1)}), bf16[8,1,128,128]{3,2,1,0:T(8,128)(2,1)S(1)}, u32[]{:S(2)}, u32[]{:S(2)}) async-start(bf16[8,1,128,128]{3,2,1,0:T(8,128)(2,1)} %broadcast_in_dim.68), calls=%async_computation.1 | async-start | bytes 524288 | tf_op jit(solution)/shard_map/all_to_all | solution.py:25
  52.0 1.7 copy.23
  53.7 5.9 %all-to-all-done.1 = bf16[8,1,128,128]{3,2,1,0:T(8,128)(2,1)S(1)} async-done(((bf16[8,1,128,128]{3,2,1,0:T(8,128)(2,1)}), bf16[8,1,128,128]{3,2,1,0:T(8,128)(2,1)S(1)}, u32[]{:S(2)}, u32[]{:S(2)}) %all-to-all-start.1) | async-done | bytes 262176 | tf_op jit(solution)/shard_map/all_to_all | solution.py:25
  59.6 2.5 %broadcast_in_dim.70 = bf16[16,256,256]{1,2,0:T(8,128)(2,1)} broadcast(bf16[256,256]{0,1:T(8,128)(2,1)} %copy.23), dimensions={1,2} | broadcast | bytes 2228224 | tf_op jit(solution)/shard_map/broadcast_in_dim | solution.py:26
  62.1 4.5 %all-to-all-start.2 = ((bf16[16,256,256]{1,2,0:T(8,128)(2,1)}), bf16[16,256,256]{1,2,0:T(8,128)(2,1)}, u32[]{:S(2)}, u32[]{:S(2)}) async-start(bf16[16,256,256]{1,2,0:T(8,128)(2,1)} %broadcast_in_dim.70), calls=%async_computation.4 | async-start | bytes 4194304 | tf_op jit(solution)/shard_map/all_to_all | solution.py:25
  66.7 2.0 %convolution_convert_fusion.6 = bf16[256,128]{1,0:T(8,128)(2,1)S(1)} fusion(bf16[256,4096]{0,1:T(8,128)(2,1)S(1)} %bitcast.113, bf16[4096,128]{1,0:T(8,128)(2,1)} %param.8), kind=kOutput, calls=%fused_computation.26 | convolution fusion | flops 268468224 | bytes 3211264 | tf_op jit(solution)/shard_map/dot_general | solution.py:109
  70.2 26.6 %all-to-all-done.2 = bf16[16,256,256]{1,2,0:T(8,128)(2,1)} async-done(((bf16[16,256,256]{1,2,0:T(8,128)(2,1)}), bf16[16,256,256]{1,2,0:T(8,128)(2,1)}, u32[]{:S(2)}, u32[]{:S(2)}) %all-to-all-start.2) | async-done | bytes 2097184 | tf_op jit(solution)/shard_map/all_to_all | solution.py:25
  96.8 2.7 %multiply_reduce_fusion = (f32[256]{0:T(256)S(1)}, f32[256]{0:T(256)S(1)}, f32[1,256,1,128]{1,3,2,0:T(8,128)}) fusion(f32[1,256,1,128]{1,3,2,0:T(8,128)S(1)} %fusion.6, bf16[128,4096]{1,0:T(8,128)(2,1)S(1)} %copy-done, bf16[256,4096]{0,1:T(8,128)(2,1)} %bitcast.10), kind=kOutput, calls=%fused_computation.49 | convolution fusion | flops 268566016 | bytes 3409920 | tf_op jit(solution)/shard_map/dot_general | solution.py:140
  99.5 2.1 %convolution_convert_fusion = bf16[256,4096]{1,0:T(8,128)(2,1)} fusion(bf16[128,4096]{1,0:T(8,128)(2,1)S(1)} %copy-done, f32[1,256,1,128]{1,3,2,0:T(8,128)S(1)} %fusion.6, f32[256]{0:T(256)S(1)} %add_rsqrt_fusion), kind=kOutput, calls=%fused_computation.2 | convolution fusion | flops 269549568 | bytes 3277824 | tf_op jit(solution)/shard_map/dot_general | solution.py:134
  103.5 4.0 %all-to-all-start.3 = ((bf16[8,1,128,128]{3,2,1,0:T(8,128)(2,1)}), bf16[8,1,128,128]{3,2,1,0:T(8,128)(2,1)}, u32[]{:S(2)}, u32[]{:S(2)}) async-start(bf16[8,1,128,128]{3,2,1,0:T(8,128)(2,1)} %broadcast_in_dim.72), calls=%async_computation.5 | async-start | bytes 524288 | tf_op jit(solution)/shard_map/all_to_all | solution.py:25
  110.2 1.8 fusion.1
  112.0 3.1 %all-to-all-done.3 = bf16[8,1,128,128]{3,2,1,0:T(8,128)(2,1)} async-done(((bf16[8,1,128,128]{3,2,1,0:T(8,128)(2,1)}), bf16[8,1,128,128]{3,2,1,0:T(8,128)(2,1)}, u32[]{:S(2)}, u32[]{:S(2)}) %all-to-all-start.3) | async-done | bytes 262176 | tf_op jit(solution)/shard_map/all_to_all | solution.py:25
  115.1 1.7 convert_reduce_fusion.2
  119.7 1.8 pad_maximum_fusion
  121.6 2.4 %convolution_convert_fusion.1 = bf16[128,4096]{1,0:T(8,128)(2,1)S(1)} fusion(bf16[256,4096]{0,1:T(8,128)(2,1)} %bitcast.10, f32[1,256,1,128]{1,3,2,0:T(8,128)S(1)} %fusion.6, f32[256]{0:T(256)S(1)} %add_rsqrt_fusion), kind=kOutput, calls=%fused_computation.4 | convolution fusion | flops 269025280 | bytes 3277824 | tf_op jit(solution)/shard_map/dot_general | solution.py:207
  124.0 1.2 copy.34
  125.2 4.3 %all-to-all-start.5 = ((bf16[8,128,512]{2,1,0:T(8,128)(2,1)}), bf16[8,128,512]{2,1,0:T(8,128)(2,1)}, u32[]{:S(2)}, u32[]{:S(2)}) async-start(bf16[8,128,512]{2,1,0:T(8,128)(2,1)} %bitcast.110), calls=%async_computation.8 | async-start | bytes 2097152 | tf_op jit(solution)/shard_map/all_to_all | solution.py:73
  132.6 1.6 copy.33
  134.2 12.7 %all-to-all-done.5 = bf16[8,128,512]{2,1,0:T(8,128)(2,1)} async-done(((bf16[8,128,512]{2,1,0:T(8,128)(2,1)}), bf16[8,128,512]{2,1,0:T(8,128)(2,1)}, u32[]{:S(2)}, u32[]{:S(2)}) %all-to-all-start.5) | async-done | bytes 1048608 | tf_op jit(solution)/shard_map/all_to_all | solution.py:73
  146.9 3.7 %all-to-all-start.4 = ((bf16[16,256,256]{2,1,0:T(8,128)(2,1)}), bf16[16,256,256]{2,1,0:T(8,128)(2,1)S(1)}, u32[]{:S(2)}, u32[]{:S(2)}) async-start(bf16[16,256,256]{2,1,0:T(8,128)(2,1)} %bitcast.108), calls=%async_computation.6 | async-start | bytes 4194304 | tf_op jit(solution)/shard_map/all_to_all | solution.py:73
  151.4 2.1 %convert_reduce_fusion.1 = f32[128,512]{1,0:T(8,128)} fusion(bf16[8,128,512]{2,1,0:T(8,128)(2,1)} %all-to-all-done.5), kind=kLoop, calls=%fused_computation.14 | loop fusion | flops 983040 | bytes 1310720 | tf_op jit(solution)/shard_map/reduce_sum | solution.py:74
  153.5 26.7 %all-to-all-done.4 = bf16[16,256,256]{2,1,0:T(8,128)(2,1)S(1)} async-done(((bf16[16,256,256]{2,1,0:T(8,128)(2,1)}), bf16[16,256,256]{2,1,0:T(8,128)(2,1)S(1)}, u32[]{:S(2)}, u32[]{:S(2)}) %all-to-all-start.4) | async-done | bytes 2097184 | tf_op jit(solution)/shard_map/all_to_all | solution.py:73
  184.8 5.2 %reduce-scatter.6.cloned.1.call-done = bf16[256,256]{1,0:T(8,128)(2,1)} async-done(((bf16[256,1024]{1,0:T(8,128)(2,1)}), bf16[256,256]{1,0:T(8,128)(2,1)}) %reduce-scatter.6.cloned.1.call-update) | async-done | bytes 131088 | tf_op jit(solution)/shard_map/reduce_scatter | solution.py:58
  (83 shorter events, 21.6 us)
Async XLA Ops:
  7.2 89.6 %copy-start = (bf16[128,4096]{1,0:T(8,128)(2,1)S(1)}, bf16[128,4096]{1,0:T(8,128)(2,1)}, u32[]{:S(2)}) copy-start(bf16[128,4096]{1,0:T(8,128)(2,1)} %param.11) | copy-start | bytes 3145732
  8.5 36.3 %copy-start.1 = (bf16[4096,128]{1,0:T(8,128)(2,1)S(1)}, bf16[4096,128]{1,0:T(8,128)(2,1)}, u32[]{:S(2)}) copy-start(bf16[4096,128]{1,0:T(8,128)(2,1)} %param.9) | copy-start | bytes 3145732
  44.8 1.2 copy-start.3
  47.7 11.8 %all-to-all-start.1 = ((bf16[8,1,128,128]{3,2,1,0:T(8,128)(2,1)}), bf16[8,1,128,128]{3,2,1,0:T(8,128)(2,1)S(1)}, u32[]{:S(2)}, u32[]{:S(2)}) async-start(bf16[8,1,128,128]{3,2,1,0:T(8,128)(2,1)} %broadcast_in_dim.68), calls=%async_computation.1 | async-start | bytes 524288 | tf_op jit(solution)/shard_map/all_to_all | solution.py:25
  59.6 2.5 %copy-start.7 = (bf16[8,1,128,128]{3,2,1,0:T(8,128)(2,1)}, bf16[8,1,128,128]{3,2,1,0:T(8,128)(2,1)S(1)}, u32[]{:S(2)}) copy-start(bf16[8,1,128,128]{3,2,1,0:T(8,128)(2,1)S(1)} %all-to-all-done.1) | copy-start | bytes 786436
  62.1 34.7 %all-to-all-start.2 = ((bf16[16,256,256]{1,2,0:T(8,128)(2,1)}), bf16[16,256,256]{1,2,0:T(8,128)(2,1)}, u32[]{:S(2)}, u32[]{:S(2)}) async-start(bf16[16,256,256]{1,2,0:T(8,128)(2,1)} %broadcast_in_dim.70), calls=%async_computation.4 | async-start | bytes 4194304 | tf_op jit(solution)/shard_map/all_to_all | solution.py:25
  66.6 84.2 %reduce-scatter.4.cloned.1.call-start = ((), (), s32[]{:S(2)}) async-start(), calls=%async_computation.9 | async-start | bytes 2621440 | tf_op jit(solution)/shard_map/reduce_scatter | solution.py:58
  66.6 2.3 %copy-start.8 = (bf16[8,1,128,128]{3,2,1,0:T(8,128)(2,1)S(1)}, bf16[8,1,128,128]{3,2,1,0:T(8,128)(2,1)}, u32[]{:S(2)}) copy-start(bf16[8,1,128,128]{3,2,1,0:T(8,128)(2,1)} %copy-done.7) | copy-start | bytes 786436
  66.7 2.4 %copy-start.16 = (f32[1,128,128]{2,1,0:T(8,128)S(1)}, f32[1,128,128]{2,1,0:T(8,128)}, u32[]{:S(2)}) copy-start(f32[1,128,128]{2,1,0:T(8,128)} %param.13) | copy-start | bytes 196612
  68.9 1.0 copy-start.11
  103.5 11.6 %all-to-all-start.3 = ((bf16[8,1,128,128]{3,2,1,0:T(8,128)(2,1)}), bf16[8,1,128,128]{3,2,1,0:T(8,128)(2,1)}, u32[]{:S(2)}, u32[]{:S(2)}) async-start(bf16[8,1,128,128]{3,2,1,0:T(8,128)(2,1)} %broadcast_in_dim.72), calls=%async_computation.5 | async-start | bytes 524288 | tf_op jit(solution)/shard_map/all_to_all | solution.py:25
  107.5 73.7 %reduce-scatter.8.cloned.1.call-start = ((), (), s32[]{:S(2)}) async-start(), calls=%async_computation.11 | async-start | bytes 3538944 | tf_op jit(solution)/shard_map/reduce_scatter | solution.py:84
  108.7 0.7 copy-start.13
  109.6 0.6 copy-start.9
  115.1 2.2 %copy-start.12 = (bf16[256,256]{1,0:T(8,128)(2,1)S(1)}, bf16[256,256]{1,0:T(8,128)(2,1)}, u32[]{:S(2)}) copy-start(bf16[256,256]{1,0:T(8,128)(2,1)} %copy-done.11) | copy-start | bytes 393220
  115.1 2.4 %copy-start.14 = (bf16[256,256]{1,0:T(8,128)(2,1)S(1)}, bf16[256,256]{1,0:T(8,128)(2,1)}, u32[]{:S(2)}) copy-start(bf16[256,256]{1,0:T(8,128)(2,1)} %copy-done.13) | copy-start | bytes 393220
  118.5 1.2 copy-start.6
  124.0 5.4 %copy-start.5 = (bf16[4096,128]{1,0:T(8,128)(2,1)S(1)}, bf16[4096,128]{1,0:T(8,128)(2,1)}, u32[]{:S(2)}) copy-start(bf16[4096,128]{1,0:T(8,128)(2,1)} %param.8) | copy-start | bytes 3145732
  124.0 5.4 %copy-start.10 = (bf16[256,128]{0,1:T(8,128)(2,1)S(1)}, bf16[256,128]{0,1:T(8,128)(2,1)}, u32[]{:S(2)}) copy-start(bf16[256,128]{0,1:T(8,128)(2,1)} %copy-done.9) | copy-start | bytes 196612
  125.2 21.8 %all-to-all-start.5 = ((bf16[8,128,512]{2,1,0:T(8,128)(2,1)}), bf16[8,128,512]{2,1,0:T(8,128)(2,1)}, u32[]{:S(2)}, u32[]{:S(2)}) async-start(bf16[8,128,512]{2,1,0:T(8,128)(2,1)} %bitcast.110), calls=%async_computation.8 | async-start | bytes 2097152 | tf_op jit(solution)/shard_map/all_to_all | solution.py:73
  129.4 1.2 copy-start.2
  130.7 1.2 copy-start.4
  146.9 33.3 %all-to-all-start.4 = ((bf16[16,256,256]{2,1,0:T(8,128)(2,1)}), bf16[16,256,256]{2,1,0:T(8,128)(2,1)S(1)}, u32[]{:S(2)}, u32[]{:S(2)}) async-start(bf16[16,256,256]{2,1,0:T(8,128)(2,1)} %bitcast.108), calls=%async_computation.6 | async-start | bytes 4194304 | tf_op jit(solution)/shard_map/all_to_all | solution.py:73
  150.7 39.3 %reduce-scatter.6.cloned.1.call-start = ((), (), s32[]{:S(2)}) async-start(), calls=%async_computation.10 | async-start | bytes 655360 | tf_op jit(solution)/shard_map/reduce_scatter | solution.py:58
  (1 other events, 0.6 us)
Sparse Core Ops, SparseCore 0:
  101.7 26.4 reduce-scatter.3
  130.8 38.8 reduce-scatter.7
  172.8 17.2 reduce-scatter.5
where the time goes:
time: 198 us; the launch traced here: 197 us
  waiting for transfers between devices  80.9 us (41%)
  blocking collectives  36.3 us (18%)
  starting transfers between devices  20.9 us (11%)
  matrix products  19.3 us (10%)
  local copies, waits for them, and re-layouts  16 us (8%)
  between operations  14.1 us (7%)
  other arithmetic  8.94 us (5%)
    all_to_all x2, waiting for transfers between devices, sent_and_summed(): tiles = lax.all_to_all(split_up(shard, dim, size), axis, 0, 0, tiled=True)  39.4 us
    all_to_all x1, blocking collectives, sent_to_all(): lax.all_to_all(jnp.broadcast_to(shard[None], (size, *shard.shape)), axis,...  36.3 us
    all_to_all x3, waiting for transfers between devices, sent_to_all(): lax.all_to_all(jnp.broadcast_to(shard[None], (size, *shard.shape)), axis,...  35.6 us
    all_to_all x3, starting transfers between devices, sent_to_all(): lax.all_to_all(jnp.broadcast_to(shard[None], (size, *shard.shape)), axis,...  12.8 us
    unnamed x39, local copies, waits for them, and re-layouts  9.05 us
    all_to_all x2, starting transfers between devices, sent_and_summed(): tiles = lax.all_to_all(split_up(shard, dim, size), axis, 0, 0, tiled=True)  7.97 us
    reduce_scatter x2, waiting for transfers between devices, sum_by_axis(): shard = lax.psum_scatter(shard, axis, scatter_dimension=dim, tiled=True)  5.18 us
    broadcast_in_dim x4, local copies, waits for them, and re-layouts, sent_to_all(): jnp.broadcast_to(shard[None], (size, *shard.shape))  4.22 us
  transfers between devices with their start and end apart: 8, of which 6 were waited for; matrix products, arithmetic and copies ran while one was open for 15% of the time, Pallas kernels for 0%

commit v1 on v0

v1 whole, which is shorter than its diff:
```python
import jax
import jax.numpy as jnp
from jax import lax
from jax.experimental import pallas as pl
from jax.experimental.pallas import tpu as pltpu
from jax.sharding import Mesh
from jax.sharding import PartitionSpec as P

SEQ = ("x", "core")
HEAD = ("y", "z")
PLANE = ("core", "y", "z")
SIDE = 4
EPSILON = 1e-06
WIDE = jnp.float32
HALF = jnp.bfloat16

NN = (((1,), (0,)), ((), ()))
NT = (((1,), (1,)), ((), ()))
TN = (((0,), (0,)), ((), ()))


def mm(a, b, dims):
    return lax.dot_general(a, b, dims, preferred_element_type=WIDE)


def plane_pairs(phase, shift):
    pairs = []
    for core in range(2):
        for y in range(SIDE):
            for z in range(SIDE):
                along_y = core == phase
                ty = (y + shift) % SIDE if along_y else y
                tz = z if along_y else (z + shift) % SIDE
                pairs.append(((core * SIDE + y) * SIDE + z, (core * SIDE + ty) * SIDE + tz))
    return pairs


def plane_shift(a, phase, shift):
    return lax.ppermute(a, PLANE, plane_pairs(phase, shift))


def x_shift(a, shift):
    return lax.ppermute(a, "x", [(i, (i + shift) % SIDE) for i in range(SIDE)])


def core_swap(a):
    return lax.ppermute(a, "core", [(0, 1), (1, 0)])


def block_table():
    core, y, z = (lax.axis_index(n) for n in PLANE)
    at = jnp.arange(SIDE * SIDE, dtype=jnp.int32)
    d2, d1 = at // SIDE, at % SIDE
    dy = jnp.where(core == 0, d1, d2)
    dz = jnp.where(core == 0, d2, d1)
    return ((y - dy) % SIDE) * SIDE + (z - dz) % SIDE


def order_weights_kernel(table, q, k, v, o, qkv_out, o_out):
    n = q.shape[1]
    qkv_out[:, :n] = q[...]
    qkv_out[:, n : 2 * n] = k[...]
    qkv_out[:, 2 * n :] = v[...]
    o_out[...] = o[...].T


def order_weights(table, w_query, w_key, w_value, w_out):
    rows, n = w_query.shape
    blocks = SIDE * SIDE
    step = rows // blocks
    tall = pl.BlockSpec((step, n), lambda i, t: (t[i], 0))
    return pl.pallas_call(
        order_weights_kernel,
        out_shape=(
            jax.ShapeDtypeStruct((rows, 3 * n), HALF),
            jax.ShapeDtypeStruct((rows, n), HALF),
        ),
        grid_spec=pltpu.PrefetchScalarGridSpec(
            num_scalar_prefetch=1,
            grid=(blocks,),
            in_specs=[tall, tall, tall, pl.BlockSpec((n, step), lambda i, t: (0, t[i]))],
            out_specs=[
                pl.BlockSpec((step, 3 * n), lambda i, t: (i, 0)),
                pl.BlockSpec((step, n), lambda i, t: (i, 0)),
            ],
        ),
        cost_estimate=pl.CostEstimate(
            flops=0, bytes_accessed=16 * rows * n, transcendentals=0
        ),
        name="order_weights",
    )(table, w_query, w_key, w_value, w_out)


def place_blocks_kernel(table, a0, a1, a2, a3, out, sem):
    step = a0.shape[0] // SIDE
    copies = []
    for d2, ref in enumerate((a0, a1, a2, a3)):
        for d1 in range(SIDE):
            to = pl.multiple_of(table[d2 * SIDE + d1] * step, step)
            copies.append(
                pltpu.make_async_copy(
                    ref.at[pl.ds(d1 * step, step)], out.at[pl.ds(to, step)], sem.at[d2 * SIDE + d1]
                )
            )
    for copy in copies:
        copy.start()
    for copy in copies:
        copy.wait()


def place_blocks(table, parts):
    rows, n = parts[0].shape
    any_spec = pl.BlockSpec(memory_space=pl.ANY)
    return pl.pallas_call(
        place_blocks_kernel,
        out_shape=jax.ShapeDtypeStruct((SIDE * rows, n), parts[0].dtype),
        in_specs=[pl.BlockSpec(memory_space=pltpu.SMEM)] + [any_spec] * SIDE,
        out_specs=any_spec,
        scratch_shapes=[pltpu.SemaphoreType.DMA((SIDE * SIDE,))],
        cost_estimate=pl.CostEstimate(
            flops=0, bytes_accessed=16 * rows * n, transcendentals=0
        ),
        name="place_blocks",
    )(table, *parts)


def spread_phase1(a):
    got = [plane_shift(a, 0, d) for d in range(1, SIDE)]
    return jnp.concatenate([a] + got, axis=0)


def spread_phase2(a):
    return [a] + [plane_shift(a, 1, d) for d in range(1, SIDE)]


def total(parts):
    acc = parts[0].astype(WIDE)
    for p in parts[1:]:
        acc = acc + p.astype(WIDE)
    return acc


def gathered_sum(terms):
    got = [plane_shift(t, 1, -d) for d, t in enumerate(terms) if d]
    mine = total([terms[0]] + got).astype(HALF)
    step = mine.shape[0] // SIDE
    parts = [mine[d * step : (d + 1) * step] for d in range(SIDE)]
    got = [plane_shift(p, 0, -d) for d, p in enumerate(parts) if d]
    return total([parts[0]] + got)


def pair_and_others(own):
    other = core_swap(own)
    pair = (own.astype(WIDE) + other.astype(WIDE)).astype(HALF)
    return other, [pair] + [x_shift(pair, d) for d in range(1, SIDE)]


def masked_sum(first, parts, keep):
    acc = first
    for part, k in zip(parts, keep):
        acc = acc + jnp.where(k, part.astype(WIDE), 0.0)
    return acc


def on_device(tokens, w_query, w_key, w_value, w_out, grad_out, state_in):
    x, core = lax.axis_index("x"), lax.axis_index("core")
    dh = w_query.shape[1]
    rows = tokens.shape[0]
    table = block_table()

    t1 = spread_phase1(tokens.T)
    g1 = spread_phase1(grad_out.T)
    w_qkv, w_o = order_weights(table, w_query, w_key, w_value, w_out)
    t_parts = spread_phase2(t1)
    g_parts = spread_phase2(g1)
    step = t1.shape[0]
    wq_parts = [w_qkv[d * step : (d + 1) * step] for d in range(SIDE)]
    wo_parts = [w_o[d * step : (d + 1) * step] for d in range(SIDE)]

    qkv = sum(mm(t, w, TN) for t, w in zip(t_parts, wq_parts)).astype(HALF)
    query, keys, values = (qkv[:, i * dh : (i + 1) * dh] for i in range(3))

    own_state = mm(keys, values, TN).astype(HALF)
    other, pairs = pair_and_others(own_state)
    prior = masked_sum(
        state_in[0], [other] + pairs[1:], [core == 1] + [x >= d for d in range(1, SIDE)]
    ).astype(HALF)

    allowed = jnp.tril(jnp.ones((rows, rows), jnp.bool_))
    scores = jnp.where(allowed, mm(query, keys, NT), 0.0).astype(HALF)
    mixed = mm(scores, values, NN) + mm(query, prior, NN)
    inv_norm = lax.rsqrt(jnp.mean(mixed * mixed, axis=-1, keepdims=True) + EPSILON)
    normed = (mixed * inv_norm).astype(HALF)

    grad_normed = sum(mm(g, w, TN) for g, w in zip(g_parts, wo_parts))
    grad_mixed = inv_norm * (
        grad_normed
        - mixed * inv_norm * inv_norm * jnp.mean(grad_normed * mixed, axis=-1, keepdims=True)
    )
    grad_mixed = grad_mixed.astype(HALF)
    own_back = mm(query, grad_mixed, TN).astype(HALF)
    other_back, back_pairs = pair_and_others(own_back)
    later = masked_sum(
        jnp.zeros((dh, dh), WIDE),
        [other_back] + back_pairs[1:],
        [core == 0] + [x < d for d in range(1, SIDE)],
    ).astype(HALF)
    grad_state = jnp.zeros((dh, dh), WIDE)
    for chip in range(SIDE):
        part = jnp.zeros((dh, dh), HALF)
        for d, p in enumerate(back_pairs):
            part = jnp.where((x - d) % SIDE == chip, p, part)
        grad_state = grad_state + part.astype(WIDE)

    out_terms = [mm(w, normed, NT).astype(HALF) for w in wo_parts]
    result = gathered_sum(out_terms).astype(HALF).T

    grad_scores = jnp.where(allowed, mm(grad_mixed, values, NT), 0.0).astype(HALF)
    grad_query = (mm(grad_scores, keys, NN) + mm(grad_mixed, prior, NT)).astype(HALF)
    tokens_all = place_blocks(table, t_parts)
    grads_all = place_blocks(table, g_parts)
    early = jnp.concatenate(
        [mm(tokens_all, grad_query, NN).astype(HALF), mm(grads_all, normed, NN).astype(HALF)],
        axis=1,
    )
    early = lax.psum_scatter(early, SEQ, scatter_dimension=0, tiled=True)

    grad_keys = (mm(grad_scores, query, TN) + mm(values, later, NT)).astype(HALF)
    grad_values = (mm(scores, grad_mixed, TN) + mm(keys, later, NN)).astype(HALF)
    grad_kv = jnp.concatenate([grad_keys, grad_values], axis=1)
    late = mm(tokens_all, grad_kv, NN).astype(HALF)
    late = lax.psum_scatter(late, SEQ, scatter_dimension=0, tiled=True)

    grad_qkv = jnp.concatenate([grad_query, grad_kv], axis=1)
    in_terms = [mm(w, grad_qkv, NT).astype(HALF) for w in wq_parts]
    grad_tokens = gathered_sum(in_terms).T

    early, late = early.astype(WIDE), late.astype(WIDE)
    return (
        result,
        grad_tokens,
        early[:, :dh],
        late[:, :dh],
        late[:, dh:],
        early[:, dh:].T,
        grad_state[None],
    )


def solution(mesh):
    sizes = (SIDE, mesh.shape["seq"] // SIDE, SIDE, SIDE)
    torus = Mesh(mesh.devices.reshape(sizes), SEQ + HEAD)
    seq_head = P(SEQ, HEAD)
    column = P(None, HEAD)
    return jax.shard_map(
        on_device,
        mesh=torus,
        in_specs=(seq_head, column, column, column, P(HEAD, None), seq_head, P(HEAD, None, None)),
        out_specs=(
            seq_head,
            seq_head,
            seq_head,
            seq_head,
            seq_head,
            P(HEAD, SEQ),
            P(HEAD, None, None),
        ),
        check_vma=False,
    )
```

time: 198 us -> 283 us (1.43)
  Pallas kernels: 0 us -> 142 us
  waiting for transfers between devices: 80.9 us -> 43.9 us
  blocking collectives: 36.3 us -> 0 us
  starting transfers between devices: 20.9 us -> 44.3 us
  other arithmetic: 8.94 us -> 4.09 us
    pallas_call x0 -> x3, Pallas kernels: none -> 142 us  [the longest x2 131 us: place_blocks(): pl.pallas_call(place_blocks_kernel, out_shape=jax.ShapeDtypeStruct((SIDE...]
    all_to_all x5 -> x0, waiting for transfers between devices: 75 us -> none  [the longest x2 39.4 us: sent_and_summed(): tiles = lax.all_to_all(split_up(shard, dim, size), axis, 0, 0, tiled=True)]
    ppermute x0 -> x32, starting transfers between devices: none -> 44.2 us  [the longest x24 35.6 us: plane_shift(): return lax.ppermute(a, PLANE, plane_pairs(phase, shift))]
    all_to_all x1 -> x0, blocking collectives: 36.3 us -> none  [sent_to_all(): lax.all_to_all(jnp.broadcast_to(shard[None], (size, *shard.shape)), axis,...]
    ppermute x0 -> x32, waiting for transfers between devices: none -> 35.1 us  [the longest x24 31 us: plane_shift(): return lax.ppermute(a, PLANE, plane_pairs(phase, shift))]
    all_to_all x5 -> x0, starting transfers between devices: 20.8 us -> none  [the longest x3 12.8 us: sent_to_all(): lax.all_to_all(jnp.broadcast_to(shard[None], (size, *shard.shape)), axis,...]
    reduce_sum x3 -> x0, other arithmetic: 4.83 us -> none  [the longest x2 3.09 us: sent_and_summed(): return jnp.sum(tiles.astype(jnp.float32), axis=0)]
    broadcast_in_dim x4 -> x0, local copies, waits for them, and re-layouts: 4.22 us -> none  [sent_to_all(): jnp.broadcast_to(shard[None], (size, *shard.shape))]
  transfers between devices with their start and end apart: 8 -> 34, of which waited for: 6 -> 14; matrix products, arithmetic and copies ran while one was open for 15% -> 8% of each run, Pallas kernels for 0% -> 50%
where the time goes in v1:
time: 283 us; the launch traced here: 282 us
  Pallas kernels  142 us (50%)
  starting transfers between devices  44.3 us (16%)
  waiting for transfers between devices  43.9 us (16%)
  matrix products  18.7 us (7%)
  between operations  14.9 us (5%)
  local copies, waits for them, and re-layouts  13.8 us (5%)
  other arithmetic  4.09 us (1%)
    pallas_call x2, Pallas kernels, place_blocks(): pl.pallas_call(place_blocks_kernel, out_shape=jax.ShapeDtypeStruct((SIDE...  131 us
    ppermute x24, starting transfers between devices, plane_shift(): return lax.ppermute(a, PLANE, plane_pairs(phase, shift))  35.6 us
    ppermute x24, waiting for transfers between devices, plane_shift(): return lax.ppermute(a, PLANE, plane_pairs(phase, shift))  31 us
    dot_general x31, matrix products, mm(): return lax.dot_general(a, b, dims, preferred_element_type=WIDE)  18.7 us
    pallas_call x1, Pallas kernels, order_weights(): pl.pallas_call(order_weights_kernel, out_shape=(jax.ShapeDtypeStruct((row...  10.9 us
    unnamed x81, local copies, waits for them, and re-layouts  10.3 us
    reduce_scatter x1, waiting for transfers between devices, on_device(): late = lax.psum_scatter(late, SEQ, scatter_dimension=0, tiled=True)  8.83 us
    ppermute x6, starting transfers between devices, x_shift(): return lax.ppermute(a, 'x', [(i, (i + shift) % SIDE) for i in range(SIDE)])  8.48 us
  transfers between devices with their start and end apart: 34, of which 14 were waited for; matrix products, arithmetic and copies ran while one was open for 8% of the time, Pallas kernels for 50%

profile of v1, /device:TPU:0, one launch (start us, length us, event | category | flops | bytes accessed | tf_op | source)
XLA Modules:
  0.0 281.7 jit_solution(5733863511296814282)
XLA Ops:
  8.2 3.2 %collective-permute-start.2 = (bf16[256,256]{1,0:T(8,128)(2,1)S(1)}, bf16[256,256]{1,0:T(8,128)(2,1)S(1)}, u32[]{:S(2)}, u32[]{:S(2)}) collective-permute-start(bf16[256,256]{1,0:T(8,128)(2,1)S(1)} %bitcast.44), channel_id=1, source_target_pairs={{0,12},{1,13},{2,14},{3,15},{4,0},{5,1},{6,2},{7,3},{8,4},{9,5},{1... | collective-permute-start | bytes 393224 | tf_op jit(solution)/shard_map/ppermute | solution.py:39
  13.0 2.3 collective-permute-done.2
  15.3 2.7 collective-permute-done.1
  20.0 4.1 %collective-permute-start.5 = (bf16[1024,256]{1,0:T(8,128)(2,1)S(1)}, bf16[1024,256]{1,0:T(8,128)(2,1)S(1)}, u32[]{:S(2)}, u32[]{:S(2)}) collective-permute-start(bf16[1024,256]{1,0:T(8,128)(2,1)S(1)} %pad_maximum_fusion.1.a0), channel_id=1, source_target_pairs={{0,3},{1,0},{2,1},{3,2},{4,7},{5,4},{6,5},{7,6},{8,11},{9,8},{10,9... | collective-permute-start | bytes 1572872 | tf_op jit(solution)/shard_map/ppermute | solution.py:39
  27.7 10.9 %order_weights.1 = (bf16[4096,384]{1,0:T(8,128)(2,1)}, bf16[4096,128]{1,0:T(8,128)(2,1)}) custom-call(s32[16]{0:T(128)} %fusion.68.table, bf16[4096,128]{1,0:T(8,128)(2,1)} %q.1, bf16[4096,128]{1,0:T(8,128)(2,1)} %k.1, bf16[4096,128]{1,0:T(8,128)(2,1)} %v.1, bf16[128,4096]{1,0:T(8,128)(2,1)} %o.1), custom_call_target="tpu_custom_call" | custom-call | bytes 8388608 | tf_op jit(solution)/shard_map/order_weights/pallas_call | solution.py:72
  41.3 2.0 collective-permute-start.21
  43.4 2.3 collective-permute-start.20
  52.1 3.7 %collective-permute-done.21.a3 = bf16[1024,256]{1,0:T(8,128)(2,1)S(1)} collective-permute-done((bf16[1024,256]{1,0:T(8,128)(2,1)S(1)}, bf16[1024,256]{1,0:T(8,128)(2,1)S(1)}, u32[]{:S(2)}, u32[]{:S(2)}) %collective-permute-start.21) | collective-permute-done | bytes 524320 | tf_op jit(solution)/shard_map/ppermute | solution.py:39
  57.0 3.6 %collective-permute-done.19.a1 = bf16[1024,256]{1,0:T(8,128)(2,1)S(1)} collective-permute-done((bf16[1024,256]{1,0:T(8,128)(2,1)S(1)}, bf16[1024,256]{1,0:T(8,128)(2,1)S(1)}, u32[]{:S(2)}, u32[]{:S(2)}) %collective-permute-start.19) | collective-permute-done | bytes 524320 | tf_op jit(solution)/shard_map/ppermute | solution.py:39
  61.8 2.8 %collective-permute-start.9 = (bf16[128,128]{1,0:T(8,128)(2,1)S(1)}, bf16[128,128]{1,0:T(8,128)(2,1)S(1)}, u32[]{:S(2)}, u32[]{:S(2)}) collective-permute-start(bf16[128,128]{1,0:T(8,128)(2,1)S(1)} %fusion.47), channel_id=1, source_target_pairs={{0,96},{32,0},{64,32},{96,64},{1,97},{33,1},{65,33},{97,65},{2,98}... | collective-permute-start | bytes 98312 | tf_op jit(solution)/shard_map/ppermute | solution.py:43
  66.6 65.4 %place_blocks.3 = bf16[4096,256]{1,0:T(8,128)(2,1)} custom-call(s32[16]{0:T(128)} %fusion.68.table, bf16[1024,256]{1,0:T(8,128)(2,1)} %copy-done.7, bf16[1024,256]{1,0:T(8,128)(2,1)} %copy-done.5, bf16[1024,256]{1,0:T(8,128)(2,1)} %copy-done.4, bf16[1024,256]{1,0:T(8,128)(2,1)} %copy-done.3), custom_call_target="tpu_custom_call" | custom-call | bytes 4194304 | tf_op jit(solution)/shard_map/place_blocks/pallas_call | solution.py:114
  132.1 65.6 %place_blocks.2 = bf16[4096,256]{1,0:T(8,128)(2,1)} custom-call(s32[16]{0:T(128)} %fusion.68.table, bf16[1024,256]{1,0:T(8,128)(2,1)} %copy-done.6, bf16[1024,256]{1,0:T(8,128)(2,1)} %copy-done.10, bf16[1024,256]{1,0:T(8,128)(2,1)} %copy-done.9, bf16[1024,256]{1,0:T(8,128)(2,1)} %copy-done.8), custom_call_target="tpu_custom_call" | custom-call | bytes 4194304 | tf_op jit(solution)/shard_map/place_blocks/pallas_call | solution.py:114
  205.0 2.4 collective-permute-start.25
  210.1 2.8 collective-permute-done.24
  215.5 2.1 convolution_convert_fusion
  218.4 2.1 collective-permute-start.11
  220.8 2.7 collective-permute-start.10
  227.6 6.5 %collective-permute-done.12 = bf16[1024,256]{1,0:T(8,128)(2,1)S(1)} collective-permute-done((bf16[1024,256]{1,0:T(8,128)(2,1)S(1)}, bf16[1024,256]{1,0:T(8,128)(2,1)S(1)}, u32[]{:S(2)}, u32[]{:S(2)}) %collective-permute-start.12) | collective-permute-done | bytes 524320 | tf_op jit(solution)/shard_map/ppermute | solution.py:39
  235.8 2.1 collective-permute-start.15
  237.8 2.2 collective-permute-start.14
  240.0 8.1 %collective-permute-done.28 = bf16[1024,256]{1,0:T(8,128)(2,1)S(1)} collective-permute-done((bf16[1024,256]{1,0:T(8,128)(2,1)S(1)}, bf16[1024,256]{1,0:T(8,128)(2,1)S(1)}, u32[]{:S(2)}, u32[]{:S(2)}) %collective-permute-start.28) | collective-permute-done | bytes 524320 | tf_op jit(solution)/shard_map/ppermute | solution.py:39
  248.1 2.6 collective-permute-start.13
  252.0 2.8 %collective-permute-start.30 = (bf16[256,256]{1,0:T(8,128)(2,1)S(1)}, bf16[256,256]{1,0:T(8,128)(2,1)S(1)}, u32[]{:S(2)}, u32[]{:S(2)}) collective-permute-start(bf16[256,256]{1,0:T(8,128)(2,1)S(1)} %get-tuple-element.22), channel_id=1, source_target_pairs={{0,8},{1,9},{2,10},{3,11},{4,12},{5,13},{6,14},{7,15},{8,0},{9,1},... | collective-permute-start | bytes 393224 | tf_op jit(solution)/shard_map/ppermute | solution.py:39
  264.2 8.8 %reduce-scatter.5.cloned.1.call-done = bf16[512,256]{1,0:T(8,128)(2,1)} async-done(((bf16[4096,256]{1,0:T(8,128)(2,1)}), bf16[512,256]{1,0:T(8,128)(2,1)}) %reduce-scatter.5.cloned.1.call-update) | async-done | bytes 262160 | tf_op jit(solution)/shard_map/reduce_scatter | solution.py:232
  (180 shorter events, 52.8 us)
Async XLA Ops:
  7.2 253.5 %reduce-scatter.3.cloned.1.call-start = ((), (), s32[]{:S(2)}) async-start(), calls=%async_computation.2 | async-start | bytes 2359296 | tf_op jit(solution)/shard_map/reduce_scatter | solution.py:226
  20.0 25.7 %collective-permute-start.5 = (bf16[1024,256]{1,0:T(8,128)(2,1)S(1)}, bf16[1024,256]{1,0:T(8,128)(2,1)S(1)}, u32[]{:S(2)}, u32[]{:S(2)}) collective-permute-start(bf16[1024,256]{1,0:T(8,128)(2,1)S(1)} %pad_maximum_fusion.1.a0), channel_id=1, source_target_pairs={{0,3},{1,0},{2,1},{3,2},{4,7},{5,4},{6,5},{7,6},{8,11},{9,8},{10,9... | collective-permute-start | bytes 1572872 | tf_op jit(solution)/shard_map/ppermute | solution.py:39
  24.1 23.4 %collective-permute-start.4 = (bf16[1024,256]{1,0:T(8,128)(2,1)S(1)}, bf16[1024,256]{1,0:T(8,128)(2,1)S(1)}, u32[]{:S(2)}, u32[]{:S(2)}) collective-permute-start(bf16[1024,256]{1,0:T(8,128)(2,1)S(1)} %pad_maximum_fusion.1.a0), channel_id=1, source_target_pairs={{0,2},{1,3},{2,0},{3,1},{4,6},{5,7},{6,4},{7,5},{8,10},{9,11},{10,... | collective-permute-start | bytes 1572872 | tf_op jit(solution)/shard_map/ppermute | solution.py:39
  25.1 13.5 %collective-permute-start.18 = (bf16[256,256]{1,0:T(8,128)(2,1)S(1)}, bf16[256,256]{1,0:T(8,128)(2,1)S(1)}, u32[]{:S(2)}, u32[]{:S(2)}) collective-permute-start(bf16[256,256]{1,0:T(8,128)(2,1)S(1)} %bitcast.39), channel_id=1, source_target_pairs={{0,12},{1,13},{2,14},{3,15},{4,0},{5,1},{6,2},{7,3},{8,4},{9,5},{1... | collective-permute-start | bytes 393224 | tf_op jit(solution)/shard_map/ppermute | solution.py:39
  25.7 14.2 %collective-permute-start.17 = (bf16[256,256]{1,0:T(8,128)(2,1)S(1)}, bf16[256,256]{1,0:T(8,128)(2,1)S(1)}, u32[]{:S(2)}, u32[]{:S(2)}) collective-permute-start(bf16[256,256]{1,0:T(8,128)(2,1)S(1)} %bitcast.40), channel_id=1, source_target_pairs={{0,8},{1,9},{2,10},{3,11},{4,12},{5,13},{6,14},{7,15},{8,0},{9,1},... | collective-permute-start | bytes 393224 | tf_op jit(solution)/shard_map/ppermute | solution.py:39
  26.4 13.6 %collective-permute-start.16 = (bf16[256,256]{1,0:T(8,128)(2,1)S(1)}, bf16[256,256]{1,0:T(8,128)(2,1)S(1)}, u32[]{:S(2)}, u32[]{:S(2)}) collective-permute-start(bf16[256,256]{1,0:T(8,128)(2,1)S(1)} %bitcast.41), channel_id=1, source_target_pairs={{0,4},{1,5},{2,6},{3,7},{4,8},{5,9},{6,10},{7,11},{8,12},{9,13},{1... | collective-permute-start | bytes 393224 | tf_op jit(solution)/shard_map/ppermute | solution.py:39
  38.6 11.3 %collective-permute-start.3 = (bf16[1024,256]{1,0:T(8,128)(2,1)S(1)}, bf16[1024,256]{1,0:T(8,128)(2,1)S(1)}, u32[]{:S(2)}, u32[]{:S(2)}) collective-permute-start(bf16[1024,256]{1,0:T(8,128)(2,1)S(1)} %pad_maximum_fusion.1.a0), channel_id=1, source_target_pairs={{0,1},{1,2},{2,3},{3,0},{4,5},{5,6},{6,7},{7,4},{8,9},{9,10},{10,1... | collective-permute-start | bytes 1572872 | tf_op jit(solution)/shard_map/ppermute | solution.py:39
  41.3 14.4 %collective-permute-start.21 = (bf16[1024,256]{1,0:T(8,128)(2,1)S(1)}, bf16[1024,256]{1,0:T(8,128)(2,1)S(1)}, u32[]{:S(2)}, u32[]{:S(2)}) collective-permute-start(bf16[1024,256]{1,0:T(8,128)(2,1)S(1)} %pad_maximum_fusion.2.a0), channel_id=1, source_target_pairs={{0,3},{1,0},{2,1},{3,2},{4,7},{5,4},{6,5},{7,6},{8,11},{9,8},{10,9... | collective-permute-start | bytes 1572872 | tf_op jit(solution)/shard_map/ppermute | solution.py:39
  43.4 12.6 %collective-permute-start.20 = (bf16[1024,256]{1,0:T(8,128)(2,1)S(1)}, bf16[1024,256]{1,0:T(8,128)(2,1)S(1)}, u32[]{:S(2)}, u32[]{:S(2)}) collective-permute-start(bf16[1024,256]{1,0:T(8,128)(2,1)S(1)} %pad_maximum_fusion.2.a0), channel_id=1, source_target_pairs={{0,2},{1,3},{2,0},{3,1},{4,6},{5,7},{6,4},{7,5},{8,10},{9,11},{10,... | collective-permute-start | bytes 1572872 | tf_op jit(solution)/shard_map/ppermute | solution.py:39
  45.7 14.9 %collective-permute-start.19 = (bf16[1024,256]{1,0:T(8,128)(2,1)S(1)}, bf16[1024,256]{1,0:T(8,128)(2,1)S(1)}, u32[]{:S(2)}, u32[]{:S(2)}) collective-permute-start(bf16[1024,256]{1,0:T(8,128)(2,1)S(1)} %pad_maximum_fusion.2.a0), channel_id=1, source_target_pairs={{0,1},{1,2},{2,3},{3,0},{4,5},{5,6},{6,7},{7,4},{8,9},{9,10},{10,1... | collective-permute-start | bytes 1572872 | tf_op jit(solution)/shard_map/ppermute | solution.py:39
  52.0 9.8 %collective-permute-start.6 = (bf16[128,128]{1,0:T(8,128)(2,1)S(1)}, bf16[128,128]{1,0:T(8,128)(2,1)S(1)}, u32[]{:S(2)}, u32[]{:S(2)}) collective-permute-start(bf16[128,128]{1,0:T(8,128)(2,1)S(1)} %convolution_convert_fusion.12), channel_id=1, source_target_pairs={{0,16},{16,0},{1,17},{17,1},{2,18},{18,2},{3,19},{19,3},{4,20},{20... | collective-permute-start | bytes 98312 | tf_op jit(solution)/shard_map/ppermute | solution.py:47
  61.8 135.9 %collective-permute-start.9 = (bf16[128,128]{1,0:T(8,128)(2,1)S(1)}, bf16[128,128]{1,0:T(8,128)(2,1)S(1)}, u32[]{:S(2)}, u32[]{:S(2)}) collective-permute-start(bf16[128,128]{1,0:T(8,128)(2,1)S(1)} %fusion.47), channel_id=1, source_target_pairs={{0,96},{32,0},{64,32},{96,64},{1,97},{33,1},{65,33},{97,65},{2,98}... | collective-permute-start | bytes 98312 | tf_op jit(solution)/shard_map/ppermute | solution.py:43
  64.6 133.1 %collective-permute-start.8 = (bf16[128,128]{1,0:T(8,128)(2,1)S(1)}, bf16[128,128]{1,0:T(8,128)(2,1)S(1)}, u32[]{:S(2)}, u32[]{:S(2)}) collective-permute-start(bf16[128,128]{1,0:T(8,128)(2,1)S(1)} %fusion.47), channel_id=1, source_target_pairs={{0,64},{32,96},{64,0},{96,32},{1,65},{33,97},{65,1},{97,33},{2,66}... | collective-permute-start | bytes 98312 | tf_op jit(solution)/shard_map/ppermute | solution.py:43
  65.4 132.3 %collective-permute-start.7 = (bf16[128,128]{1,0:T(8,128)(2,1)S(1)}, bf16[128,128]{1,0:T(8,128)(2,1)S(1)}, u32[]{:S(2)}, u32[]{:S(2)}) collective-permute-start(bf16[128,128]{1,0:T(8,128)(2,1)S(1)} %fusion.47), channel_id=1, source_target_pairs={{0,32},{32,64},{64,96},{96,0},{1,33},{33,65},{65,97},{97,1},{2,34}... | collective-permute-start | bytes 98312 | tf_op jit(solution)/shard_map/ppermute | solution.py:43
  203.4 69.6 %reduce-scatter.5.cloned.1.call-start = ((), (), s32[]{:S(2)}) async-start(), calls=%async_computation.3 | async-start | bytes 2359296 | tf_op jit(solution)/shard_map/reduce_scatter | solution.py:232
  218.0 16.1 %collective-permute-start.12 = (bf16[1024,256]{1,0:T(8,128)(2,1)S(1)}, bf16[1024,256]{1,0:T(8,128)(2,1)S(1)}, u32[]{:S(2)}, u32[]{:S(2)}) collective-permute-start(bf16[1024,256]{1,0:T(8,128)(2,1)S(1)} %convolution_convert_fusion.7), channel_id=1, source_target_pairs={{0,1},{1,2},{2,3},{3,0},{4,5},{5,6},{6,7},{7,4},{8,9},{9,10},{10,1... | collective-permute-start | bytes 1572872 | tf_op jit(solution)/shard_map/ppermute | solution.py:39
  218.4 16.4 %collective-permute-start.11 = (bf16[1024,256]{1,0:T(8,128)(2,1)S(1)}, bf16[1024,256]{1,0:T(8,128)(2,1)S(1)}, u32[]{:S(2)}, u32[]{:S(2)}) collective-permute-start(bf16[1024,256]{1,0:T(8,128)(2,1)S(1)} %convolution_convert_fusion.8), channel_id=1, source_target_pairs={{0,2},{1,3},{2,0},{3,1},{4,6},{5,7},{6,4},{7,5},{8,10},{9,11},{10,... | collective-permute-start | bytes 1572872 | tf_op jit(solution)/shard_map/ppermute | solution.py:39
  220.8 14.5 %collective-permute-start.10 = (bf16[1024,256]{1,0:T(8,128)(2,1)S(1)}, bf16[1024,256]{1,0:T(8,128)(2,1)S(1)}, u32[]{:S(2)}, u32[]{:S(2)}) collective-permute-start(bf16[1024,256]{1,0:T(8,128)(2,1)S(1)} %convolution_convert_fusion.9), channel_id=1, source_target_pairs={{0,3},{1,0},{2,1},{3,2},{4,7},{5,4},{6,5},{7,6},{8,11},{9,8},{10,9... | collective-permute-start | bytes 1572872 | tf_op jit(solution)/shard_map/ppermute | solution.py:39
  225.5 22.6 %collective-permute-start.28 = (bf16[1024,256]{1,0:T(8,128)(2,1)S(1)}, bf16[1024,256]{1,0:T(8,128)(2,1)S(1)}, u32[]{:S(2)}, u32[]{:S(2)}) collective-permute-start(bf16[1024,256]{1,0:T(8,128)(2,1)S(1)} %convolution_convert_fusion.3), channel_id=1, source_target_pairs={{0,1},{1,2},{2,3},{3,0},{4,5},{5,6},{6,7},{7,4},{8,9},{9,10},{10,1... | collective-permute-start | bytes 1572872 | tf_op jit(solution)/shard_map/ppermute | solution.py:39
  225.6 25.2 %collective-permute-start.27 = (bf16[1024,256]{1,0:T(8,128)(2,1)S(1)}, bf16[1024,256]{1,0:T(8,128)(2,1)S(1)}, u32[]{:S(2)}, u32[]{:S(2)}) collective-permute-start(bf16[1024,256]{1,0:T(8,128)(2,1)S(1)} %convolution_convert_fusion.4), channel_id=1, source_target_pairs={{0,2},{1,3},{2,0},{3,1},{4,6},{5,7},{6,4},{7,5},{8,10},{9,11},{10,... | collective-permute-start | bytes 1572872 | tf_op jit(solution)/shard_map/ppermute | solution.py:39
  234.1 16.7 %collective-permute-start.26 = (bf16[1024,256]{1,0:T(8,128)(2,1)S(1)}, bf16[1024,256]{1,0:T(8,128)(2,1)S(1)}, u32[]{:S(2)}, u32[]{:S(2)}) collective-permute-start(bf16[1024,256]{1,0:T(8,128)(2,1)S(1)} %convolution_convert_fusion.5), channel_id=1, source_target_pairs={{0,3},{1,0},{2,1},{3,2},{4,7},{5,4},{6,5},{7,6},{8,11},{9,8},{10,9... | collective-permute-start | bytes 1572872 | tf_op jit(solution)/shard_map/ppermute | solution.py:39
  235.8 19.1 %collective-permute-start.15 = (bf16[256,256]{1,0:T(8,128)(2,1)S(1)}, bf16[256,256]{1,0:T(8,128)(2,1)S(1)}, u32[]{:S(2)}, u32[]{:S(2)}) collective-permute-start(bf16[256,256]{1,0:T(8,128)(2,1)S(1)} %get-tuple-element.24), channel_id=1, source_target_pairs={{0,4},{1,5},{2,6},{3,7},{4,8},{5,9},{6,10},{7,11},{8,12},{9,13},{1... | collective-permute-start | bytes 393224 | tf_op jit(solution)/shard_map/ppermute | solution.py:39
  237.8 18.9 %collective-permute-start.14 = (bf16[256,256]{1,0:T(8,128)(2,1)S(1)}, bf16[256,256]{1,0:T(8,128)(2,1)S(1)}, u32[]{:S(2)}, u32[]{:S(2)}) collective-permute-start(bf16[256,256]{1,0:T(8,128)(2,1)S(1)} %get-tuple-element.25), channel_id=1, source_target_pairs={{0,8},{1,9},{2,10},{3,11},{4,12},{5,13},{6,14},{7,15},{8,0},{9,1},... | collective-permute-start | bytes 393224 | tf_op jit(solution)/shard_map/ppermute | solution.py:39
  248.1 8.6 %collective-permute-start.13 = (bf16[256,256]{1,0:T(8,128)(2,1)S(1)}, bf16[256,256]{1,0:T(8,128)(2,1)S(1)}, u32[]{:S(2)}, u32[]{:S(2)}) collective-permute-start(bf16[256,256]{1,0:T(8,128)(2,1)S(1)} %get-tuple-element.23), channel_id=1, source_target_pairs={{0,12},{1,13},{2,14},{3,15},{4,0},{5,1},{6,2},{7,3},{8,4},{9,5},{1... | collective-permute-start | bytes 393224 | tf_op jit(solution)/shard_map/ppermute | solution.py:39
  (48 other events, 785.3 us)
Sparse Core Ops, SparseCore 0:
  203.5 34.5 reduce-scatter.2
  240.6 32.4 reduce-scatter.4

commit v2 on v1

v2 whole, which is shorter than its diff:
```python
import jax
import jax.numpy as jnp
from jax import lax
from jax.experimental import pallas as pl
from jax.experimental.pallas import tpu as pltpu
from jax.sharding import Mesh
from jax.sharding import PartitionSpec as P

SEQ = ("x", "core")
HEAD = ("y", "z")
PLANE = ("core", "y", "z")
SIDE = 4
EPSILON = 1e-06
WIDE = jnp.float32
HALF = jnp.bfloat16

NN = (((1,), (0,)), ((), ()))
NT = (((1,), (1,)), ((), ()))
TN = (((0,), (0,)), ((), ()))


def mm(a, b, dims):
    return lax.dot_general(a, b, dims, preferred_element_type=WIDE)


def plane_pairs(phase, shift):
    pairs = []
    for core in range(2):
        for y in range(SIDE):
            for z in range(SIDE):
                along_y = core == phase
                ty = (y + shift) % SIDE if along_y else y
                tz = z if along_y else (z + shift) % SIDE
                pairs.append(((core * SIDE + y) * SIDE + z, (core * SIDE + ty) * SIDE + tz))
    return pairs


def plane_shift(a, phase, shift):
    return lax.ppermute(a, PLANE, plane_pairs(phase, shift))


def x_shift(a, shift):
    return lax.ppermute(a, "x", [(i, (i + shift) % SIDE) for i in range(SIDE)])


def core_swap(a):
    return lax.ppermute(a, "core", [(0, 1), (1, 0)])


def block_tables():
    x, core, y, z = (lax.axis_index(n) for n in ("x",) + PLANE)
    at = jnp.arange(SIDE * SIDE, dtype=jnp.int32)
    d2, d1 = at // SIDE, at % SIDE
    from_y = (y - jnp.where(core == 0, d1, d2)) % SIDE
    from_z = (z - jnp.where(core == 0, d2, d1)) % SIDE
    other_core = (from_z // 2 + core) % 2
    slots = other_core * 8 + ((from_y - x) % SIDE) * 2 + from_z % 2
    return from_y * SIDE + from_z, slots


def order_weights_kernel(table, q, k, v, o, qkv_out, o_out):
    n = q.shape[1]
    step = q.shape[0] // (SIDE * SIDE)
    for i in range(SIDE * SIDE):
        at = pl.ds(pl.multiple_of(table[i] * step, step), step)
        to = slice(i * step, (i + 1) * step)
        qkv_out[to, :n] = q[at, :]
        qkv_out[to, n : 2 * n] = k[at, :]
        qkv_out[to, 2 * n :] = v[at, :]
        o_out[to, :] = o[:, at].T


def order_weights(table, w_query, w_key, w_value, w_out):
    rows, n = w_query.shape
    vmem = pl.BlockSpec(memory_space=pltpu.VMEM)
    return pl.pallas_call(
        order_weights_kernel,
        out_shape=(
            jax.ShapeDtypeStruct((rows, 3 * n), HALF),
            jax.ShapeDtypeStruct((rows, n), HALF),
        ),
        in_specs=[pl.BlockSpec(memory_space=pltpu.SMEM)] + [vmem] * 4,
        out_specs=(vmem, vmem),
        compiler_params=pltpu.CompilerParams(vmem_limit_bytes=24 << 20),
        cost_estimate=pl.CostEstimate(
            flops=0, bytes_accessed=16 * rows * n, transcendentals=0
        ),
        name="order_weights",
    )(table, w_query, w_key, w_value, w_out)


def weight_grads_kernel(slots, *refs):
    *ins, keep, send = refs
    groups = [ins[i : i + SIDE + 1] for i in range(0, len(ins), SIDE + 1)]
    step = ins[0].shape[0] // SIDE
    half = SIDE * SIDE // 2
    for d2 in range(SIDE):
        for d1 in range(SIDE):
            terms = [
                jnp.dot(
                    g[d2][d1 * step : (d1 + 1) * step, :], g[SIDE][...], preferred_element_type=WIDE
                ).astype(HALF)
                for g in groups
            ]
            slot = slots[d2 * SIDE + d1]

            @pl.when(slot < half)
            def _():
                at = 0
                for t in terms:
                    keep[slot, :, at : at + t.shape[1]] = t
                    at += t.shape[1]

            @pl.when(slot >= half)
            def _():
                at = 0
                for t in terms:
                    send[slot - half, :, at : at + t.shape[1]] = t
                    at += t.shape[1]


def weight_grads(slots, *groups):
    rows, tokens = groups[0][0][0].shape
    step = rows // SIDE
    n = sum(g.shape[1] for _, g in groups)
    vmem = pl.BlockSpec(memory_space=pltpu.VMEM)
    args = [a for parts, g in groups for a in (*parts, g)]
    half = jax.ShapeDtypeStruct((SIDE * SIDE // 2, step, n), HALF)
    return pl.pallas_call(
        weight_grads_kernel,
        out_shape=(half, half),
        in_specs=[pl.BlockSpec(memory_space=pltpu.SMEM)] + [vmem] * len(args),
        out_specs=(vmem, vmem),
        compiler_params=pltpu.CompilerParams(vmem_limit_bytes=24 << 20),
        cost_estimate=pl.CostEstimate(
            flops=2 * SIDE * rows * tokens * n,
            bytes_accessed=2 * SIDE * rows * (tokens * len(groups) + n),
            transcendentals=0,
        ),
        name="weight_grads",
    )(slots, *args)


def seq_sum(keep, send):
    mine = (keep.astype(WIDE) + core_swap(send).astype(WIDE)).astype(HALF)
    n = mine.shape[2]
    parts = [mine[2 * d : 2 * d + 2] for d in range(SIDE)]
    got = [x_shift(p, d) for d, p in enumerate(parts) if d]
    return total([parts[0]] + got).reshape(-1, n)


def spread_phase1(a):
    return [a] + [plane_shift(a, 0, d) for d in range(1, SIDE)]


def spread_phase2(a):
    return [a] + [plane_shift(a, 1, d) for d in range(1, SIDE)]


def total(parts):
    acc = parts[0].astype(WIDE)
    for p in parts[1:]:
        acc = acc + p.astype(WIDE)
    return acc


def fold_phase1(terms):
    return [terms[0]] + [plane_shift(t, 1, -d) for d, t in enumerate(terms) if d]


def fold_phase2(got):
    mine = total(got).astype(HALF)
    step = mine.shape[0] // SIDE
    parts = [mine[d * step : (d + 1) * step] for d in range(SIDE)]
    return [parts[0]] + [plane_shift(p, 0, -d) for d, p in enumerate(parts) if d]


def pair_and_others(own):
    other = core_swap(own)
    pair = (own.astype(WIDE) + other.astype(WIDE)).astype(HALF)
    return other, [pair] + [x_shift(pair, d) for d in range(1, SIDE)]


def masked_sum(first, parts, keep):
    acc = first
    for part, k in zip(parts, keep):
        acc = acc + jnp.where(k, part.astype(WIDE), 0.0)
    return acc


def on_device(tokens, w_query, w_key, w_value, w_out, grad_out, state_in):
    x, core = lax.axis_index("x"), lax.axis_index("core")
    dh = w_query.shape[1]
    rows = tokens.shape[0]
    table, slots = block_tables()

    t1 = spread_phase1(tokens.T)
    g1 = spread_phase1(grad_out.T)
    weights = order_weights(table, w_query, w_key, w_value, w_out)
    t1, g1, (w_qkv, w_o) = lax.optimization_barrier((t1, g1, weights))
    t_parts = spread_phase2(jnp.concatenate(t1, axis=0))
    t_parts, g1 = lax.optimization_barrier((t_parts, jnp.concatenate(g1, axis=0)))
    g_parts = spread_phase2(g1)
    step = g1.shape[0]
    wq_parts = [w_qkv[d * step : (d + 1) * step] for d in range(SIDE)]
    wo_parts = [w_o[d * step : (d + 1) * step] for d in range(SIDE)]

    qkv = sum(mm(t, w, TN) for t, w in zip(t_parts, wq_parts)).astype(HALF)
    query, keys, values = (qkv[:, i * dh : (i + 1) * dh] for i in range(3))

    own_state = mm(keys, values, TN).astype(HALF)
    other, pairs = pair_and_others(own_state)
    prior = masked_sum(
        state_in[0], [other] + pairs[1:], [core == 1] + [x >= d for d in range(1, SIDE)]
    ).astype(HALF)

    allowed = jnp.tril(jnp.ones((rows, rows), jnp.bool_))
    scores = jnp.where(allowed, mm(query, keys, NT), 0.0).astype(HALF)
    mixed = mm(scores, values, NN) + mm(query, prior, NN)
    inv_norm = lax.rsqrt(jnp.mean(mixed * mixed, axis=-1, keepdims=True) + EPSILON)
    normed = (mixed * inv_norm).astype(HALF)
    normed, g_parts = lax.optimization_barrier((normed, g_parts))

    grad_normed = sum(mm(g, w, TN) for g, w in zip(g_parts, wo_parts))
    grad_mixed = inv_norm * (
        grad_normed
        - mixed * inv_norm * inv_norm * jnp.mean(grad_normed * mixed, axis=-1, keepdims=True)
    )
    grad_mixed = grad_mixed.astype(HALF)
    own_back = mm(query, grad_mixed, TN).astype(HALF)
    other_back, back_pairs = pair_and_others(own_back)

    out_terms = [mm(w, normed, NT).astype(HALF) for w in wo_parts]
    out_got = fold_phase1(out_terms)

    grad_scores = jnp.where(allowed, mm(grad_mixed, values, NT), 0.0).astype(HALF)
    grad_query = (mm(grad_scores, keys, NN) + mm(grad_mixed, prior, NT)).astype(HALF)
    early = weight_grads(slots, (t_parts, grad_query), (g_parts, normed))

    later = masked_sum(
        jnp.zeros((dh, dh), WIDE),
        [other_back] + back_pairs[1:],
        [core == 0] + [x < d for d in range(1, SIDE)],
    ).astype(HALF)
    grad_state = jnp.zeros((dh, dh), WIDE)
    for chip in range(SIDE):
        part = jnp.zeros((dh, dh), HALF)
        for d, p in enumerate(back_pairs):
            part = jnp.where((x - d) % SIDE == chip, p, part)
        grad_state = grad_state + part.astype(WIDE)

    grad_keys = (mm(grad_scores, query, TN) + mm(values, later, NT)).astype(HALF)
    grad_values = (mm(scores, grad_mixed, TN) + mm(keys, later, NN)).astype(HALF)
    grad_qkv = jnp.concatenate([grad_query, grad_keys, grad_values], axis=1)
    grad_qkv, out_got = lax.optimization_barrier((grad_qkv, out_got))
    in_terms = [mm(w, grad_qkv, NT).astype(HALF) for w in wq_parts]
    in_got = fold_phase1(in_terms)
    result = total(fold_phase2(out_got)).astype(HALF).T
    late = weight_grads(slots, (t_parts, grad_qkv[:, dh:]))
    early = seq_sum(*early)
    late = seq_sum(*late)
    grad_tokens = total(fold_phase2(in_got)).T
    return (
        result,
        grad_tokens,
        early[:, :dh],
        late[:, :dh],
        late[:, dh:],
        early[:, dh:].T,
        grad_state[None],
    )


def solution(mesh):
    sizes = (SIDE, mesh.shape["seq"] // SIDE, SIDE, SIDE)
    torus = Mesh(mesh.devices.reshape(sizes), SEQ + HEAD)
    seq_head = P(SEQ, HEAD)
    column = P(None, HEAD)
    return jax.shard_map(
        on_device,
        mesh=torus,
        in_specs=(seq_head, column, column, column, P(HEAD, None), seq_head, P(HEAD, None, None)),
        out_specs=(
            seq_head,
            seq_head,
            seq_head,
            seq_head,
            seq_head,
            P(HEAD, SEQ),
            P(HEAD, None, None),
        ),
        check_vma=False,
    )
```

time: 283 us -> 156 us (0.55)
  Pallas kernels: 142 us -> 11.5 us
  between operations: 14.9 us -> 1.06 us
  waiting for transfers between devices: 43.9 us -> 51.1 us
  starting transfers between devices: 44.3 us -> 51.1 us
  other arithmetic: 4.09 us -> 8 us
  matrix products: 18.7 us -> 14.9 us
  local copies, waits for them, and re-layouts: 13.8 us -> 17.3 us
    pallas_call x2, Pallas kernels: 131 us -> 10.2 us  [weight_grads(): pl.pallas_call(weight_grads_kernel, out_shape=(half, half), in_specs=[pl....]
    ppermute x24, waiting for transfers between devices: 31 us -> 42.4 us  [plane_shift(): return lax.ppermute(a, PLANE, plane_pairs(phase, shift))]
    ppermute x6 -> x12, starting transfers between devices: 8.48 us -> 19.4 us  [x_shift(): return lax.ppermute(a, 'x', [(i, (i + shift) % SIDE) for i in range(SIDE)])]
    pallas_call x1, Pallas kernels: 10.9 us -> 1.28 us  [order_weights(): pl.pallas_call(order_weights_kernel, out_shape=(jax.ShapeDtypeStruct((row...]
    reduce_scatter x2 -> x0, waiting for transfers between devices: 8.83 us -> none  [the longest x1 8.83 us: on_device(): late = lax.psum_scatter(late, SEQ, scatter_dimension=0, tiled=True)]
    ppermute x24, starting transfers between devices: 35.6 us -> 30.1 us  [plane_shift(): return lax.ppermute(a, PLANE, plane_pairs(phase, shift))]
    ppermute x6 -> x12, waiting for transfers between devices: 3.99 us -> 8.7 us  [x_shift(): return lax.ppermute(a, 'x', [(i, (i + shift) % SIDE) for i in range(SIDE)])]
    dot_general x31 -> x28, matrix products: 18.7 us -> 14.9 us  [mm(): return lax.dot_general(a, b, dims, preferred_element_type=WIDE)]
  transfers between devices with their start and end apart: 34 -> 40, of which waited for: 14 -> 14; matrix products, arithmetic and copies ran while one was open for 8% -> 13% of each run, Pallas kernels for 50% -> 7%
where the time goes in v2:
time: 156 us; the launch traced here: 155 us
  starting transfers between devices  51.1 us (33%)
  waiting for transfers between devices  51.1 us (33%)
  local copies, waits for them, and re-layouts  17.3 us (11%)
  matrix products  14.9 us (10%)
  Pallas kernels  11.5 us (7%)
  other arithmetic  8 us (5%)
    ppermute x24, waiting for transfers between devices, plane_shift(): return lax.ppermute(a, PLANE, plane_pairs(phase, shift))  42.4 us
    ppermute x24, starting transfers between devices, plane_shift(): return lax.ppermute(a, PLANE, plane_pairs(phase, shift))  30.1 us
    ppermute x12, starting transfers between devices, x_shift(): return lax.ppermute(a, 'x', [(i, (i + shift) % SIDE) for i in range(SIDE)])  19.4 us
    dot_general x28, matrix products, mm(): return lax.dot_general(a, b, dims, preferred_element_type=WIDE)  14.9 us
    unnamed x26, local copies, waits for them, and re-layouts  13.8 us
    pallas_call x2, Pallas kernels, weight_grads(): pl.pallas_call(weight_grads_kernel, out_shape=(half, half), in_specs=[pl....  10.2 us
    ppermute x12, waiting for transfers between devices, x_shift(): return lax.ppermute(a, 'x', [(i, (i + shift) % SIDE) for i in range(SIDE)])  8.7 us
  transfers between devices with their start and end apart: 40, of which 14 were waited for; matrix products, arithmetic and copies ran while one was open for 13% of the time, Pallas kernels for 7%

profile of v2, /device:TPU:0, one launch (start us, length us, event | category | flops | bytes accessed | tf_op | source)
XLA Modules:
  0.0 155.0 jit_solution(11977137803477794314)
XLA Ops:
  1.6 3.2 %collective-permute-start.5 = (bf16[256,256]{1,0:T(8,128)(2,1)S(1)}, bf16[256,256]{1,0:T(8,128)(2,1)}, u32[]{:S(2)}, u32[]{:S(2)}) collective-permute-start(bf16[256,256]{1,0:T(8,128)(2,1)S(1)} %bitcast.47), channel_id=1, source_target_pairs={{0,12},{1,13},{2,14},{3,15},{4,0},{5,1},{6,2},{7,3},{8,4},{9,5},{1... | collective-permute-start | bytes 393224 | tf_op jit(solution)/shard_map/ppermute | solution.py:39
  7.4 2.3 %collective-permute-start.2 = (bf16[256,256]{1,0:T(8,128)(2,1)S(1)}, bf16[256,256]{1,0:T(8,128)(2,1)S(1)}, u32[]{:S(2)}, u32[]{:S(2)}) collective-permute-start(bf16[256,256]{1,0:T(8,128)(2,1)S(1)} %bitcast.43), channel_id=1, source_target_pairs={{0,12},{1,13},{2,14},{3,15},{4,0},{5,1},{6,2},{7,3},{8,4},{9,5},{1... | collective-permute-start | bytes 393224 | tf_op jit(solution)/shard_map/ppermute | solution.py:39
  21.2 4.1 %collective-permute-start.8 = (bf16[1024,256]{1,0:T(8,128)(2,1)S(1)}, bf16[1024,256]{1,0:T(8,128)(2,1)S(1)}, u32[]{:S(2)}, u32[]{:S(2)}) collective-permute-start(bf16[1024,256]{1,0:T(8,128)(2,1)S(1)} %constant_dynamic-update-slice_fusion.refs_0_), channel_id=1, source_target_pairs={{0,3},{1,0},{2,1},{3,2},{4,7},{5,4},{6,5},{7,6},{8,11},{9,8},{10,9... | collective-permute-start | bytes 1572872 | tf_op jit(solution)/shard_map/ppermute | solution.py:39
  27.8 9.8 %collective-permute-done.8.refs_3_ = bf16[1024,256]{1,0:T(8,128)(2,1)S(1)} collective-permute-done((bf16[1024,256]{1,0:T(8,128)(2,1)S(1)}, bf16[1024,256]{1,0:T(8,128)(2,1)S(1)}, u32[]{:S(2)}, u32[]{:S(2)}) %collective-permute-start.8) | collective-permute-done | bytes 524320 | tf_op jit(solution)/shard_map/ppermute | solution.py:39
  37.6 3.7 %collective-permute-done.6.refs_1_ = bf16[1024,256]{1,0:T(8,128)(2,1)S(1)} collective-permute-done((bf16[1024,256]{1,0:T(8,128)(2,1)S(1)}, bf16[1024,256]{1,0:T(8,128)(2,1)S(1)}, u32[]{:S(2)}, u32[]{:S(2)}) %collective-permute-start.6) | collective-permute-done | bytes 524320 | tf_op jit(solution)/shard_map/ppermute | solution.py:39
  47.0 2.8 %collective-permute-start.12 = (bf16[128,128]{1,0:T(8,128)(2,1)S(1)}, bf16[128,128]{1,0:T(8,128)(2,1)S(1)}, u32[]{:S(2)}, u32[]{:S(2)}) collective-permute-start(bf16[128,128]{1,0:T(8,128)(2,1)S(1)} %fusion.43), channel_id=1, source_target_pairs={{0,96},{32,0},{64,32},{96,64},{1,97},{33,1},{65,33},{97,65},{2,98}... | collective-permute-start | bytes 98312 | tf_op jit(solution)/shard_map/ppermute | solution.py:43
  52.9 2.4 %collective-permute-done.11 = bf16[128,128]{1,0:T(8,128)(2,1)S(1)} collective-permute-done((bf16[128,128]{1,0:T(8,128)(2,1)S(1)}, bf16[128,128]{1,0:T(8,128)(2,1)S(1)}, u32[]{:S(2)}, u32[]{:S(2)}) %collective-permute-start.11) | collective-permute-done | bytes 32800 | tf_op jit(solution)/shard_map/ppermute | solution.py:43
  57.7 5.6 %collective-permute-done.13.refs_6_ = bf16[1024,256]{1,0:T(8,128)(2,1)S(1)} collective-permute-done((bf16[1024,256]{1,0:T(8,128)(2,1)S(1)}, bf16[1024,256]{1,0:T(8,128)(2,1)S(1)}, u32[]{:S(2)}, u32[]{:S(2)}) %collective-permute-start.13) | collective-permute-done | bytes 524320 | tf_op jit(solution)/shard_map/ppermute | solution.py:39
  69.8 2.8 %collective-permute-start.19 = (bf16[128,128]{1,0:T(8,128)(2,1)S(1)}, bf16[128,128]{1,0:T(8,128)(2,1)S(1)}, u32[]{:S(2)}, u32[]{:S(2)}) collective-permute-start(bf16[128,128]{1,0:T(8,128)(2,1)S(1)} %fusion.48), channel_id=1, source_target_pairs={{0,96},{32,0},{64,32},{96,64},{1,97},{33,1},{65,33},{97,65},{2,98}... | collective-permute-start | bytes 98312 | tf_op jit(solution)/shard_map/ppermute | solution.py:43
  74.3 5.1 %weight_grads.2 = (bf16[8,256,256]{2,1,0:T(8,128)(2,1)S(1)}, bf16[8,256,256]{2,1,0:T(8,128)(2,1)}) custom-call(s32[16]{0:T(128)S(1)} %fusion.64.slots, bf16[1024,256]{1,0:T(8,128)(2,1)S(1)} %constant_dynamic-update-slice_fusion.refs_0_, bf16[1024,256]{1,0:T(8,128)(2,1)S(1)} %collective-permute-done.6.refs_1_, ...), custom_call_target="tpu_custom_call" | custom-call | flops 536870912 | bytes 6291456 | tf_op jit(solution)/shard_map/weight_grads/pallas_call | solution.py:129
  81.7 8.7 %collective-permute-done.22 = bf16[1024,256]{1,0:T(8,128)(2,1)S(1)} collective-permute-done((bf16[1024,256]{1,0:T(8,128)(2,1)S(1)}, bf16[1024,256]{1,0:T(8,128)(2,1)S(1)}, u32[]{:S(2)}, u32[]{:S(2)}) %collective-permute-start.22) | collective-permute-done | bytes 524320 | tf_op jit(solution)/shard_map/ppermute | solution.py:39
  90.7 1.9 %collective-permute-start.23 = (bf16[256,256]{1,0:T(8,128)(2,1)S(1)}, bf16[256,256]{1,0:T(8,128)(2,1)S(1)}, u32[]{:S(2)}, u32[]{:S(2)}) collective-permute-start(bf16[256,256]{1,0:T(8,128)(2,1)S(1)} %get-tuple-element.89), channel_id=1, source_target_pairs={{0,12},{1,13},{2,14},{3,15},{4,0},{5,1},{6,2},{7,3},{8,4},{9,5},{1... | collective-permute-start | bytes 393224 | tf_op jit(solution)/shard_map/ppermute | solution.py:39
  98.0 2.1 %collective-permute-start.26 = (bf16[1024,256]{1,0:T(8,128)(2,1)}, bf16[1024,256]{1,0:T(8,128)(2,1)}, u32[]{:S(2)}, u32[]{:S(2)}) collective-permute-start(bf16[1024,256]{1,0:T(8,128)(2,1)} %convolution_convert_fusion.2), channel_id=1, source_target_pairs={{0,3},{1,0},{2,1},{3,2},{4,7},{5,4},{6,5},{7,6},{8,11},{9,8},{10,9... | collective-permute-start | bytes 1572872 | tf_op jit(solution)/shard_map/ppermute | solution.py:39
  100.1 5.1 %weight_grads.3 = (bf16[8,256,256]{2,1,0:T(8,128)(2,1)S(1)}, bf16[8,256,256]{2,1,0:T(8,128)(2,1)}) custom-call(s32[16]{0:T(128)S(1)} %fusion.64.slots, bf16[1024,256]{1,0:T(8,128)(2,1)S(1)} %constant_dynamic-update-slice_fusion.refs_0_, bf16[1024,256]{1,0:T(8,128)(2,1)S(1)} %collective-permute-done.6.refs_1_, ...), custom_call_target="tpu_custom_call" | custom-call | flops 536870912 | bytes 4194304 | tf_op jit(solution)/shard_map/weight_grads/pallas_call | solution.py:129
  110.1 7.2 %collective-permute-done.27 = bf16[1024,256]{1,0:T(8,128)(2,1)} collective-permute-done((bf16[1024,256]{1,0:T(8,128)(2,1)}, bf16[1024,256]{1,0:T(8,128)(2,1)}, u32[]{:S(2)}, u32[]{:S(2)}) %collective-permute-start.27) | collective-permute-done | bytes 524320 | tf_op jit(solution)/shard_map/ppermute | solution.py:39
  117.3 5.4 %collective-permute-done.28 = bf16[1024,256]{1,0:T(8,128)(2,1)} collective-permute-done((bf16[1024,256]{1,0:T(8,128)(2,1)}, bf16[1024,256]{1,0:T(8,128)(2,1)}, u32[]{:S(2)}, u32[]{:S(2)}) %collective-permute-start.28) | collective-permute-done | bytes 524320 | tf_op jit(solution)/shard_map/ppermute | solution.py:39
  122.7 2.1 %fusion.4 = bf16[1024,256]{1,0:T(8,128)(2,1)S(1)} fusion(bf16[256,384]{1,0:T(8,128)(2,1)S(1)} %pad_maximum_fusion.1, bf16[1024,256]{1,0:T(8,128)(2,1)} %collective-permute-done.28, bf16[1024,256]{1,0:T(8,128)(2,1)} %collective-permute-done.27, bf16[1024,256]{1,0:T(8,128)(2,1)} %collective-permute-done.26, bf16[4096,384]{1,0:T(8,128)(2,1)} %copy-done.6), kind=kOutput, calls=%fused_computation.10 | convolution fusion | flops 203685888 | bytes 3080192 | tf_op jit(solution)/shard_map/dot_general | solution.py:23
  127.4 2.0 %collective-permute-start.30 = (bf16[256,256]{1,0:T(8,128)(2,1)S(1)}, bf16[256,256]{1,0:T(8,128)(2,1)S(1)}, u32[]{:S(2)}, u32[]{:S(2)}) collective-permute-start(bf16[256,256]{1,0:T(8,128)(2,1)S(1)} %get-tuple-element.88), channel_id=1, source_target_pairs={{0,8},{1,9},{2,10},{3,11},{4,12},{5,13},{6,14},{7,15},{8,0},{9,1},... | collective-permute-start | bytes 393224 | tf_op jit(solution)/shard_map/ppermute | solution.py:39
  130.3 2.0 %collective-permute-start.33 = (bf16[2,256,256]{2,1,0:T(8,128)(2,1)}, bf16[2,256,256]{2,1,0:T(8,128)(2,1)S(1)}, u32[]{:S(2)}, u32[]{:S(2)}) collective-permute-start(bf16[2,256,256]{2,1,0:T(8,128)(2,1)} %get-tuple-element.79), channel_id=1, source_target_pairs={{0,32},{32,64},{64,96},{96,0},{1,33},{33,65},{65,97},{97,1},{2,34}... | collective-permute-start | bytes 786440 | tf_op jit(solution)/shard_map/ppermute | solution.py:43
  134.0 2.1 %collective-permute-start.34 = (bf16[2,256,256]{2,1,0:T(8,128)(2,1)}, bf16[2,256,256]{2,1,0:T(8,128)(2,1)}, u32[]{:S(2)}, u32[]{:S(2)}) collective-permute-start(bf16[2,256,256]{2,1,0:T(8,128)(2,1)} %get-tuple-element.81), channel_id=1, source_target_pairs={{0,64},{32,96},{64,0},{96,32},{1,65},{33,97},{65,1},{97,33},{2,66}... | collective-permute-start | bytes 786440 | tf_op jit(solution)/shard_map/ppermute | solution.py:43
  140.8 1.9 %collective-permute-start.39 = (bf16[2,256,256]{2,1,0:T(8,128)(2,1)}, bf16[2,256,256]{2,1,0:T(8,128)(2,1)}, u32[]{:S(2)}, u32[]{:S(2)}) collective-permute-start(bf16[2,256,256]{2,1,0:T(8,128)(2,1)} %get-tuple-element.77), channel_id=1, source_target_pairs={{0,96},{32,0},{64,32},{96,64},{1,97},{33,1},{65,33},{97,65},{2,98}... | collective-permute-start | bytes 786440 | tf_op jit(solution)/shard_map/ppermute | solution.py:43
  142.7 1.8 %collective-permute-start.38 = (bf16[2,256,256]{2,1,0:T(8,128)(2,1)}, bf16[2,256,256]{2,1,0:T(8,128)(2,1)}, u32[]{:S(2)}, u32[]{:S(2)}) collective-permute-start(bf16[2,256,256]{2,1,0:T(8,128)(2,1)} %get-tuple-element.78), channel_id=1, source_target_pairs={{0,64},{32,96},{64,0},{96,32},{1,65},{33,97},{65,1},{97,33},{2,66}... | collective-permute-start | bytes 786440 | tf_op jit(solution)/shard_map/ppermute | solution.py:43
  147.8 2.3 %collective-permute-done.37 = bf16[2,256,256]{2,1,0:T(8,128)(2,1)S(1)} collective-permute-done((bf16[2,256,256]{2,1,0:T(8,128)(2,1)}, bf16[2,256,256]{2,1,0:T(8,128)(2,1)S(1)}, u32[]{:S(2)}, u32[]{:S(2)}) %collective-permute-start.37) | collective-permute-done | bytes 262176 | tf_op jit(solution)/shard_map/ppermute | solution.py:43
  150.2 2.8 %collective-permute-done.38 = bf16[2,256,256]{2,1,0:T(8,128)(2,1)} collective-permute-done((bf16[2,256,256]{2,1,0:T(8,128)(2,1)}, bf16[2,256,256]{2,1,0:T(8,128)(2,1)}, u32[]{:S(2)}, u32[]{:S(2)}) %collective-permute-start.38) | collective-permute-done | bytes 262176 | tf_op jit(solution)/shard_map/ppermute | solution.py:43
  (141 shorter events, 64.9 us)
Async XLA Ops:
  4.8 14.5 %collective-permute-start.4 = (bf16[256,256]{1,0:T(8,128)(2,1)S(1)}, bf16[256,256]{1,0:T(8,128)(2,1)}, u32[]{:S(2)}, u32[]{:S(2)}) collective-permute-start(bf16[256,256]{1,0:T(8,128)(2,1)S(1)} %bitcast.48), channel_id=1, source_target_pairs={{0,8},{1,9},{2,10},{3,11},{4,12},{5,13},{6,14},{7,15},{8,0},{9,1},... | collective-permute-start | bytes 393224 | tf_op jit(solution)/shard_map/ppermute | solution.py:39
  5.4 13.9 %collective-permute-start.3 = (bf16[256,256]{1,0:T(8,128)(2,1)S(1)}, bf16[256,256]{1,0:T(8,128)(2,1)}, u32[]{:S(2)}, u32[]{:S(2)}) collective-permute-start(bf16[256,256]{1,0:T(8,128)(2,1)S(1)} %bitcast.49), channel_id=1, source_target_pairs={{0,4},{1,5},{2,6},{3,7},{4,8},{5,9},{6,10},{7,11},{8,12},{9,13},{1... | collective-permute-start | bytes 393224 | tf_op jit(solution)/shard_map/ppermute | solution.py:39
  7.4 11.9 %collective-permute-start.2 = (bf16[256,256]{1,0:T(8,128)(2,1)S(1)}, bf16[256,256]{1,0:T(8,128)(2,1)S(1)}, u32[]{:S(2)}, u32[]{:S(2)}) collective-permute-start(bf16[256,256]{1,0:T(8,128)(2,1)S(1)} %bitcast.43), channel_id=1, source_target_pairs={{0,12},{1,13},{2,14},{3,15},{4,0},{5,1},{6,2},{7,3},{8,4},{9,5},{1... | collective-permute-start | bytes 393224 | tf_op jit(solution)/shard_map/ppermute | solution.py:39
  21.2 16.4 %collective-permute-start.8 = (bf16[1024,256]{1,0:T(8,128)(2,1)S(1)}, bf16[1024,256]{1,0:T(8,128)(2,1)S(1)}, u32[]{:S(2)}, u32[]{:S(2)}) collective-permute-start(bf16[1024,256]{1,0:T(8,128)(2,1)S(1)} %constant_dynamic-update-slice_fusion.refs_0_), channel_id=1, source_target_pairs={{0,3},{1,0},{2,1},{3,2},{4,7},{5,4},{6,5},{7,6},{8,11},{9,8},{10,9... | collective-permute-start | bytes 1572872 | tf_op jit(solution)/shard_map/ppermute | solution.py:39
  25.3 12.3 %collective-permute-start.7 = (bf16[1024,256]{1,0:T(8,128)(2,1)S(1)}, bf16[1024,256]{1,0:T(8,128)(2,1)S(1)}, u32[]{:S(2)}, u32[]{:S(2)}) collective-permute-start(bf16[1024,256]{1,0:T(8,128)(2,1)S(1)} %constant_dynamic-update-slice_fusion.refs_0_), channel_id=1, source_target_pairs={{0,2},{1,3},{2,0},{3,1},{4,6},{5,7},{6,4},{7,5},{8,10},{9,11},{10,... | collective-permute-start | bytes 1572872 | tf_op jit(solution)/shard_map/ppermute | solution.py:39
  25.3 16.0 %collective-permute-start.6 = (bf16[1024,256]{1,0:T(8,128)(2,1)S(1)}, bf16[1024,256]{1,0:T(8,128)(2,1)S(1)}, u32[]{:S(2)}, u32[]{:S(2)}) collective-permute-start(bf16[1024,256]{1,0:T(8,128)(2,1)S(1)} %constant_dynamic-update-slice_fusion.refs_0_), channel_id=1, source_target_pairs={{0,1},{1,2},{2,3},{3,0},{4,5},{5,6},{6,7},{7,4},{8,9},{9,10},{10,1... | collective-permute-start | bytes 1572872 | tf_op jit(solution)/shard_map/ppermute | solution.py:39
  46.9 10.7 %collective-permute-start.14 = (bf16[1024,256]{1,0:T(8,128)(2,1)S(1)}, bf16[1024,256]{1,0:T(8,128)(2,1)S(1)}, u32[]{:S(2)}, u32[]{:S(2)}) collective-permute-start(bf16[1024,256]{1,0:T(8,128)(2,1)S(1)} %pad_maximum_fusion.refs_5_), channel_id=1, source_target_pairs={{0,2},{1,3},{2,0},{3,1},{4,6},{5,7},{6,4},{7,5},{8,10},{9,11},{10,... | collective-permute-start | bytes 1572872 | tf_op jit(solution)/shard_map/ppermute | solution.py:39
  51.7 11.6 %collective-permute-start.13 = (bf16[1024,256]{1,0:T(8,128)(2,1)S(1)}, bf16[1024,256]{1,0:T(8,128)(2,1)S(1)}, u32[]{:S(2)}, u32[]{:S(2)}) collective-permute-start(bf16[1024,256]{1,0:T(8,128)(2,1)S(1)} %pad_maximum_fusion.refs_5_), channel_id=1, source_target_pairs={{0,1},{1,2},{2,3},{3,0},{4,5},{5,6},{6,7},{7,4},{8,9},{9,10},{10,1... | collective-permute-start | bytes 1572872 | tf_op jit(solution)/shard_map/ppermute | solution.py:39
  68.8 12.9 %collective-permute-start.20 = (bf16[1024,256]{1,0:T(8,128)(2,1)S(1)}, bf16[1024,256]{1,0:T(8,128)(2,1)S(1)}, u32[]{:S(2)}, u32[]{:S(2)}) collective-permute-start(bf16[1024,256]{1,0:T(8,128)(2,1)S(1)} %convolution_convert_fusion.6), channel_id=1, source_target_pairs={{0,3},{1,0},{2,1},{3,2},{4,7},{5,4},{6,5},{7,6},{8,11},{9,8},{10,9... | collective-permute-start | bytes 1572872 | tf_op jit(solution)/shard_map/ppermute | solution.py:39
  69.7 12.0 %collective-permute-start.21 = (bf16[1024,256]{1,0:T(8,128)(2,1)S(1)}, bf16[1024,256]{1,0:T(8,128)(2,1)S(1)}, u32[]{:S(2)}, u32[]{:S(2)}) collective-permute-start(bf16[1024,256]{1,0:T(8,128)(2,1)S(1)} %convolution_convert_fusion.5), channel_id=1, source_target_pairs={{0,2},{1,3},{2,0},{3,1},{4,6},{5,7},{6,4},{7,5},{8,10},{9,11},{10,... | collective-permute-start | bytes 1572872 | tf_op jit(solution)/shard_map/ppermute | solution.py:39
  79.4 11.0 %collective-permute-start.22 = (bf16[1024,256]{1,0:T(8,128)(2,1)S(1)}, bf16[1024,256]{1,0:T(8,128)(2,1)S(1)}, u32[]{:S(2)}, u32[]{:S(2)}) collective-permute-start(bf16[1024,256]{1,0:T(8,128)(2,1)S(1)} %convolution_convert_fusion.4), channel_id=1, source_target_pairs={{0,1},{1,2},{2,3},{3,0},{4,5},{5,6},{6,7},{7,4},{8,9},{9,10},{10,1... | collective-permute-start | bytes 1572872 | tf_op jit(solution)/shard_map/ppermute | solution.py:39
  80.6 28.0 %collective-permute-start.32 = (bf16[8,256,256]{2,1,0:T(8,128)(2,1)}, bf16[8,256,256]{2,1,0:T(8,128)(2,1)}, u32[]{:S(2)}, u32[]{:S(2)}) collective-permute-start(bf16[8,256,256]{2,1,0:T(8,128)(2,1)} %get-tuple-element.66), channel_id=1, source_target_pairs={{0,16},{16,0},{1,17},{17,1},{2,18},{18,2},{3,19},{19,3},{4,20},{20... | collective-permute-start | bytes 3145736 | tf_op jit(solution)/shard_map/ppermute | solution.py:47
  90.7 15.5 %collective-permute-start.23 = (bf16[256,256]{1,0:T(8,128)(2,1)S(1)}, bf16[256,256]{1,0:T(8,128)(2,1)S(1)}, u32[]{:S(2)}, u32[]{:S(2)}) collective-permute-start(bf16[256,256]{1,0:T(8,128)(2,1)S(1)} %get-tuple-element.89), channel_id=1, source_target_pairs={{0,12},{1,13},{2,14},{3,15},{4,0},{5,1},{6,2},{7,3},{8,4},{9,5},{1... | collective-permute-start | bytes 393224 | tf_op jit(solution)/shard_map/ppermute | solution.py:39
  92.6 13.7 %collective-permute-start.25 = (bf16[256,256]{1,0:T(8,128)(2,1)S(1)}, bf16[256,256]{1,0:T(8,128)(2,1)S(1)}, u32[]{:S(2)}, u32[]{:S(2)}) collective-permute-start(bf16[256,256]{1,0:T(8,128)(2,1)S(1)} %get-tuple-element.90), channel_id=1, source_target_pairs={{0,4},{1,5},{2,6},{3,7},{4,8},{5,9},{6,10},{7,11},{8,12},{9,13},{1... | collective-permute-start | bytes 393224 | tf_op jit(solution)/shard_map/ppermute | solution.py:39
  92.8 14.9 %collective-permute-start.24 = (bf16[256,256]{1,0:T(8,128)(2,1)S(1)}, bf16[256,256]{1,0:T(8,128)(2,1)S(1)}, u32[]{:S(2)}, u32[]{:S(2)}) collective-permute-start(bf16[256,256]{1,0:T(8,128)(2,1)S(1)} %get-tuple-element.91), channel_id=1, source_target_pairs={{0,8},{1,9},{2,10},{3,11},{4,12},{5,13},{6,14},{7,15},{8,0},{9,1},... | collective-permute-start | bytes 393224 | tf_op jit(solution)/shard_map/ppermute | solution.py:39
  98.0 12.1 %collective-permute-start.26 = (bf16[1024,256]{1,0:T(8,128)(2,1)}, bf16[1024,256]{1,0:T(8,128)(2,1)}, u32[]{:S(2)}, u32[]{:S(2)}) collective-permute-start(bf16[1024,256]{1,0:T(8,128)(2,1)} %convolution_convert_fusion.2), channel_id=1, source_target_pairs={{0,3},{1,0},{2,1},{3,2},{4,7},{5,4},{6,5},{7,6},{8,11},{9,8},{10,9... | collective-permute-start | bytes 1572872 | tf_op jit(solution)/shard_map/ppermute | solution.py:39
  106.2 11.1 %collective-permute-start.27 = (bf16[1024,256]{1,0:T(8,128)(2,1)}, bf16[1024,256]{1,0:T(8,128)(2,1)}, u32[]{:S(2)}, u32[]{:S(2)}) collective-permute-start(bf16[1024,256]{1,0:T(8,128)(2,1)} %convolution_convert_fusion.1), channel_id=1, source_target_pairs={{0,2},{1,3},{2,0},{3,1},{4,6},{5,7},{6,4},{7,5},{8,10},{9,11},{10,... | collective-permute-start | bytes 1572872 | tf_op jit(solution)/shard_map/ppermute | solution.py:39
  106.3 16.3 %collective-permute-start.28 = (bf16[1024,256]{1,0:T(8,128)(2,1)}, bf16[1024,256]{1,0:T(8,128)(2,1)}, u32[]{:S(2)}, u32[]{:S(2)}) collective-permute-start(bf16[1024,256]{1,0:T(8,128)(2,1)} %convolution_convert_fusion), channel_id=1, source_target_pairs={{0,1},{1,2},{2,3},{3,0},{4,5},{5,6},{6,7},{7,4},{8,9},{9,10},{10,1... | collective-permute-start | bytes 1572872 | tf_op jit(solution)/shard_map/ppermute | solution.py:39
  107.7 29.3 %collective-permute-start.36 = (bf16[8,256,256]{2,1,0:T(8,128)(2,1)}, bf16[8,256,256]{2,1,0:T(8,128)(2,1)}, u32[]{:S(2)}, u32[]{:S(2)}) collective-permute-start(bf16[8,256,256]{2,1,0:T(8,128)(2,1)} %get-tuple-element.68), channel_id=1, source_target_pairs={{0,16},{16,0},{1,17},{17,1},{2,18},{18,2},{3,19},{19,3},{4,20},{20... | collective-permute-start | bytes 3145736 | tf_op jit(solution)/shard_map/ppermute | solution.py:47
  130.3 12.4 %collective-permute-start.33 = (bf16[2,256,256]{2,1,0:T(8,128)(2,1)}, bf16[2,256,256]{2,1,0:T(8,128)(2,1)S(1)}, u32[]{:S(2)}, u32[]{:S(2)}) collective-permute-start(bf16[2,256,256]{2,1,0:T(8,128)(2,1)} %get-tuple-element.79), channel_id=1, source_target_pairs={{0,32},{32,64},{64,96},{96,0},{1,33},{33,65},{65,97},{97,1},{2,34}... | collective-permute-start | bytes 786440 | tf_op jit(solution)/shard_map/ppermute | solution.py:43
  132.3 12.2 %collective-permute-start.35 = (bf16[2,256,256]{2,1,0:T(8,128)(2,1)}, bf16[2,256,256]{2,1,0:T(8,128)(2,1)}, u32[]{:S(2)}, u32[]{:S(2)}) collective-permute-start(bf16[2,256,256]{2,1,0:T(8,128)(2,1)} %get-tuple-element.80), channel_id=1, source_target_pairs={{0,96},{32,0},{64,32},{96,64},{1,97},{33,1},{65,33},{97,65},{2,98}... | collective-permute-start | bytes 786440 | tf_op jit(solution)/shard_map/ppermute | solution.py:43
  134.0 11.0 %collective-permute-start.34 = (bf16[2,256,256]{2,1,0:T(8,128)(2,1)}, bf16[2,256,256]{2,1,0:T(8,128)(2,1)}, u32[]{:S(2)}, u32[]{:S(2)}) collective-permute-start(bf16[2,256,256]{2,1,0:T(8,128)(2,1)} %get-tuple-element.81), channel_id=1, source_target_pairs={{0,64},{32,96},{64,0},{96,32},{1,65},{33,97},{65,1},{97,33},{2,66}... | collective-permute-start | bytes 786440 | tf_op jit(solution)/shard_map/ppermute | solution.py:43
  139.4 10.6 %collective-permute-start.37 = (bf16[2,256,256]{2,1,0:T(8,128)(2,1)}, bf16[2,256,256]{2,1,0:T(8,128)(2,1)S(1)}, u32[]{:S(2)}, u32[]{:S(2)}) collective-permute-start(bf16[2,256,256]{2,1,0:T(8,128)(2,1)} %get-tuple-element.76), channel_id=1, source_target_pairs={{0,32},{32,64},{64,96},{96,0},{1,33},{33,65},{65,97},{97,1},{2,34}... | collective-permute-start | bytes 786440 | tf_op jit(solution)/shard_map/ppermute | solution.py:43
  142.7 10.3 %collective-permute-start.38 = (bf16[2,256,256]{2,1,0:T(8,128)(2,1)}, bf16[2,256,256]{2,1,0:T(8,128)(2,1)}, u32[]{:S(2)}, u32[]{:S(2)}) collective-permute-start(bf16[2,256,256]{2,1,0:T(8,128)(2,1)} %get-tuple-element.78), channel_id=1, source_target_pairs={{0,64},{32,96},{64,0},{96,32},{1,65},{33,97},{65,1},{97,33},{2,66}... | collective-permute-start | bytes 786440 | tf_op jit(solution)/shard_map/ppermute | solution.py:43
  (25 other events, 178.4 us)

commit v3 on v2

v3 whole, which is shorter than its diff:
```python
import jax
import jax.numpy as jnp
from jax import lax
from jax.experimental import pallas as pl
from jax.experimental.pallas import tpu as pltpu
from jax.sharding import Mesh
from jax.sharding import PartitionSpec as P

SEQ = ("x", "core")
HEAD = ("y", "z")
PLANE = ("core", "y", "z")
SIDE = 4
EPSILON = 1e-06
WIDE = jnp.float32
HALF = jnp.bfloat16

NN = (((1,), (0,)), ((), ()))
NT = (((1,), (1,)), ((), ()))
TN = (((0,), (0,)), ((), ()))


def mm(a, b, dims):
    return lax.dot_general(a, b, dims, preferred_element_type=WIDE)


def after(first, then):
    return lax.optimization_barrier((first, then))[1]


def plane_pairs(phase, shift):
    pairs = []
    for core in range(2):
        for y in range(SIDE):
            for z in range(SIDE):
                along_y = core == phase
                ty = (y + shift) % SIDE if along_y else y
                tz = z if along_y else (z + shift) % SIDE
                pairs.append(((core * SIDE + y) * SIDE + z, (core * SIDE + ty) * SIDE + tz))
    return pairs


def plane_shift(a, phase, shift):
    return lax.ppermute(a, PLANE, plane_pairs(phase, shift))


def x_shift(a, shift):
    return lax.ppermute(a, "x", [(i, (i + shift) % SIDE) for i in range(SIDE)])


def x_outward(a):
    pairs = []
    for i in range(SIDE):
        pairs.append((2 * i, 2 * ((i + 1) % SIDE)))
        pairs.append((2 * i + 1, 2 * ((i - 1) % SIDE) + 1))
    return lax.ppermute(a, SEQ, pairs)


def core_swap(a):
    return lax.ppermute(a, "core", [(0, 1), (1, 0)])


def block_tables():
    core, y, z = (lax.axis_index(n) for n in PLANE)
    at = jnp.arange(SIDE * SIDE, dtype=jnp.int32)
    d2, d1 = at // SIDE, at % SIDE
    from_y = (y - jnp.where(core == 0, d1, d2)) % SIDE
    from_z = (z - jnp.where(core == 0, d2, d1)) % SIDE
    other_core = (from_z // 2 + core) % 2
    slots = other_core * 8 + from_y * 2 + from_z % 2
    return from_y * SIDE + from_z, slots


def order_weights_kernel(table, q, k, v, o, qkv_out, o_out):
    n = q.shape[1]
    step = q.shape[0] // (SIDE * SIDE)
    for i in range(SIDE * SIDE):
        at = pl.ds(pl.multiple_of(table[i] * step, step), step)
        to = slice(i * step, (i + 1) * step)
        qkv_out[to, :n] = q[at, :]
        qkv_out[to, n : 2 * n] = k[at, :]
        qkv_out[to, 2 * n :] = v[at, :]
        o_out[to, :] = o[:, at].T


def order_weights(table, w_query, w_key, w_value, w_out):
    rows, n = w_query.shape
    tall = pl.BlockSpec((rows, n), lambda i: (0, 0))
    return pl.pallas_call(
        order_weights_kernel,
        out_shape=(
            jax.ShapeDtypeStruct((rows, 3 * n), HALF),
            jax.ShapeDtypeStruct((rows, n), HALF),
        ),
        grid=(1,),
        in_specs=[pl.BlockSpec(memory_space=pltpu.SMEM), tall, tall, tall]
        + [pl.BlockSpec((n, rows), lambda i: (0, 0))],
        out_specs=(pl.BlockSpec((rows, 3 * n), lambda i: (0, 0)), tall),
        compiler_params=pltpu.CompilerParams(vmem_limit_bytes=18 << 20),
        cost_estimate=pl.CostEstimate(
            flops=0, bytes_accessed=16 * rows * n, transcendentals=0
        ),
        name="order_weights",
    )(table, w_query, w_key, w_value, w_out)


def sort_blocks_kernel(slots, a0, a1, a2, a3, out):
    step = a0.shape[0] // SIDE
    for d2, part in enumerate((a0, a1, a2, a3)):
        for d1 in range(SIDE):
            out[slots[d2 * SIDE + d1]] = part[d1 * step : (d1 + 1) * step, :]


def sort_blocks(slots, parts):
    rows, n = parts[0].shape
    shape = (SIDE * SIDE, rows // SIDE, n)
    return pl.pallas_call(
        sort_blocks_kernel,
        out_shape=jax.ShapeDtypeStruct(shape, HALF),
        grid=(1,),
        in_specs=[pl.BlockSpec(memory_space=pltpu.SMEM)]
        + [pl.BlockSpec((rows, n), lambda i: (0, 0))] * SIDE,
        out_specs=pl.BlockSpec(shape, lambda i: (0, 0, 0)),
        compiler_params=pltpu.CompilerParams(vmem_limit_bytes=9 << 20),
        cost_estimate=pl.CostEstimate(
            flops=0, bytes_accessed=16 * rows * n, transcendentals=0
        ),
        name="sort_blocks",
    )(slots, *parts)


def weight_grads_kernel(t_own, t_other, g_own, g_other, d_own, d_other, out):
    n = d_own.shape[1]
    split = n - n // SIDE
    for s in range(t_own.shape[0]):
        for own, other, at in ((t_own, t_other, slice(0, split)), (g_own, g_other, slice(split, n))):
            term = jnp.dot(own[s], d_own[:, at], preferred_element_type=WIDE)
            term = term + jnp.dot(other[s], d_other[:, at], preferred_element_type=WIDE)
            out[s, :, at] = term.astype(HALF)


def weight_grads(t_sorted, t_other, g_sorted, g_other, d_own, d_other):
    half, step, tokens = t_other.shape
    n = d_own.shape[1]
    first = pl.BlockSpec((half, step, tokens), lambda i: (0, 0, 0))
    flat = pl.BlockSpec((tokens, n), lambda i: (0, 0))
    return pl.pallas_call(
        weight_grads_kernel,
        out_shape=jax.ShapeDtypeStruct((half, step, n), HALF),
        grid=(1,),
        in_specs=[first] * 4 + [flat] * 2,
        out_specs=pl.BlockSpec((half, step, n), lambda i: (0, 0, 0)),
        compiler_params=pltpu.CompilerParams(vmem_limit_bytes=14 << 20),
        cost_estimate=pl.CostEstimate(
            flops=4 * half * step * tokens * n,
            bytes_accessed=2 * half * step * (4 * tokens + n),
            transcendentals=0,
        ),
        name="weight_grads",
    )(t_sorted, t_other, g_sorted, g_other, d_own, d_other)


def part_terms_kernel(w, cotangent, out):
    step = w.shape[0] // SIDE
    for i in range(SIDE):
        at = slice(i * step, (i + 1) * step)
        out[at, :] = mm(cotangent[...], w[at, :], NT).astype(HALF)


def part_terms(weights, part, cotangent):
    rows, n = weights.shape
    rows = rows // SIDE
    tokens = cotangent.shape[0]
    return pl.pallas_call(
        part_terms_kernel,
        out_shape=jax.ShapeDtypeStruct((SIDE * tokens, rows // SIDE), HALF),
        grid=(1,),
        in_specs=[
            pl.BlockSpec((rows, n), lambda i: (part, 0)),
            pl.BlockSpec((tokens, n), lambda i: (0, 0)),
        ],
        out_specs=pl.BlockSpec((SIDE * tokens, rows // SIDE), lambda i: (0, 0)),
        compiler_params=pltpu.CompilerParams(vmem_limit_bytes=4 << 20),
        cost_estimate=pl.CostEstimate(
            flops=2 * rows * n * tokens, bytes_accessed=2 * rows * (n + tokens), transcendentals=0
        ),
        name="part_terms",
    )(weights, cotangent)


def x_spread(blocks):
    _, step, n = blocks.shape
    return lax.all_to_all(blocks.reshape(SIDE, 2 * step, n), "x", 0, 0, tiled=True)


def split_sum_kernel(got, q, k, v, o):
    n = q.shape[1]
    for i, out in enumerate((q, k, v, o)):
        at = slice(i * n, (i + 1) * n)
        acc = got[0, :, at].astype(WIDE)
        for d in range(1, SIDE):
            acc = acc + got[d, :, at].astype(WIDE)
        out[...] = acc if out is not o else acc.T


def split_sum(got):
    _, rows, width = got.shape
    n = width // SIDE
    flat = pl.BlockSpec((rows, n), lambda i: (0, 0))
    tall = jax.ShapeDtypeStruct((rows, n), WIDE)
    return pl.pallas_call(
        split_sum_kernel,
        out_shape=(tall, tall, tall, jax.ShapeDtypeStruct((n, rows), WIDE)),
        grid=(1,),
        in_specs=[pl.BlockSpec(got.shape, lambda i: (0, 0, 0))],
        out_specs=(flat, flat, flat, pl.BlockSpec((n, rows), lambda i: (0, 0))),
        compiler_params=pltpu.CompilerParams(vmem_limit_bytes=7 << 20),
        cost_estimate=pl.CostEstimate(
            flops=SIDE * rows * width, bytes_accessed=12 * rows * width, transcendentals=0
        ),
        name="split_sum",
    )(got)


def spread_phase1(a):
    return [a] + [plane_shift(a, 0, d) for d in range(1, SIDE)]


def spread_phase2(a):
    return [a] + [plane_shift(a, 1, d) for d in range(1, SIDE)]


def total(parts):
    acc = parts[0].astype(WIDE)
    for p in parts[1:]:
        acc = acc + p.astype(WIDE)
    return acc


def fold_phase1(terms):
    return [terms[0]] + [plane_shift(t, 1, -d) for d, t in enumerate(terms) if d]


def fold_phase2(mine):
    step = mine[0].shape[0] // SIDE
    parts = [jnp.stack([m[d * step : (d + 1) * step] for m in mine]) for d in range(SIDE)]
    return [parts[0]] + [plane_shift(p, 0, -d) for d, p in enumerate(parts) if d]


def pair_sums(own, other):
    core = lax.axis_index("core")
    pair = (own.astype(WIDE) + other.astype(WIDE)).astype(HALF)
    near, far = lax.optimization_barrier((x_outward(pair), x_shift(pair, 2)))
    across = core_swap(near)
    return [
        pair,
        jnp.where(core == 0, near, across),
        far,
        jnp.where(core == 0, across, near),
    ]


def masked_sum(first, parts, keep):
    acc = first
    for part, k in zip(parts, keep):
        acc = acc + jnp.where(k, part.astype(WIDE), 0.0)
    return acc


def on_device(tokens, w_query, w_key, w_value, w_out, grad_out, state_in):
    x, core = lax.axis_index("x"), lax.axis_index("core")
    dh = w_query.shape[1]
    rows = tokens.shape[0]
    table, slots = block_tables()

    t1 = jnp.concatenate(spread_phase1(tokens.T), axis=0)
    g1 = jnp.concatenate(spread_phase1(grad_out.T), axis=0)
    t1, raw = lax.optimization_barrier((t1, (w_query, w_key, w_value, w_out)))
    t_parts = spread_phase2(t1)
    w_qkv, w_o = order_weights(table, *raw)
    g_parts = spread_phase2(g1)
    step = g1.shape[0]
    wq_parts = [w_qkv[d * step : (d + 1) * step] for d in range(SIDE)]
    wo_parts = [w_o[d * step : (d + 1) * step] for d in range(SIDE)]

    qkv = sum(mm(t, w, TN) for t, w in zip(t_parts, wq_parts)).astype(HALF)
    query, keys, values = (qkv[:, i * dh : (i + 1) * dh] for i in range(3))

    own_state = mm(keys, values, TN).astype(HALF)
    other = core_swap(own_state)
    g_parts = after(other, g_parts)
    pairs = pair_sums(own_state, other)
    prior = masked_sum(
        state_in[0], [other] + pairs[1:], [core == 1] + [x >= d for d in range(1, SIDE)]
    ).astype(HALF)

    allowed = jnp.tril(jnp.ones((rows, rows), jnp.bool_))
    scores = jnp.where(allowed, mm(query, keys, NT), 0.0).astype(HALF)
    mixed = mm(scores, values, NN) + mm(query, prior, NN)
    inv_norm = lax.rsqrt(jnp.mean(mixed * mixed, axis=-1, keepdims=True) + EPSILON)
    normed = (mixed * inv_norm).astype(HALF)
    out_terms = [part_terms(w_o, d, normed) for d in range(SIDE)]
    out_got = fold_phase1(out_terms)

    grad_normed = sum(mm(g, w, TN) for g, w in zip(g_parts, wo_parts))
    grad_mixed = inv_norm * (
        grad_normed
        - mixed * inv_norm * inv_norm * jnp.mean(grad_normed * mixed, axis=-1, keepdims=True)
    )
    grad_mixed = grad_mixed.astype(HALF)
    own_back = mm(query, grad_mixed, TN).astype(HALF)
    half = SIDE * SIDE // 2
    t_sorted, g_sorted = sort_blocks(slots, t_parts), sort_blocks(slots, g_parts)
    t_other, g_other = (core_swap(after(prior, a[half:])) for a in (t_sorted, g_sorted))
    own_back = after((t_other, g_other), own_back)
    other_back = core_swap(own_back)
    back_pairs = pair_sums(own_back, other_back)

    grad_scores = jnp.where(allowed, mm(grad_mixed, values, NT), 0.0).astype(HALF)
    grad_query = (mm(grad_scores, keys, NN) + mm(grad_mixed, prior, NT)).astype(HALF)
    later = masked_sum(
        jnp.zeros((dh, dh), WIDE),
        [other_back] + back_pairs[1:],
        [core == 0] + [x < d for d in range(1, SIDE)],
    ).astype(HALF)
    grad_state = jnp.zeros((dh, dh), WIDE)
    for chip in range(SIDE):
        part = jnp.zeros((dh, dh), HALF)
        for d, p in enumerate(back_pairs):
            part = jnp.where((x - d) % SIDE == chip, p, part)
        grad_state = grad_state + part.astype(WIDE)

    grad_keys = (mm(grad_scores, query, TN) + mm(values, later, NT)).astype(HALF)
    grad_values = (mm(scores, grad_mixed, TN) + mm(keys, later, NN)).astype(HALF)
    cotangents = jnp.concatenate([grad_query, grad_keys, grad_values, normed], axis=1)
    blocks = weight_grads(
        t_sorted, t_other, g_sorted, g_other, cotangents, core_swap(cotangents)
    )
    out_sum = total(out_got).astype(HALF)
    cotangents, out_sum, blocks = lax.optimization_barrier((cotangents, out_sum, blocks))
    in_terms = [part_terms(w_qkv, d, cotangents) for d in range(SIDE)]
    in_got = fold_phase1(in_terms)
    grads = split_sum(x_spread(after(in_terms, blocks)))
    got = fold_phase2((out_sum, total(in_got).astype(HALF)))
    sums = total(after(grads, got))
    result, grad_tokens = sums[0].astype(HALF), sums[1]
    return (
        result,
        grad_tokens,
        *grads,
        grad_state[None],
    )


def solution(mesh):
    sizes = (SIDE, mesh.shape["seq"] // SIDE, SIDE, SIDE)
    torus = Mesh(mesh.devices.reshape(sizes), SEQ + HEAD)
    seq_head = P(SEQ, HEAD)
    column = P(None, HEAD)
    return jax.shard_map(
        on_device,
        mesh=torus,
        in_specs=(seq_head, column, column, column, P(HEAD, None), seq_head, P(HEAD, None, None)),
        out_specs=(
            seq_head,
            seq_head,
            seq_head,
            seq_head,
            seq_head,
            P(HEAD, SEQ),
            P(HEAD, None, None),
        ),
        check_vma=False,
    )
```

time: 156 us -> 119 us (0.76)
  waiting for transfers between devices: 51.1 us -> 40.2 us
  local copies, waits for them, and re-layouts: 17.3 us -> 7.31 us
  matrix products: 14.9 us -> 5.5 us
  starting transfers between devices: 51.1 us -> 46.8 us
  other arithmetic: 8 us -> 5.92 us
    ppermute x24 -> x21, waiting for transfers between devices: 42.4 us -> 25.6 us  [plane_shift(): return lax.ppermute(a, PLANE, plane_pairs(phase, shift))]
    ppermute x12 -> x2, starting transfers between devices: 19.4 us -> 6.2 us  [x_shift(): return lax.ppermute(a, 'x', [(i, (i + shift) % SIDE) for i in range(SIDE)])]
    dot_general x28 -> x20, matrix products: 14.9 us -> 5.5 us  [mm(): return lax.dot_general(a, b, dims, preferred_element_type=WIDE)]
    unnamed x26 -> x12, local copies, waits for them, and re-layouts: 13.8 us -> 4.61 us
    all_to_all x0 -> x1, waiting for transfers between devices: none -> 9.02 us  [x_spread(): lax.all_to_all(blocks.reshape(SIDE, 2 * step, n), 'x', 0, 0, tiled=True)]
    ppermute x12 -> x2, waiting for transfers between devices: 8.7 us -> 0.01 us  [x_shift(): return lax.ppermute(a, 'x', [(i, (i + shift) % SIDE) for i in range(SIDE)])]
    ppermute x4 -> x7, waiting for transfers between devices: 0.04 us -> 4.39 us  [core_swap(): return lax.ppermute(a, 'core', [(0, 1), (1, 0)])]
    ppermute x24 -> x21, starting transfers between devices: 30.1 us -> 34.1 us  [plane_shift(): return lax.ppermute(a, PLANE, plane_pairs(phase, shift))]
  transfers between devices with their start and end apart: 40 -> 33, of which waited for: 14 -> 16; matrix products, arithmetic and copies ran while one was open for 13% -> 10% of each run, Pallas kernels for 7% -> 5%
where the time goes in v3:
time: 119 us; the launch traced here: 118 us
  starting transfers between devices  46.8 us (39%)
  waiting for transfers between devices  40.2 us (34%)
  Pallas kernels  11.6 us (10%)
  local copies, waits for them, and re-layouts  7.31 us (6%)
  other arithmetic  5.92 us (5%)
  matrix products  5.5 us (5%)
    ppermute x21, starting transfers between devices, plane_shift(): return lax.ppermute(a, PLANE, plane_pairs(phase, shift))  34.1 us
    ppermute x21, waiting for transfers between devices, plane_shift(): return lax.ppermute(a, PLANE, plane_pairs(phase, shift))  25.6 us
    all_to_all x1, waiting for transfers between devices, x_spread(): lax.all_to_all(blocks.reshape(SIDE, 2 * step, n), 'x', 0, 0, tiled=True)  9.02 us
    ppermute x2, starting transfers between devices, x_shift(): return lax.ppermute(a, 'x', [(i, (i + shift) % SIDE) for i in range(SIDE)])  6.2 us
    dot_general x20, matrix products, mm(): return lax.dot_general(a, b, dims, preferred_element_type=WIDE)  5.5 us
    pallas_call x8, Pallas kernels, part_terms(): pl.pallas_call(part_terms_kernel, out_shape=jax.ShapeDtypeStruct((SIDE *...  4.7 us
    unnamed x12, local copies, waits for them, and re-layouts  4.61 us
    ppermute x7, waiting for transfers between devices, core_swap(): return lax.ppermute(a, 'core', [(0, 1), (1, 0)])  4.39 us
  transfers between devices with their start and end apart: 33, of which 16 were waited for; matrix products, arithmetic and copies ran while one was open for 10% of the time, Pallas kernels for 5%

profile of v3, /device:TPU:0, one launch (start us, length us, event | category | flops | bytes accessed | tf_op | source)
XLA Modules:
  0.0 118.4 jit_solution(7319345113927244351)
XLA Ops:
  1.8 3.2 %collective-permute-start.2 = (bf16[256,256]{1,0:T(8,128)(2,1)S(1)}, bf16[256,256]{1,0:T(8,128)(2,1)S(1)}, u32[]{:S(2)}, u32[]{:S(2)}) collective-permute-start(bf16[256,256]{1,0:T(8,128)(2,1)S(1)} %bitcast.51), channel_id=1, source_target_pairs={{0,12},{1,13},{2,14},{3,15},{4,0},{5,1},{6,2},{7,3},{8,4},{9,5},{1... | collective-permute-start | bytes 393224 | tf_op jit(solution)/shard_map/ppermute | solution.py:43
  7.6 2.3 %collective-permute-start.12 = (bf16[256,256]{1,0:T(8,128)(2,1)S(1)}, bf16[256,256]{1,0:T(8,128)(2,1)S(1)}, u32[]{:S(2)}, u32[]{:S(2)}) collective-permute-start(bf16[256,256]{1,0:T(8,128)(2,1)S(1)} %bitcast.47), channel_id=1, source_target_pairs={{0,12},{1,13},{2,14},{3,15},{4,0},{5,1},{6,2},{7,3},{8,4},{9,5},{1... | collective-permute-start | bytes 393224 | tf_op jit(solution)/shard_map/ppermute | solution.py:43
  9.9 1.7 %collective-permute-start.11 = (bf16[256,256]{1,0:T(8,128)(2,1)S(1)}, bf16[256,256]{1,0:T(8,128)(2,1)S(1)}, u32[]{:S(2)}, u32[]{:S(2)}) collective-permute-start(bf16[256,256]{1,0:T(8,128)(2,1)S(1)} %bitcast.48), channel_id=1, source_target_pairs={{0,8},{1,9},{2,10},{3,11},{4,12},{5,13},{6,14},{7,15},{8,0},{9,1},... | collective-permute-start | bytes 393224 | tf_op jit(solution)/shard_map/ppermute | solution.py:43
  12.9 4.1 %collective-permute-start.5 = (bf16[1024,256]{1,0:T(8,128)(2,1)S(1)}, bf16[1024,256]{1,0:T(8,128)(2,1)S(1)}, u32[]{:S(2)}, u32[]{:S(2)}) collective-permute-start(bf16[1024,256]{1,0:T(8,128)(2,1)S(1)} %pad_maximum_fusion.a0), channel_id=1, source_target_pairs={{0,3},{1,0},{2,1},{3,2},{4,7},{5,4},{6,5},{7,6},{8,11},{9,8},{10,9... | collective-permute-start | bytes 1572872 | tf_op jit(solution)/shard_map/ppermute | solution.py:43
  19.4 9.9 %collective-permute-start.15 = (bf16[1024,256]{1,0:T(8,128)(2,1)S(1)}, bf16[1024,256]{1,0:T(8,128)(2,1)S(1)}, u32[]{:S(2)}, u32[]{:S(2)}) collective-permute-start(bf16[1024,256]{1,0:T(8,128)(2,1)S(1)} %pad_maximum_fusion.1.a0), channel_id=1, source_target_pairs={{0,3},{1,0},{2,1},{3,2},{4,7},{5,4},{6,5},{7,6},{8,11},{9,8},{10,9... | collective-permute-start | bytes 1572872 | tf_op jit(solution)/shard_map/ppermute | solution.py:43
  32.0 1.3 %order_weights.1 = (bf16[4096,384]{1,0:T(8,128)(2,1)S(1)}, bf16[4096,128]{1,0:T(8,128)(2,1)S(1)}) custom-call(s32[16]{0:T(128)S(1)} %multiply_add_fusion.table, bf16[4096,128]{1,0:T(8,128)(2,1)S(1)} %copy-done, bf16[4096,128]{1,0:T(8,128)(2,1)S(1)} %copy-done.1, bf16[4096,128]{1,0:T(8,128)(2,1)S(1)} %copy-done.2, bf16[128,4096]{1,0:T(8,128)(2,1)S(1)} %copy-done.3), custom_call_target="tpu_custom_call" | custom-call | bytes 8388608 | tf_op jit(solution)/shard_map/order_weights/pallas_call | solution.py:88
  33.7 1.4 %collective-permute-start.13 = (bf16[1024,256]{1,0:T(8,128)(2,1)S(1)}, bf16[1024,256]{1,0:T(8,128)(2,1)S(1)}, u32[]{:S(2)}, u32[]{:S(2)}) collective-permute-start(bf16[1024,256]{1,0:T(8,128)(2,1)S(1)} %pad_maximum_fusion.1.a0), channel_id=1, source_target_pairs={{0,1},{1,2},{2,3},{3,0},{4,5},{5,6},{6,7},{7,4},{8,9},{9,10},{10,1... | collective-permute-start | bytes 1572872 | tf_op jit(solution)/shard_map/ppermute | solution.py:43
  38.1 3.1 %collective-permute-start.8 = (bf16[128,128]{1,0:T(8,128)(2,1)S(1)}, bf16[128,128]{1,0:T(8,128)(2,1)S(1)}, u32[]{:S(2)}, u32[]{:S(2)}) collective-permute-start(bf16[128,128]{1,0:T(8,128)(2,1)S(1)} %fusion.28), channel_id=1, source_target_pairs={{0,64},{32,96},{64,0},{96,32},{1,65},{33,97},{65,1},{97,33},{2,66}... | collective-permute-start | bytes 98312 | tf_op jit(solution)/shard_map/ppermute | solution.py:47
  41.8 3.8 %collective-permute-done.13.a1 = bf16[1024,256]{1,0:T(8,128)(2,1)S(1)} collective-permute-done((bf16[1024,256]{1,0:T(8,128)(2,1)S(1)}, bf16[1024,256]{1,0:T(8,128)(2,1)S(1)}, u32[]{:S(2)}, u32[]{:S(2)}) %collective-permute-start.13) | collective-permute-done | bytes 524320 | tf_op jit(solution)/shard_map/ppermute | solution.py:43
  50.6 1.5 %collective-permute-done.16.t_other = bf16[8,256,256]{2,1,0:T(8,128)(2,1)S(1)} collective-permute-done((bf16[8,256,256]{2,1,0:T(8,128)(2,1)S(1)}, bf16[8,256,256]{2,1,0:T(8,128)(2,1)S(1)}, u32[]{:S(2)}, u32[]{:S(2)}) %collective-permute-start.16) | collective-permute-done | bytes 1048608 | tf_op jit(solution)/shard_map/ppermute | solution.py:59
  53.3 3.1 %collective-permute-start.20 = (bf16[128,128]{1,0:T(8,128)(2,1)S(1)}, bf16[128,128]{1,0:T(8,128)(2,1)S(1)}, u32[]{:S(2)}, u32[]{:S(2)}) collective-permute-start(bf16[128,128]{1,0:T(8,128)(2,1)S(1)} %fusion.33), channel_id=1, source_target_pairs={{0,64},{32,96},{64,0},{96,32},{1,65},{33,97},{65,1},{97,33},{2,66}... | collective-permute-start | bytes 98312 | tf_op jit(solution)/shard_map/ppermute | solution.py:47
  63.9 2.9 %collective-permute-done.22 = bf16[1024,256]{1,0:T(8,128)(2,1)S(1)} collective-permute-done((bf16[1024,256]{1,0:T(8,128)(2,1)S(1)}, bf16[1024,256]{1,0:T(8,128)(2,1)S(1)}, u32[]{:S(2)}, u32[]{:S(2)}) %collective-permute-start.22) | collective-permute-done | bytes 524320 | tf_op jit(solution)/shard_map/ppermute | solution.py:43
  66.8 2.6 %collective-permute-done.23 = bf16[1024,256]{1,0:T(8,128)(2,1)S(1)} collective-permute-done((bf16[1024,256]{1,0:T(8,128)(2,1)S(1)}, bf16[1024,256]{1,0:T(8,128)(2,1)S(1)}, u32[]{:S(2)}, u32[]{:S(2)}) %collective-permute-start.23) | collective-permute-done | bytes 524320 | tf_op jit(solution)/shard_map/ppermute | solution.py:43
  69.3 5.5 %collective-permute-done.24 = bf16[1024,256]{1,0:T(8,128)(2,1)S(1)} collective-permute-done((bf16[1024,256]{1,0:T(8,128)(2,1)S(1)}, bf16[1024,256]{1,0:T(8,128)(2,1)S(1)}, u32[]{:S(2)}, u32[]{:S(2)}) %collective-permute-start.24) | collective-permute-done | bytes 524320 | tf_op jit(solution)/shard_map/ppermute | solution.py:43
  75.9 3.2 %weight_grads.1 = bf16[8,256,512]{2,1,0:T(8,128)(2,1)} custom-call(bf16[16,256,256]{2,1,0:T(8,128)(2,1)S(1)} %sort_blocks.2.t_own, bf16[8,256,256]{2,1,0:T(8,128)(2,1)S(1)} %collective-permute-done.16.t_other, bf16[16,256,256]{2,1,0:T(8,128)(2,1)S(1)} %sort_blocks.3.g_own, bf16[8,256,256]{2,1,0:T(8,128)(2,1)S(1)} %collective-permute-done.17.g_other, ...), custom_call_target="tpu_custom_call" | custom-call | flops 1073741824 | bytes 6291456 | tf_op jit(solution)/shard_map/weight_grads/pallas_call | solution.py:146
  80.8 1.3 %part_terms.13 = bf16[1024,256]{1,0:T(8,128)(2,1)} custom-call(bf16[4096,384]{1,0:T(8,128)(2,1)S(1)} %get-tuple-element.41.w, bf16[256,512]{1,0:T(8,128)(2,1)S(1)} %pad_maximum_fusion.2.d_own.cotangent), custom_call_target="tpu_custom_call" | custom-call | flops 201326592 | bytes 1310720 | tf_op jit(solution)/shard_map/part_terms/pallas_call | solution.py:173
  84.7 3.9 %all-to-all-start = ((bf16[4,512,512]{2,1,0:T(8,128)(2,1)}), bf16[4,512,512]{2,1,0:T(8,128)(2,1)S(1)}, u32[]{:S(2)}, u32[]{:S(2)}) async-start(bf16[4,512,512]{2,1,0:T(8,128)(2,1)} %bitcast.3), calls=%async_computation | async-start | bytes 4194304 | tf_op jit(solution)/shard_map/all_to_all | solution.py:192
  89.7 1.9 %collective-permute-done.26 = bf16[1024,256]{1,0:T(8,128)(2,1)} collective-permute-done((bf16[1024,256]{1,0:T(8,128)(2,1)}, bf16[1024,256]{1,0:T(8,128)(2,1)}, u32[]{:S(2)}, u32[]{:S(2)}) %collective-permute-start.26) | collective-permute-done | bytes 524320 | tf_op jit(solution)/shard_map/ppermute | solution.py:43
  91.6 2.2 %collective-permute-done.27 = bf16[1024,256]{1,0:T(8,128)(2,1)} collective-permute-done((bf16[1024,256]{1,0:T(8,128)(2,1)}, bf16[1024,256]{1,0:T(8,128)(2,1)}, u32[]{:S(2)}, u32[]{:S(2)}) %collective-permute-start.27) | collective-permute-done | bytes 524320 | tf_op jit(solution)/shard_map/ppermute | solution.py:43
  93.8 5.5 %collective-permute-done.28 = bf16[1024,256]{1,0:T(8,128)(2,1)} collective-permute-done((bf16[1024,256]{1,0:T(8,128)(2,1)S(1)}, bf16[1024,256]{1,0:T(8,128)(2,1)}, u32[]{:S(2)}, u32[]{:S(2)}) %collective-permute-start.28) | collective-permute-done | bytes 524320 | tf_op jit(solution)/shard_map/ppermute | solution.py:43
  99.3 1.6 %add_convert_fusion = bf16[1024,256]{1,0:T(8,128)(2,1)S(1)} fusion(bf16[1024,256]{1,0:T(8,128)(2,1)} %collective-permute-done.28, bf16[1024,256]{1,0:T(8,128)(2,1)} %collective-permute-done.27, bf16[1024,256]{1,0:T(8,128)(2,1)} %collective-permute-done.26, bf16[1024,256]{1,0:T(8,128)(2,1)S(1)} %part_terms.12), kind=kLoop, calls=%fused_computation.20 | loop fusion | flops 2097152 | bytes 2621440 | tf_op jit(solution)/shard_map/convert_element_type | solution.py:343
  101.0 1.3 %collective-permute-start.29 = (bf16[2,256,256]{2,1,0:T(8,128)(2,1)S(1)}, bf16[2,256,256]{2,1,0:T(8,128)(2,1)S(1)}, u32[]{:S(2)}, u32[]{:S(2)}) collective-permute-start(bf16[2,256,256]{2,1,0:T(8,128)(2,1)S(1)} %pad_maximum_fusion.4), channel_id=1, source_target_pairs={{0,12},{1,13},{2,14},{3,15},{4,0},{5,1},{6,2},{7,3},{8,4},{9,5},{1... | collective-permute-start | bytes 786440 | tf_op jit(solution)/shard_map/ppermute | solution.py:43
  103.5 1.5 %collective-permute-start.31 = (bf16[2,256,256]{2,1,0:T(8,128)(2,1)S(1)}, bf16[2,256,256]{2,1,0:T(8,128)(2,1)}, u32[]{:S(2)}, u32[]{:S(2)}) collective-permute-start(bf16[2,256,256]{2,1,0:T(8,128)(2,1)S(1)} %pad_maximum_fusion.6), channel_id=1, source_target_pairs={{0,4},{1,5},{2,6},{3,7},{4,8},{5,9},{6,10},{7,11},{8,12},{9,13},{1... | collective-permute-start | bytes 786440 | tf_op jit(solution)/shard_map/ppermute | solution.py:43
  105.7 9.0 %all-to-all-done.got = bf16[4,512,512]{2,1,0:T(8,128)(2,1)S(1)} async-done(((bf16[4,512,512]{2,1,0:T(8,128)(2,1)}), bf16[4,512,512]{2,1,0:T(8,128)(2,1)S(1)}, u32[]{:S(2)}, u32[]{:S(2)}) %all-to-all-start) | async-done | bytes 2097184 | tf_op jit(solution)/shard_map/all_to_all | solution.py:192
  (112 shorter events, 39.6 us)
Async XLA Ops:
  1.8 9.8 %collective-permute-start.2 = (bf16[256,256]{1,0:T(8,128)(2,1)S(1)}, bf16[256,256]{1,0:T(8,128)(2,1)S(1)}, u32[]{:S(2)}, u32[]{:S(2)}) collective-permute-start(bf16[256,256]{1,0:T(8,128)(2,1)S(1)} %bitcast.51), channel_id=1, source_target_pairs={{0,12},{1,13},{2,14},{3,15},{4,0},{5,1},{6,2},{7,3},{8,4},{9,5},{1... | collective-permute-start | bytes 393224 | tf_op jit(solution)/shard_map/ppermute | solution.py:43
  5.6 7.2 %collective-permute-start = (bf16[256,256]{1,0:T(8,128)(2,1)S(1)}, bf16[256,256]{1,0:T(8,128)(2,1)S(1)}, u32[]{:S(2)}, u32[]{:S(2)}) collective-permute-start(bf16[256,256]{1,0:T(8,128)(2,1)S(1)} %bitcast.53), channel_id=1, source_target_pairs={{0,4},{1,5},{2,6},{3,7},{4,8},{5,9},{6,10},{7,11},{8,12},{9,13},{1... | collective-permute-start | bytes 393224 | tf_op jit(solution)/shard_map/ppermute | solution.py:43
  7.6 9.6 %collective-permute-start.12 = (bf16[256,256]{1,0:T(8,128)(2,1)S(1)}, bf16[256,256]{1,0:T(8,128)(2,1)S(1)}, u32[]{:S(2)}, u32[]{:S(2)}) collective-permute-start(bf16[256,256]{1,0:T(8,128)(2,1)S(1)} %bitcast.47), channel_id=1, source_target_pairs={{0,12},{1,13},{2,14},{3,15},{4,0},{5,1},{6,2},{7,3},{8,4},{9,5},{1... | collective-permute-start | bytes 393224 | tf_op jit(solution)/shard_map/ppermute | solution.py:43
  9.9 8.5 %collective-permute-start.11 = (bf16[256,256]{1,0:T(8,128)(2,1)S(1)}, bf16[256,256]{1,0:T(8,128)(2,1)S(1)}, u32[]{:S(2)}, u32[]{:S(2)}) collective-permute-start(bf16[256,256]{1,0:T(8,128)(2,1)S(1)} %bitcast.48), channel_id=1, source_target_pairs={{0,8},{1,9},{2,10},{3,11},{4,12},{5,13},{6,14},{7,15},{8,0},{9,1},... | collective-permute-start | bytes 393224 | tf_op jit(solution)/shard_map/ppermute | solution.py:43
  11.6 6.8 %collective-permute-start.10 = (bf16[256,256]{1,0:T(8,128)(2,1)S(1)}, bf16[256,256]{1,0:T(8,128)(2,1)}, u32[]{:S(2)}, u32[]{:S(2)}) collective-permute-start(bf16[256,256]{1,0:T(8,128)(2,1)S(1)} %bitcast.49), channel_id=1, source_target_pairs={{0,4},{1,5},{2,6},{3,7},{4,8},{5,9},{6,10},{7,11},{8,12},{9,13},{1... | collective-permute-start | bytes 393224 | tf_op jit(solution)/shard_map/ppermute | solution.py:43
  12.9 20.8 %collective-permute-start.5 = (bf16[1024,256]{1,0:T(8,128)(2,1)S(1)}, bf16[1024,256]{1,0:T(8,128)(2,1)S(1)}, u32[]{:S(2)}, u32[]{:S(2)}) collective-permute-start(bf16[1024,256]{1,0:T(8,128)(2,1)S(1)} %pad_maximum_fusion.a0), channel_id=1, source_target_pairs={{0,3},{1,0},{2,1},{3,2},{4,7},{5,4},{6,5},{7,6},{8,11},{9,8},{10,9... | collective-permute-start | bytes 1572872 | tf_op jit(solution)/shard_map/ppermute | solution.py:43
  17.1 19.0 %collective-permute-start.4 = (bf16[1024,256]{1,0:T(8,128)(2,1)S(1)}, bf16[1024,256]{1,0:T(8,128)(2,1)S(1)}, u32[]{:S(2)}, u32[]{:S(2)}) collective-permute-start(bf16[1024,256]{1,0:T(8,128)(2,1)S(1)} %pad_maximum_fusion.a0), channel_id=1, source_target_pairs={{0,2},{1,3},{2,0},{3,1},{4,6},{5,7},{6,4},{7,5},{8,10},{9,11},{10,... | collective-permute-start | bytes 1572872 | tf_op jit(solution)/shard_map/ppermute | solution.py:43
  17.2 18.4 %collective-permute-start.3 = (bf16[1024,256]{1,0:T(8,128)(2,1)S(1)}, bf16[1024,256]{1,0:T(8,128)(2,1)S(1)}, u32[]{:S(2)}, u32[]{:S(2)}) collective-permute-start(bf16[1024,256]{1,0:T(8,128)(2,1)S(1)} %pad_maximum_fusion.a0), channel_id=1, source_target_pairs={{0,1},{1,2},{2,3},{3,0},{4,5},{5,6},{6,7},{7,4},{8,9},{9,10},{10,1... | collective-permute-start | bytes 1572872 | tf_op jit(solution)/shard_map/ppermute | solution.py:43
  19.4 22.4 %collective-permute-start.15 = (bf16[1024,256]{1,0:T(8,128)(2,1)S(1)}, bf16[1024,256]{1,0:T(8,128)(2,1)S(1)}, u32[]{:S(2)}, u32[]{:S(2)}) collective-permute-start(bf16[1024,256]{1,0:T(8,128)(2,1)S(1)} %pad_maximum_fusion.1.a0), channel_id=1, source_target_pairs={{0,3},{1,0},{2,1},{3,2},{4,7},{5,4},{6,5},{7,6},{8,11},{9,8},{10,9... | collective-permute-start | bytes 1572872 | tf_op jit(solution)/shard_map/ppermute | solution.py:43
  29.3 12.5 %collective-permute-start.14 = (bf16[1024,256]{1,0:T(8,128)(2,1)S(1)}, bf16[1024,256]{1,0:T(8,128)(2,1)S(1)}, u32[]{:S(2)}, u32[]{:S(2)}) collective-permute-start(bf16[1024,256]{1,0:T(8,128)(2,1)S(1)} %pad_maximum_fusion.1.a0), channel_id=1, source_target_pairs={{0,2},{1,3},{2,0},{3,1},{4,6},{5,7},{6,4},{7,5},{8,10},{9,11},{10,... | collective-permute-start | bytes 1572872 | tf_op jit(solution)/shard_map/ppermute | solution.py:43
  33.7 11.8 %collective-permute-start.13 = (bf16[1024,256]{1,0:T(8,128)(2,1)S(1)}, bf16[1024,256]{1,0:T(8,128)(2,1)S(1)}, u32[]{:S(2)}, u32[]{:S(2)}) collective-permute-start(bf16[1024,256]{1,0:T(8,128)(2,1)S(1)} %pad_maximum_fusion.1.a0), channel_id=1, source_target_pairs={{0,1},{1,2},{2,3},{3,0},{4,5},{5,6},{6,7},{7,4},{8,9},{9,10},{10,1... | collective-permute-start | bytes 1572872 | tf_op jit(solution)/shard_map/ppermute | solution.py:43
  38.1 8.2 %collective-permute-start.8 = (bf16[128,128]{1,0:T(8,128)(2,1)S(1)}, bf16[128,128]{1,0:T(8,128)(2,1)S(1)}, u32[]{:S(2)}, u32[]{:S(2)}) collective-permute-start(bf16[128,128]{1,0:T(8,128)(2,1)S(1)} %fusion.28), channel_id=1, source_target_pairs={{0,64},{32,96},{64,0},{96,32},{1,65},{33,97},{65,1},{97,33},{2,66}... | collective-permute-start | bytes 98312 | tf_op jit(solution)/shard_map/ppermute | solution.py:47
  53.3 7.1 %collective-permute-start.20 = (bf16[128,128]{1,0:T(8,128)(2,1)S(1)}, bf16[128,128]{1,0:T(8,128)(2,1)S(1)}, u32[]{:S(2)}, u32[]{:S(2)}) collective-permute-start(bf16[128,128]{1,0:T(8,128)(2,1)S(1)} %fusion.33), channel_id=1, source_target_pairs={{0,64},{32,96},{64,0},{96,32},{1,65},{33,97},{65,1},{97,33},{2,66}... | collective-permute-start | bytes 98312 | tf_op jit(solution)/shard_map/ppermute | solution.py:47
  57.5 9.3 %collective-permute-start.22 = (bf16[1024,256]{1,0:T(8,128)(2,1)S(1)}, bf16[1024,256]{1,0:T(8,128)(2,1)S(1)}, u32[]{:S(2)}, u32[]{:S(2)}) collective-permute-start(bf16[1024,256]{1,0:T(8,128)(2,1)S(1)} %part_terms.9), channel_id=1, source_target_pairs={{0,3},{1,0},{2,1},{3,2},{4,7},{5,4},{6,5},{7,6},{8,11},{9,8},{10,9... | collective-permute-start | bytes 1572872 | tf_op jit(solution)/shard_map/ppermute | solution.py:43
  58.4 10.9 %collective-permute-start.23 = (bf16[1024,256]{1,0:T(8,128)(2,1)S(1)}, bf16[1024,256]{1,0:T(8,128)(2,1)S(1)}, u32[]{:S(2)}, u32[]{:S(2)}) collective-permute-start(bf16[1024,256]{1,0:T(8,128)(2,1)S(1)} %part_terms.10), channel_id=1, source_target_pairs={{0,2},{1,3},{2,0},{3,1},{4,6},{5,7},{6,4},{7,5},{8,10},{9,11},{10,... | collective-permute-start | bytes 1572872 | tf_op jit(solution)/shard_map/ppermute | solution.py:43
  59.5 15.3 %collective-permute-start.24 = (bf16[1024,256]{1,0:T(8,128)(2,1)S(1)}, bf16[1024,256]{1,0:T(8,128)(2,1)S(1)}, u32[]{:S(2)}, u32[]{:S(2)}) collective-permute-start(bf16[1024,256]{1,0:T(8,128)(2,1)S(1)} %part_terms.11), channel_id=1, source_target_pairs={{0,1},{1,2},{2,3},{3,0},{4,5},{5,6},{6,7},{7,4},{8,9},{9,10},{10,1... | collective-permute-start | bytes 1572872 | tf_op jit(solution)/shard_map/ppermute | solution.py:43
  63.7 12.2 %collective-permute-start.25 = (bf16[256,512]{1,0:T(8,128)(2,1)S(1)}, bf16[256,512]{1,0:T(8,128)(2,1)S(1)}, u32[]{:S(2)}, u32[]{:S(2)}) collective-permute-start(bf16[256,512]{1,0:T(8,128)(2,1)S(1)} %pad_maximum_fusion.2.d_own.cotangent), channel_id=1, source_target_pairs={{0,16},{16,0},{1,17},{17,1},{2,18},{18,2},{3,19},{19,3},{4,20},{20... | collective-permute-start | bytes 786440 | tf_op jit(solution)/shard_map/ppermute | solution.py:59
  82.1 9.5 %collective-permute-start.26 = (bf16[1024,256]{1,0:T(8,128)(2,1)}, bf16[1024,256]{1,0:T(8,128)(2,1)}, u32[]{:S(2)}, u32[]{:S(2)}) collective-permute-start(bf16[1024,256]{1,0:T(8,128)(2,1)} %part_terms.13), channel_id=1, source_target_pairs={{0,3},{1,0},{2,1},{3,2},{4,7},{5,4},{6,5},{7,6},{8,11},{9,8},{10,9... | collective-permute-start | bytes 1572872 | tf_op jit(solution)/shard_map/ppermute | solution.py:43
  82.7 11.1 %collective-permute-start.27 = (bf16[1024,256]{1,0:T(8,128)(2,1)}, bf16[1024,256]{1,0:T(8,128)(2,1)}, u32[]{:S(2)}, u32[]{:S(2)}) collective-permute-start(bf16[1024,256]{1,0:T(8,128)(2,1)} %part_terms.14), channel_id=1, source_target_pairs={{0,2},{1,3},{2,0},{3,1},{4,6},{5,7},{6,4},{7,5},{8,10},{9,11},{10,... | collective-permute-start | bytes 1572872 | tf_op jit(solution)/shard_map/ppermute | solution.py:43
  83.4 16.0 %collective-permute-start.28 = (bf16[1024,256]{1,0:T(8,128)(2,1)S(1)}, bf16[1024,256]{1,0:T(8,128)(2,1)}, u32[]{:S(2)}, u32[]{:S(2)}) collective-permute-start(bf16[1024,256]{1,0:T(8,128)(2,1)S(1)} %part_terms.15), channel_id=1, source_target_pairs={{0,1},{1,2},{2,3},{3,0},{4,5},{5,6},{6,7},{7,4},{8,9},{9,10},{10,1... | collective-permute-start | bytes 1572872 | tf_op jit(solution)/shard_map/ppermute | solution.py:43
  84.7 30.0 %all-to-all-start = ((bf16[4,512,512]{2,1,0:T(8,128)(2,1)}), bf16[4,512,512]{2,1,0:T(8,128)(2,1)S(1)}, u32[]{:S(2)}, u32[]{:S(2)}) async-start(bf16[4,512,512]{2,1,0:T(8,128)(2,1)} %bitcast.3), calls=%async_computation | async-start | bytes 4194304 | tf_op jit(solution)/shard_map/all_to_all | solution.py:192
  101.0 14.8 %collective-permute-start.29 = (bf16[2,256,256]{2,1,0:T(8,128)(2,1)S(1)}, bf16[2,256,256]{2,1,0:T(8,128)(2,1)S(1)}, u32[]{:S(2)}, u32[]{:S(2)}) collective-permute-start(bf16[2,256,256]{2,1,0:T(8,128)(2,1)S(1)} %pad_maximum_fusion.4), channel_id=1, source_target_pairs={{0,12},{1,13},{2,14},{3,15},{4,0},{5,1},{6,2},{7,3},{8,4},{9,5},{1... | collective-permute-start | bytes 786440 | tf_op jit(solution)/shard_map/ppermute | solution.py:43
  102.3 13.5 %collective-permute-start.30 = (bf16[2,256,256]{2,1,0:T(8,128)(2,1)S(1)}, bf16[2,256,256]{2,1,0:T(8,128)(2,1)}, u32[]{:S(2)}, u32[]{:S(2)}) collective-permute-start(bf16[2,256,256]{2,1,0:T(8,128)(2,1)S(1)} %pad_maximum_fusion.5), channel_id=1, source_target_pairs={{0,8},{1,9},{2,10},{3,11},{4,12},{5,13},{6,14},{7,15},{8,0},{9,1},... | collective-permute-start | bytes 786440 | tf_op jit(solution)/shard_map/ppermute | solution.py:43
  103.5 12.3 %collective-permute-start.31 = (bf16[2,256,256]{2,1,0:T(8,128)(2,1)S(1)}, bf16[2,256,256]{2,1,0:T(8,128)(2,1)}, u32[]{:S(2)}, u32[]{:S(2)}) collective-permute-start(bf16[2,256,256]{2,1,0:T(8,128)(2,1)S(1)} %pad_maximum_fusion.6), channel_id=1, source_target_pairs={{0,4},{1,5},{2,6},{3,7},{4,8},{5,9},{6,10},{7,11},{8,12},{9,13},{1... | collective-permute-start | bytes 786440 | tf_op jit(solution)/shard_map/ppermute | solution.py:43
  (14 other events, 89.6 us)

commit v4 on v3

--- a/solution.py
+++ b/solution.py
@@ -55,18 +55,25 @@
     return lax.ppermute(a, SEQ, pairs)
 
 
+def x_partner(a, bits):
+    pairs = [(2 * i + c, 2 * (i ^ bits[c]) + c) for i in range(SIDE) for c in range(2)]
+    return lax.ppermute(a, SEQ, pairs)
+
+
 def core_swap(a):
     return lax.ppermute(a, "core", [(0, 1), (1, 0)])
 
 
 def block_tables():
-    core, y, z = (lax.axis_index(n) for n in PLANE)
+    x, core, y, z = (lax.axis_index(n) for n in ("x",) + PLANE)
     at = jnp.arange(SIDE * SIDE, dtype=jnp.int32)
     d2, d1 = at // SIDE, at % SIDE
     from_y = (y - jnp.where(core == 0, d1, d2)) % SIDE
     from_z = (z - jnp.where(core == 0, d2, d1)) % SIDE
     other_core = (from_z // 2 + core) % 2
-    slots = other_core * 8 + from_y * 2 + from_z % 2
+    away = x ^ from_y
+    place = jnp.where(away % 2 == 0, away // 2, 2 + ((away // 2) ^ (from_z // 2)))
+    slots = other_core * 8 + place * 2 + from_z % 2
     return from_y * SIDE + from_z, slots
 
 
@@ -128,14 +135,18 @@
     )(slots, *parts)
 
 
-def weight_grads_kernel(t_own, t_other, g_own, g_other, d_own, d_other, out):
+def weight_grads_kernel(t_own, t_other, g_own, g_other, d_own, d_other, keep, send):
     n = d_own.shape[1]
+    half = keep.shape[0]
     split = n - n // SIDE
     for s in range(t_own.shape[0]):
         for own, other, at in ((t_own, t_other, slice(0, split)), (g_own, g_other, slice(split, n))):
             term = jnp.dot(own[s], d_own[:, at], preferred_element_type=WIDE)
             term = term + jnp.dot(other[s], d_other[:, at], preferred_element_type=WIDE)
-            out[s, :, at] = term.astype(HALF)
+            if s < half:
+                keep[s, :, at] = term.astype(HALF)
+            else:
+                send[s - half, :, at] = term.astype(HALF)
 
 
 def weight_grads(t_sorted, t_other, g_sorted, g_other, d_own, d_other):
@@ -145,10 +156,10 @@
     flat = pl.BlockSpec((tokens, n), lambda i: (0, 0))
     return pl.pallas_call(
         weight_grads_kernel,
-        out_shape=jax.ShapeDtypeStruct((half, step, n), HALF),
+        out_shape=[jax.ShapeDtypeStruct((half // 2, step, n), HALF)] * 2,
         grid=(1,),
         in_specs=[first] * 4 + [flat] * 2,
-        out_specs=pl.BlockSpec((half, step, n), lambda i: (0, 0, 0)),
+        out_specs=[pl.BlockSpec((half // 2, step, n), lambda i: (0, 0, 0))] * 2,
         compiler_params=pltpu.CompilerParams(vmem_limit_bytes=14 << 20),
         cost_estimate=pl.CostEstimate(
             flops=4 * half * step * tokens * n,
@@ -187,23 +198,16 @@
     )(weights, cotangent)
 
 
-def x_spread(blocks):
-    _, step, n = blocks.shape
-    return lax.all_to_all(blocks.reshape(SIDE, 2 * step, n), "x", 0, 0, tiled=True)
-
-
-def split_sum_kernel(got, q, k, v, o):
+def split_sum_kernel(mine, got, q, k, v, o):
     n = q.shape[1]
     for i, out in enumerate((q, k, v, o)):
         at = slice(i * n, (i + 1) * n)
-        acc = got[0, :, at].astype(WIDE)
-        for d in range(1, SIDE):
-            acc = acc + got[d, :, at].astype(WIDE)
+        acc = mine[:, at].astype(WIDE) + got[:, at].astype(WIDE)
         out[...] = acc if out is not o else acc.T
 
 
-def split_sum(got):
-    _, rows, width = got.shape
+def split_sum(mine, got):
+    rows, width = got.shape
     n = width // SIDE
     flat = pl.BlockSpec((rows, n), lambda i: (0, 0))
     tall = jax.ShapeDtypeStruct((rows, n), WIDE)
@@ -211,14 +215,14 @@
         split_sum_kernel,
         out_shape=(tall, tall, tall, jax.ShapeDtypeStruct((n, rows), WIDE)),
         grid=(1,),
-        in_specs=[pl.BlockSpec(got.shape, lambda i: (0, 0, 0))],
+        in_specs=[pl.BlockSpec((rows, width), lambda i: (0, 0))] * 2,
         out_specs=(flat, flat, flat, pl.BlockSpec((n, rows), lambda i: (0, 0))),
-        compiler_params=pltpu.CompilerParams(vmem_limit_bytes=7 << 20),
-        cost_estimate=pl.CostEstimate(
-            flops=SIDE * rows * width, bytes_accessed=12 * rows * width, transcendentals=0
+        compiler_params=pltpu.CompilerParams(vmem_limit_bytes=5 << 20),
+        cost_estimate=pl.CostEstimate(
+            flops=rows * width, bytes_accessed=8 * rows * width, transcendentals=0
         ),
         name="split_sum",
-    )(got)
+    )(mine, got)
 
 
 def spread_phase1(a):
@@ -266,6 +270,25 @@
     return acc
 
 
+def rounded_sum(a, b):
+    return (a.astype(WIDE) + b.astype(WIDE)).astype(HALF)
+
+
+def seq_exchange(own, earlier):
+    x, core = lax.axis_index("x"), lax.axis_index("core")
+    other = core_swap(own)
+    pair = rounded_sum(own, other)
+    near = x_partner(pair, (1, 1))
+    four = rounded_sum(pair, near)
+    far = x_partner(four, (2, 2))
+    ahead = [core == 1, x % 2 == 1, x >= 2]
+    acc = jnp.zeros(own.shape, WIDE)
+    for part, before in zip((other, near, far), ahead):
+        keep = before if earlier else jnp.logical_not(before)
+        acc = acc + jnp.where(keep, part.astype(WIDE), 0.0)
+    return acc, (four, far), other
+
+
 def on_device(tokens, w_query, w_key, w_value, w_out, grad_out, state_in):
     x, core = lax.axis_index("x"), lax.axis_index("core")
     dh = w_query.shape[1]
@@ -310,39 +333,34 @@
     own_back = mm(query, grad_mixed, TN).astype(HALF)
     half = SIDE * SIDE // 2
     t_sorted, g_sorted = sort_blocks(slots, t_parts), sort_blocks(slots, g_parts)
-    t_other, g_other = (core_swap(after(prior, a[half:])) for a in (t_sorted, g_sorted))
-    own_back = after((t_other, g_other), own_back)
-    other_back = core_swap(own_back)
-    back_pairs = pair_sums(own_back, other_back)
+    own_back = after(out_terms, own_back)
+    behind, halves, _ = seq_exchange(own_back, False)
+    t_other, g_other = (core_swap(after(halves[0], a[half:])) for a in (t_sorted, g_sorted))
 
     grad_scores = jnp.where(allowed, mm(grad_mixed, values, NT), 0.0).astype(HALF)
     grad_query = (mm(grad_scores, keys, NN) + mm(grad_mixed, prior, NT)).astype(HALF)
-    later = masked_sum(
-        jnp.zeros((dh, dh), WIDE),
-        [other_back] + back_pairs[1:],
-        [core == 0] + [x < d for d in range(1, SIDE)],
-    ).astype(HALF)
-    grad_state = jnp.zeros((dh, dh), WIDE)
-    for chip in range(SIDE):
-        part = jnp.zeros((dh, dh), HALF)
-        for d, p in enumerate(back_pairs):
-            part = jnp.where((x - d) % SIDE == chip, p, part)
-        grad_state = grad_state + part.astype(WIDE)
-
+    later = behind.astype(HALF)
+    grad_state = total(halves)
     grad_keys = (mm(grad_scores, query, TN) + mm(values, later, NT)).astype(HALF)
     grad_values = (mm(scores, grad_mixed, TN) + mm(keys, later, NN)).astype(HALF)
+    out_sum = total(out_got).astype(HALF)
     cotangents = jnp.concatenate([grad_query, grad_keys, grad_values, normed], axis=1)
-    blocks = weight_grads(
+    cotangents, out_sum = lax.optimization_barrier((cotangents, out_sum))
+    keep, send = weight_grads(
         t_sorted, t_other, g_sorted, g_other, cotangents, core_swap(cotangents)
     )
-    out_sum = total(out_got).astype(HALF)
-    cotangents, out_sum, blocks = lax.optimization_barrier((cotangents, out_sum, blocks))
+    sent = x_partner(send, (1, 3))
     in_terms = [part_terms(w_qkv, d, cotangents) for d in range(SIDE)]
     in_got = fold_phase1(in_terms)
-    grads = split_sum(x_spread(after(in_terms, blocks)))
+    mine = (keep.astype(WIDE) + sent.astype(WIDE)).astype(HALF)
+    mine = mine.reshape(2, -1, mine.shape[2])
+    own, send = mine[0], mine[1]
+    in_got = after((own, send), in_got)
+    grads = split_sum(own, x_partner(send, (2, 2)))
     got = fold_phase2((out_sum, total(in_got).astype(HALF)))
-    sums = total(after(grads, got))
-    result, grad_tokens = sums[0].astype(HALF), sums[1]
+    got = after(grads, got)
+    result = total([g[0] for g in got]).astype(HALF)
+    grad_tokens = total([g[1] for g in got])
     return (
         result,
         grad_tokens,

time: 119 us -> 106 us (0.89)
  waiting for transfers between devices: 40.2 us -> 35.6 us
  Pallas kernels: 11.6 us -> 8.59 us
  local copies, waits for them, and re-layouts: 7.31 us -> 4.9 us
  other arithmetic: 5.92 us -> 3.79 us
    ppermute x0 -> x4, waiting for transfers between devices: none -> 23.8 us  [x_partner(): return lax.ppermute(a, SEQ, pairs)]
    ppermute x21, waiting for transfers between devices: 25.6 us -> 8.9 us  [plane_shift(): return lax.ppermute(a, PLANE, plane_pairs(phase, shift))]
    all_to_all x1 -> x0, waiting for transfers between devices: 9.02 us -> none  [x_spread(): lax.all_to_all(blocks.reshape(SIDE, 2 * step, n), 'x', 0, 0, tiled=True)]
    ppermute x0 -> x4, starting transfers between devices: none -> 4.73 us  [x_partner(): return lax.ppermute(a, SEQ, pairs)]
    all_to_all x1 -> x0, starting transfers between devices: 3.91 us -> none  [x_spread(): lax.all_to_all(blocks.reshape(SIDE, 2 * step, n), 'x', 0, 0, tiled=True)]
    ppermute x2 -> x1, starting transfers between devices: 6.2 us -> 3.1 us  [x_shift(): return lax.ppermute(a, 'x', [(i, (i + shift) % SIDE) for i in range(SIDE)])]
    ppermute x21, starting transfers between devices: 34.1 us -> 37.1 us  [plane_shift(): return lax.ppermute(a, PLANE, plane_pairs(phase, shift))]
    pallas_call x8, Pallas kernels: 4.7 us -> 3.08 us  [part_terms(): pl.pallas_call(part_terms_kernel, out_shape=jax.ShapeDtypeStruct((SIDE *...]
  transfers between devices with their start and end apart: 33 -> 33, of which waited for: 16 -> 12; matrix products, arithmetic and copies ran while one was open for 10% -> 8% of each run, Pallas kernels for 5% -> 5%
where the time goes in v4:
time: 106 us; the launch traced here: 105 us
  starting transfers between devices  45.8 us (43%)
  waiting for transfers between devices  35.6 us (34%)
  Pallas kernels  8.59 us (8%)
  matrix products  5.51 us (5%)
  local copies, waits for them, and re-layouts  4.9 us (5%)
  other arithmetic  3.79 us (4%)
  between operations  1.16 us (1%)
    ppermute x21, starting transfers between devices, plane_shift(): return lax.ppermute(a, PLANE, plane_pairs(phase, shift))  37.1 us
    ppermute x4, waiting for transfers between devices, x_partner(): return lax.ppermute(a, SEQ, pairs)  23.8 us
    ppermute x21, waiting for transfers between devices, plane_shift(): return lax.ppermute(a, PLANE, plane_pairs(phase, shift))  8.9 us
    dot_general x20, matrix products, mm(): return lax.dot_general(a, b, dims, preferred_element_type=WIDE)  5.51 us
    ppermute x4, starting transfers between devices, x_partner(): return lax.ppermute(a, SEQ, pairs)  4.73 us
    unnamed x12, local copies, waits for them, and re-layouts  4.61 us
    ppermute x1, starting transfers between devices, x_shift(): return lax.ppermute(a, 'x', [(i, (i + shift) % SIDE) for i in range(SIDE)])  3.1 us
    pallas_call x8, Pallas kernels, part_terms(): pl.pallas_call(part_terms_kernel, out_shape=jax.ShapeDtypeStruct((SIDE *...  3.08 us
  transfers between devices with their start and end apart: 33, of which 12 were waited for; matrix products, arithmetic and copies ran while one was open for 8% of the time, Pallas kernels for 5%

profile of v4, /device:TPU:0, one launch (start us, length us, event | category | flops | bytes accessed | tf_op | source)
XLA Modules:
  0.0 105.4 jit_solution(7366441508130689981)
XLA Ops:
  1.8 3.2 %collective-permute-start.2 = (bf16[256,256]{1,0:T(8,128)(2,1)S(1)}, bf16[256,256]{1,0:T(8,128)(2,1)S(1)}, u32[]{:S(2)}, u32[]{:S(2)}) collective-permute-start(bf16[256,256]{1,0:T(8,128)(2,1)S(1)} %bitcast.54), channel_id=1, source_target_pairs={{0,12},{1,13},{2,14},{3,15},{4,0},{5,1},{6,2},{7,3},{8,4},{9,5},{1... | collective-permute-start | bytes 393224 | tf_op jit(solution)/shard_map/ppermute | solution.py:43
  7.6 2.3 %collective-permute-start.12 = (bf16[256,256]{1,0:T(8,128)(2,1)S(1)}, bf16[256,256]{1,0:T(8,128)(2,1)S(1)}, u32[]{:S(2)}, u32[]{:S(2)}) collective-permute-start(bf16[256,256]{1,0:T(8,128)(2,1)S(1)} %bitcast.50), channel_id=1, source_target_pairs={{0,12},{1,13},{2,14},{3,15},{4,0},{5,1},{6,2},{7,3},{8,4},{9,5},{1... | collective-permute-start | bytes 393224 | tf_op jit(solution)/shard_map/ppermute | solution.py:43
  9.9 1.7 %collective-permute-start.11 = (bf16[256,256]{1,0:T(8,128)(2,1)S(1)}, bf16[256,256]{1,0:T(8,128)(2,1)S(1)}, u32[]{:S(2)}, u32[]{:S(2)}) collective-permute-start(bf16[256,256]{1,0:T(8,128)(2,1)S(1)} %bitcast.51), channel_id=1, source_target_pairs={{0,8},{1,9},{2,10},{3,11},{4,12},{5,13},{6,14},{7,15},{8,0},{9,1},... | collective-permute-start | bytes 393224 | tf_op jit(solution)/shard_map/ppermute | solution.py:43
  12.9 4.1 %collective-permute-start.5 = (bf16[1024,256]{1,0:T(8,128)(2,1)S(1)}, bf16[1024,256]{1,0:T(8,128)(2,1)S(1)}, u32[]{:S(2)}, u32[]{:S(2)}) collective-permute-start(bf16[1024,256]{1,0:T(8,128)(2,1)S(1)} %pad_maximum_fusion.a0), channel_id=1, source_target_pairs={{0,3},{1,0},{2,1},{3,2},{4,7},{5,4},{6,5},{7,6},{8,11},{9,8},{10,9... | collective-permute-start | bytes 1572872 | tf_op jit(solution)/shard_map/ppermute | solution.py:43
  17.2 1.2 %collective-permute-start.3 = (bf16[1024,256]{1,0:T(8,128)(2,1)S(1)}, bf16[1024,256]{1,0:T(8,128)(2,1)S(1)}, u32[]{:S(2)}, u32[]{:S(2)}) collective-permute-start(bf16[1024,256]{1,0:T(8,128)(2,1)S(1)} %pad_maximum_fusion.a0), channel_id=1, source_target_pairs={{0,1},{1,2},{2,3},{3,0},{4,5},{5,6},{6,7},{7,4},{8,9},{9,10},{10,1... | collective-permute-start | bytes 1572872 | tf_op jit(solution)/shard_map/ppermute | solution.py:43
  19.4 9.9 %collective-permute-start.15 = (bf16[1024,256]{1,0:T(8,128)(2,1)S(1)}, bf16[1024,256]{1,0:T(8,128)(2,1)S(1)}, u32[]{:S(2)}, u32[]{:S(2)}) collective-permute-start(bf16[1024,256]{1,0:T(8,128)(2,1)S(1)} %pad_maximum_fusion.1.a0), channel_id=1, source_target_pairs={{0,3},{1,0},{2,1},{3,2},{4,7},{5,4},{6,5},{7,6},{8,11},{9,8},{10,9... | collective-permute-start | bytes 1572872 | tf_op jit(solution)/shard_map/ppermute | solution.py:43
  31.9 1.3 %order_weights.1 = (bf16[4096,384]{1,0:T(8,128)(2,1)S(1)}, bf16[4096,128]{1,0:T(8,128)(2,1)S(1)}) custom-call(s32[16]{0:T(128)S(1)} %multiply_add_fusion.table, bf16[4096,128]{1,0:T(8,128)(2,1)S(1)} %copy-done, bf16[4096,128]{1,0:T(8,128)(2,1)S(1)} %copy-done.1, bf16[4096,128]{1,0:T(8,128)(2,1)S(1)} %copy-done.2, bf16[128,4096]{1,0:T(8,128)(2,1)S(1)} %copy-done.3), custom_call_target="tpu_custom_call" | custom-call | bytes 8388608 | tf_op jit(solution)/shard_map/order_weights/pallas_call | solution.py:95
  33.7 1.4 %collective-permute-start.13 = (bf16[1024,256]{1,0:T(8,128)(2,1)S(1)}, bf16[1024,256]{1,0:T(8,128)(2,1)S(1)}, u32[]{:S(2)}, u32[]{:S(2)}) collective-permute-start(bf16[1024,256]{1,0:T(8,128)(2,1)S(1)} %pad_maximum_fusion.1.a0), channel_id=1, source_target_pairs={{0,1},{1,2},{2,3},{3,0},{4,5},{5,6},{6,7},{7,4},{8,9},{9,10},{10,1... | collective-permute-start | bytes 1572872 | tf_op jit(solution)/shard_map/ppermute | solution.py:43
  38.0 3.1 %collective-permute-start.8 = (bf16[128,128]{1,0:T(8,128)(2,1)S(1)}, bf16[128,128]{1,0:T(8,128)(2,1)S(1)}, u32[]{:S(2)}, u32[]{:S(2)}) collective-permute-start(bf16[128,128]{1,0:T(8,128)(2,1)S(1)} %fusion.28), channel_id=1, source_target_pairs={{0,64},{32,96},{64,0},{96,32},{1,65},{33,97},{65,1},{97,33},{2,66}... | collective-permute-start | bytes 98312 | tf_op jit(solution)/shard_map/ppermute | solution.py:47
  41.8 3.8 %collective-permute-done.13.a1 = bf16[1024,256]{1,0:T(8,128)(2,1)S(1)} collective-permute-done((bf16[1024,256]{1,0:T(8,128)(2,1)S(1)}, bf16[1024,256]{1,0:T(8,128)(2,1)S(1)}, u32[]{:S(2)}, u32[]{:S(2)}) %collective-permute-start.13) | collective-permute-done | bytes 524320 | tf_op jit(solution)/shard_map/ppermute | solution.py:43
  50.3 1.9 %collective-permute-start.21 = (bf16[1024,256]{1,0:T(8,128)(2,1)S(1)}, bf16[1024,256]{1,0:T(8,128)(2,1)S(1)}, u32[]{:S(2)}, u32[]{:S(2)}) collective-permute-start(bf16[1024,256]{1,0:T(8,128)(2,1)S(1)} %part_terms.9), channel_id=1, source_target_pairs={{0,3},{1,0},{2,1},{3,2},{4,7},{5,4},{6,5},{7,6},{8,11},{9,8},{10,9... | collective-permute-start | bytes 1572872 | tf_op jit(solution)/shard_map/ppermute | solution.py:43
  52.2 2.1 %collective-permute-start.22 = (bf16[1024,256]{1,0:T(8,128)(2,1)S(1)}, bf16[1024,256]{1,0:T(8,128)(2,1)S(1)}, u32[]{:S(2)}, u32[]{:S(2)}) collective-permute-start(bf16[1024,256]{1,0:T(8,128)(2,1)S(1)} %part_terms.10), channel_id=1, source_target_pairs={{0,2},{1,3},{2,0},{3,1},{4,6},{5,7},{6,4},{7,5},{8,10},{9,11},{10,... | collective-permute-start | bytes 1572872 | tf_op jit(solution)/shard_map/ppermute | solution.py:43
  56.3 3.2 %collective-permute-done.17 = bf16[128,128]{1,0:T(8,128)(2,1)S(1)} collective-permute-done((bf16[128,128]{1,0:T(8,128)(2,1)S(1)}, bf16[128,128]{1,0:T(8,128)(2,1)S(1)}, u32[]{:S(2)}, u32[]{:S(2)}) %collective-permute-start.17) | collective-permute-done | bytes 32800 | tf_op jit(solution)/shard_map/ppermute | solution.py:60
  59.5 2.1 %collective-permute-start.20 = (bf16[128,128]{1,0:T(8,128)(2,1)S(1)}, bf16[128,128]{1,0:T(8,128)(2,1)S(1)}, u32[]{:S(2)}, u32[]{:S(2)}) collective-permute-start(bf16[128,128]{1,0:T(8,128)(2,1)S(1)} %fusion.33), channel_id=1, source_target_pairs={{0,64},{16,80},{32,96},{48,112},{64,0},{80,16},{96,32},{112,48},{1... | collective-permute-start | bytes 98312 | tf_op jit(solution)/shard_map/ppermute | solution.py:60
  62.0 3.1 %collective-permute-done.20 = bf16[128,128]{1,0:T(8,128)(2,1)S(1)} collective-permute-done((bf16[128,128]{1,0:T(8,128)(2,1)S(1)}, bf16[128,128]{1,0:T(8,128)(2,1)S(1)}, u32[]{:S(2)}, u32[]{:S(2)}) %collective-permute-start.20) | collective-permute-done | bytes 32800 | tf_op jit(solution)/shard_map/ppermute | solution.py:60
  66.1 2.4 %collective-permute-done.23 = bf16[1024,256]{1,0:T(8,128)(2,1)S(1)} collective-permute-done((bf16[1024,256]{1,0:T(8,128)(2,1)S(1)}, bf16[1024,256]{1,0:T(8,128)(2,1)S(1)}, u32[]{:S(2)}, u32[]{:S(2)}) %collective-permute-start.23) | collective-permute-done | bytes 524320 | tf_op jit(solution)/shard_map/ppermute | solution.py:43
  68.9 1.5 %collective-permute-done.24.d_other = bf16[256,512]{1,0:T(8,128)(2,1)S(1)} collective-permute-done((bf16[256,512]{1,0:T(8,128)(2,1)S(1)}, bf16[256,512]{1,0:T(8,128)(2,1)S(1)}, u32[]{:S(2)}, u32[]{:S(2)}) %collective-permute-start.24) | collective-permute-done | bytes 262176 | tf_op jit(solution)/shard_map/ppermute | solution.py:64
  70.5 1.8 %weight_grads.1 = (bf16[4,256,512]{2,1,0:T(8,128)(2,1)S(1)}, bf16[4,256,512]{2,1,0:T(8,128)(2,1)S(1)}) custom-call(bf16[16,256,256]{2,1,0:T(8,128)(2,1)S(1)} %sort_blocks.2.t_own, bf16[8,256,256]{2,1,0:T(8,128)(2,1)S(1)} %collective-permute-done.18.t_other, bf16[16,256,256]{2,1,0:T(8,128)(2,1)S(1)} %sort_blocks.3.g_own, ...), custom_call_target="tpu_custom_call" | custom-call | flops 1073741824 | bytes 6291456 | tf_op jit(solution)/shard_map/weight_grads/pallas_call | solution.py:157
  74.3 1.8 %collective-permute-start.28 = (bf16[1024,256]{1,0:T(8,128)(2,1)S(1)}, bf16[1024,256]{1,0:T(8,128)(2,1)S(1)}, u32[]{:S(2)}, u32[]{:S(2)}) collective-permute-start(bf16[1024,256]{1,0:T(8,128)(2,1)S(1)} %part_terms.14), channel_id=1, source_target_pairs={{0,2},{1,3},{2,0},{3,1},{4,6},{5,7},{6,4},{7,5},{8,10},{9,11},{10,... | collective-permute-start | bytes 1572872 | tf_op jit(solution)/shard_map/ppermute | solution.py:43
  78.0 9.1 %collective-permute-done.25 = bf16[4,256,512]{2,1,0:T(8,128)(2,1)S(1)} collective-permute-done((bf16[4,256,512]{2,1,0:T(8,128)(2,1)S(1)}, bf16[4,256,512]{2,1,0:T(8,128)(2,1)S(1)}, u32[]{:S(2)}, u32[]{:S(2)}) %collective-permute-start.25) | collective-permute-done | bytes 1048608 | tf_op jit(solution)/shard_map/ppermute | solution.py:60
  87.5 1.8 %collective-permute-start.26 = (bf16[512,512]{1,0:T(8,128)(2,1)S(1)}, bf16[512,512]{1,0:T(8,128)(2,1)S(1)}, u32[]{:S(2)}, u32[]{:S(2)}) collective-permute-start(bf16[512,512]{1,0:T(8,128)(2,1)S(1)} %bitcast.49), channel_id=1, source_target_pairs={{0,64},{16,80},{32,96},{48,112},{64,0},{80,16},{96,32},{112,48},{1... | collective-permute-start | bytes 1572872 | tf_op jit(solution)/shard_map/ppermute | solution.py:60
  89.3 1.4 %collective-permute-done.29 = bf16[1024,256]{1,0:T(8,128)(2,1)S(1)} collective-permute-done((bf16[1024,256]{1,0:T(8,128)(2,1)S(1)}, bf16[1024,256]{1,0:T(8,128)(2,1)S(1)}, u32[]{:S(2)}, u32[]{:S(2)}) %collective-permute-start.29) | collective-permute-done | bytes 524320 | tf_op jit(solution)/shard_map/ppermute | solution.py:43
  93.5 1.5 %collective-permute-start.32 = (bf16[2,256,256]{2,1,0:T(8,128)(2,1)S(1)}, bf16[2,256,256]{2,1,0:T(8,128)(2,1)S(1)}, u32[]{:S(2)}, u32[]{:S(2)}) collective-permute-start(bf16[2,256,256]{2,1,0:T(8,128)(2,1)S(1)} %pad_maximum_fusion.6), channel_id=1, source_target_pairs={{0,4},{1,5},{2,6},{3,7},{4,8},{5,9},{6,10},{7,11},{8,12},{9,13},{1... | collective-permute-start | bytes 786440 | tf_op jit(solution)/shard_map/ppermute | solution.py:43
  95.0 8.4 %collective-permute-done.26.got = bf16[512,512]{1,0:T(8,128)(2,1)S(1)} collective-permute-done((bf16[512,512]{1,0:T(8,128)(2,1)S(1)}, bf16[512,512]{1,0:T(8,128)(2,1)S(1)}, u32[]{:S(2)}, u32[]{:S(2)}) %collective-permute-start.26) | collective-permute-done | bytes 524320 | tf_op jit(solution)/shard_map/ppermute | solution.py:60
  (112 shorter events, 30.1 us)
Async XLA Ops:
  1.8 9.8 %collective-permute-start.2 = (bf16[256,256]{1,0:T(8,128)(2,1)S(1)}, bf16[256,256]{1,0:T(8,128)(2,1)S(1)}, u32[]{:S(2)}, u32[]{:S(2)}) collective-permute-start(bf16[256,256]{1,0:T(8,128)(2,1)S(1)} %bitcast.54), channel_id=1, source_target_pairs={{0,12},{1,13},{2,14},{3,15},{4,0},{5,1},{6,2},{7,3},{8,4},{9,5},{1... | collective-permute-start | bytes 393224 | tf_op jit(solution)/shard_map/ppermute | solution.py:43
  5.6 7.2 %collective-permute-start = (bf16[256,256]{1,0:T(8,128)(2,1)S(1)}, bf16[256,256]{1,0:T(8,128)(2,1)S(1)}, u32[]{:S(2)}, u32[]{:S(2)}) collective-permute-start(bf16[256,256]{1,0:T(8,128)(2,1)S(1)} %bitcast.56), channel_id=1, source_target_pairs={{0,4},{1,5},{2,6},{3,7},{4,8},{5,9},{6,10},{7,11},{8,12},{9,13},{1... | collective-permute-start | bytes 393224 | tf_op jit(solution)/shard_map/ppermute | solution.py:43
  7.6 9.6 %collective-permute-start.12 = (bf16[256,256]{1,0:T(8,128)(2,1)S(1)}, bf16[256,256]{1,0:T(8,128)(2,1)S(1)}, u32[]{:S(2)}, u32[]{:S(2)}) collective-permute-start(bf16[256,256]{1,0:T(8,128)(2,1)S(1)} %bitcast.50), channel_id=1, source_target_pairs={{0,12},{1,13},{2,14},{3,15},{4,0},{5,1},{6,2},{7,3},{8,4},{9,5},{1... | collective-permute-start | bytes 393224 | tf_op jit(solution)/shard_map/ppermute | solution.py:43
  9.9 8.5 %collective-permute-start.11 = (bf16[256,256]{1,0:T(8,128)(2,1)S(1)}, bf16[256,256]{1,0:T(8,128)(2,1)S(1)}, u32[]{:S(2)}, u32[]{:S(2)}) collective-permute-start(bf16[256,256]{1,0:T(8,128)(2,1)S(1)} %bitcast.51), channel_id=1, source_target_pairs={{0,8},{1,9},{2,10},{3,11},{4,12},{5,13},{6,14},{7,15},{8,0},{9,1},... | collective-permute-start | bytes 393224 | tf_op jit(solution)/shard_map/ppermute | solution.py:43
  11.6 6.8 %collective-permute-start.10 = (bf16[256,256]{1,0:T(8,128)(2,1)S(1)}, bf16[256,256]{1,0:T(8,128)(2,1)}, u32[]{:S(2)}, u32[]{:S(2)}) collective-permute-start(bf16[256,256]{1,0:T(8,128)(2,1)S(1)} %bitcast.52), channel_id=1, source_target_pairs={{0,4},{1,5},{2,6},{3,7},{4,8},{5,9},{6,10},{7,11},{8,12},{9,13},{1... | collective-permute-start | bytes 393224 | tf_op jit(solution)/shard_map/ppermute | solution.py:43
  12.9 20.8 %collective-permute-start.5 = (bf16[1024,256]{1,0:T(8,128)(2,1)S(1)}, bf16[1024,256]{1,0:T(8,128)(2,1)S(1)}, u32[]{:S(2)}, u32[]{:S(2)}) collective-permute-start(bf16[1024,256]{1,0:T(8,128)(2,1)S(1)} %pad_maximum_fusion.a0), channel_id=1, source_target_pairs={{0,3},{1,0},{2,1},{3,2},{4,7},{5,4},{6,5},{7,6},{8,11},{9,8},{10,9... | collective-permute-start | bytes 1572872 | tf_op jit(solution)/shard_map/ppermute | solution.py:43
  17.1 19.0 %collective-permute-start.4 = (bf16[1024,256]{1,0:T(8,128)(2,1)S(1)}, bf16[1024,256]{1,0:T(8,128)(2,1)S(1)}, u32[]{:S(2)}, u32[]{:S(2)}) collective-permute-start(bf16[1024,256]{1,0:T(8,128)(2,1)S(1)} %pad_maximum_fusion.a0), channel_id=1, source_target_pairs={{0,2},{1,3},{2,0},{3,1},{4,6},{5,7},{6,4},{7,5},{8,10},{9,11},{10,... | collective-permute-start | bytes 1572872 | tf_op jit(solution)/shard_map/ppermute | solution.py:43
  17.2 18.4 %collective-permute-start.3 = (bf16[1024,256]{1,0:T(8,128)(2,1)S(1)}, bf16[1024,256]{1,0:T(8,128)(2,1)S(1)}, u32[]{:S(2)}, u32[]{:S(2)}) collective-permute-start(bf16[1024,256]{1,0:T(8,128)(2,1)S(1)} %pad_maximum_fusion.a0), channel_id=1, source_target_pairs={{0,1},{1,2},{2,3},{3,0},{4,5},{5,6},{6,7},{7,4},{8,9},{9,10},{10,1... | collective-permute-start | bytes 1572872 | tf_op jit(solution)/shard_map/ppermute | solution.py:43
  19.4 22.4 %collective-permute-start.15 = (bf16[1024,256]{1,0:T(8,128)(2,1)S(1)}, bf16[1024,256]{1,0:T(8,128)(2,1)S(1)}, u32[]{:S(2)}, u32[]{:S(2)}) collective-permute-start(bf16[1024,256]{1,0:T(8,128)(2,1)S(1)} %pad_maximum_fusion.1.a0), channel_id=1, source_target_pairs={{0,3},{1,0},{2,1},{3,2},{4,7},{5,4},{6,5},{7,6},{8,11},{9,8},{10,9... | collective-permute-start | bytes 1572872 | tf_op jit(solution)/shard_map/ppermute | solution.py:43
  29.2 12.5 %collective-permute-start.14 = (bf16[1024,256]{1,0:T(8,128)(2,1)S(1)}, bf16[1024,256]{1,0:T(8,128)(2,1)S(1)}, u32[]{:S(2)}, u32[]{:S(2)}) collective-permute-start(bf16[1024,256]{1,0:T(8,128)(2,1)S(1)} %pad_maximum_fusion.1.a0), channel_id=1, source_target_pairs={{0,2},{1,3},{2,0},{3,1},{4,6},{5,7},{6,4},{7,5},{8,10},{9,11},{10,... | collective-permute-start | bytes 1572872 | tf_op jit(solution)/shard_map/ppermute | solution.py:43
  33.7 11.8 %collective-permute-start.13 = (bf16[1024,256]{1,0:T(8,128)(2,1)S(1)}, bf16[1024,256]{1,0:T(8,128)(2,1)S(1)}, u32[]{:S(2)}, u32[]{:S(2)}) collective-permute-start(bf16[1024,256]{1,0:T(8,128)(2,1)S(1)} %pad_maximum_fusion.1.a0), channel_id=1, source_target_pairs={{0,1},{1,2},{2,3},{3,0},{4,5},{5,6},{6,7},{7,4},{8,9},{9,10},{10,1... | collective-permute-start | bytes 1572872 | tf_op jit(solution)/shard_map/ppermute | solution.py:43
  38.0 8.2 %collective-permute-start.8 = (bf16[128,128]{1,0:T(8,128)(2,1)S(1)}, bf16[128,128]{1,0:T(8,128)(2,1)S(1)}, u32[]{:S(2)}, u32[]{:S(2)}) collective-permute-start(bf16[128,128]{1,0:T(8,128)(2,1)S(1)} %fusion.28), channel_id=1, source_target_pairs={{0,64},{32,96},{64,0},{96,32},{1,65},{33,97},{65,1},{97,33},{2,66}... | collective-permute-start | bytes 98312 | tf_op jit(solution)/shard_map/ppermute | solution.py:47
  50.3 15.8 %collective-permute-start.21 = (bf16[1024,256]{1,0:T(8,128)(2,1)S(1)}, bf16[1024,256]{1,0:T(8,128)(2,1)S(1)}, u32[]{:S(2)}, u32[]{:S(2)}) collective-permute-start(bf16[1024,256]{1,0:T(8,128)(2,1)S(1)} %part_terms.9), channel_id=1, source_target_pairs={{0,3},{1,0},{2,1},{3,2},{4,7},{5,4},{6,5},{7,6},{8,11},{9,8},{10,9... | collective-permute-start | bytes 1572872 | tf_op jit(solution)/shard_map/ppermute | solution.py:43
  52.2 13.8 %collective-permute-start.22 = (bf16[1024,256]{1,0:T(8,128)(2,1)S(1)}, bf16[1024,256]{1,0:T(8,128)(2,1)S(1)}, u32[]{:S(2)}, u32[]{:S(2)}) collective-permute-start(bf16[1024,256]{1,0:T(8,128)(2,1)S(1)} %part_terms.10), channel_id=1, source_target_pairs={{0,2},{1,3},{2,0},{3,1},{4,6},{5,7},{6,4},{7,5},{8,10},{9,11},{10,... | collective-permute-start | bytes 1572872 | tf_op jit(solution)/shard_map/ppermute | solution.py:43
  54.3 14.2 %collective-permute-start.23 = (bf16[1024,256]{1,0:T(8,128)(2,1)S(1)}, bf16[1024,256]{1,0:T(8,128)(2,1)S(1)}, u32[]{:S(2)}, u32[]{:S(2)}) collective-permute-start(bf16[1024,256]{1,0:T(8,128)(2,1)S(1)} %part_terms.11), channel_id=1, source_target_pairs={{0,1},{1,2},{2,3},{3,0},{4,5},{5,6},{6,7},{7,4},{8,9},{9,10},{10,1... | collective-permute-start | bytes 1572872 | tf_op jit(solution)/shard_map/ppermute | solution.py:43
  61.9 8.6 %collective-permute-start.19 = (bf16[8,256,256]{2,1,0:T(8,128)(2,1)S(1)}, bf16[8,256,256]{2,1,0:T(8,128)(2,1)S(1)}, u32[]{:S(2)}, u32[]{:S(2)}) collective-permute-start(bf16[8,256,256]{2,1,0:T(8,128)(2,1)S(1)} %slice.130), channel_id=1, source_target_pairs={{0,16},{16,0},{1,17},{17,1},{2,18},{18,2},{3,19},{19,3},{4,20},{20... | collective-permute-start | bytes 3145736 | tf_op jit(solution)/shard_map/ppermute | solution.py:64
  72.3 14.9 %collective-permute-start.25 = (bf16[4,256,512]{2,1,0:T(8,128)(2,1)S(1)}, bf16[4,256,512]{2,1,0:T(8,128)(2,1)S(1)}, u32[]{:S(2)}, u32[]{:S(2)}) collective-permute-start(bf16[4,256,512]{2,1,0:T(8,128)(2,1)S(1)} %get-tuple-element.57), channel_id=1, source_target_pairs={{0,32},{16,112},{32,0},{48,80},{64,96},{80,48},{96,64},{112,16},{1... | collective-permute-start | bytes 3145736 | tf_op jit(solution)/shard_map/ppermute | solution.py:60
  73.0 16.3 %collective-permute-start.27 = (bf16[1024,256]{1,0:T(8,128)(2,1)S(1)}, bf16[1024,256]{1,0:T(8,128)(2,1)S(1)}, u32[]{:S(2)}, u32[]{:S(2)}) collective-permute-start(bf16[1024,256]{1,0:T(8,128)(2,1)S(1)} %part_terms.13), channel_id=1, source_target_pairs={{0,3},{1,0},{2,1},{3,2},{4,7},{5,4},{6,5},{7,6},{8,11},{9,8},{10,9... | collective-permute-start | bytes 1572872 | tf_op jit(solution)/shard_map/ppermute | solution.py:43
  74.3 15.0 %collective-permute-start.28 = (bf16[1024,256]{1,0:T(8,128)(2,1)S(1)}, bf16[1024,256]{1,0:T(8,128)(2,1)S(1)}, u32[]{:S(2)}, u32[]{:S(2)}) collective-permute-start(bf16[1024,256]{1,0:T(8,128)(2,1)S(1)} %part_terms.14), channel_id=1, source_target_pairs={{0,2},{1,3},{2,0},{3,1},{4,6},{5,7},{6,4},{7,5},{8,10},{9,11},{10,... | collective-permute-start | bytes 1572872 | tf_op jit(solution)/shard_map/ppermute | solution.py:43
  76.6 14.1 %collective-permute-start.29 = (bf16[1024,256]{1,0:T(8,128)(2,1)S(1)}, bf16[1024,256]{1,0:T(8,128)(2,1)S(1)}, u32[]{:S(2)}, u32[]{:S(2)}) collective-permute-start(bf16[1024,256]{1,0:T(8,128)(2,1)S(1)} %part_terms.15), channel_id=1, source_target_pairs={{0,1},{1,2},{2,3},{3,0},{4,5},{5,6},{6,7},{7,4},{8,9},{9,10},{10,1... | collective-permute-start | bytes 1572872 | tf_op jit(solution)/shard_map/ppermute | solution.py:43
  87.5 15.9 %collective-permute-start.26 = (bf16[512,512]{1,0:T(8,128)(2,1)S(1)}, bf16[512,512]{1,0:T(8,128)(2,1)S(1)}, u32[]{:S(2)}, u32[]{:S(2)}) collective-permute-start(bf16[512,512]{1,0:T(8,128)(2,1)S(1)} %bitcast.49), channel_id=1, source_target_pairs={{0,64},{16,80},{32,96},{48,112},{64,0},{80,16},{96,32},{112,48},{1... | collective-permute-start | bytes 1572872 | tf_op jit(solution)/shard_map/ppermute | solution.py:60
  91.1 13.4 %collective-permute-start.30 = (bf16[2,256,256]{2,1,0:T(8,128)(2,1)S(1)}, bf16[2,256,256]{2,1,0:T(8,128)(2,1)S(1)}, u32[]{:S(2)}, u32[]{:S(2)}) collective-permute-start(bf16[2,256,256]{2,1,0:T(8,128)(2,1)S(1)} %pad_maximum_fusion.4), channel_id=1, source_target_pairs={{0,12},{1,13},{2,14},{3,15},{4,0},{5,1},{6,2},{7,3},{8,4},{9,5},{1... | collective-permute-start | bytes 786440 | tf_op jit(solution)/shard_map/ppermute | solution.py:43
  92.3 12.2 %collective-permute-start.31 = (bf16[2,256,256]{2,1,0:T(8,128)(2,1)S(1)}, bf16[2,256,256]{2,1,0:T(8,128)(2,1)S(1)}, u32[]{:S(2)}, u32[]{:S(2)}) collective-permute-start(bf16[2,256,256]{2,1,0:T(8,128)(2,1)S(1)} %pad_maximum_fusion.5), channel_id=1, source_target_pairs={{0,8},{1,9},{2,10},{3,11},{4,12},{5,13},{6,14},{7,15},{8,0},{9,1},... | collective-permute-start | bytes 786440 | tf_op jit(solution)/shard_map/ppermute | solution.py:43
  93.5 11.0 %collective-permute-start.32 = (bf16[2,256,256]{2,1,0:T(8,128)(2,1)S(1)}, bf16[2,256,256]{2,1,0:T(8,128)(2,1)S(1)}, u32[]{:S(2)}, u32[]{:S(2)}) collective-permute-start(bf16[2,256,256]{2,1,0:T(8,128)(2,1)S(1)} %pad_maximum_fusion.6), channel_id=1, source_target_pairs={{0,4},{1,5},{2,6},{3,7},{4,8},{5,9},{6,10},{7,11},{8,12},{9,13},{1... | collective-permute-start | bytes 786440 | tf_op jit(solution)/shard_map/ppermute | solution.py:43
  (14 other events, 93.0 us)

commit v5 on v4

--- a/solution.py
+++ b/solution.py
@@ -345,9 +345,10 @@
     grad_values = (mm(scores, grad_mixed, TN) + mm(keys, later, NN)).astype(HALF)
     out_sum = total(out_got).astype(HALF)
     cotangents = jnp.concatenate([grad_query, grad_keys, grad_values, normed], axis=1)
+    other_cotangents = core_swap(cotangents)
     cotangents, out_sum = lax.optimization_barrier((cotangents, out_sum))
     keep, send = weight_grads(
-        t_sorted, t_other, g_sorted, g_other, cotangents, core_swap(cotangents)
+        t_sorted, t_other, g_sorted, g_other, cotangents, other_cotangents
     )
     sent = x_partner(send, (1, 3))
     in_terms = [part_terms(w_qkv, d, cotangents) for d in range(SIDE)]
@@ -356,11 +357,10 @@
     mine = mine.reshape(2, -1, mine.shape[2])
     own, send = mine[0], mine[1]
     in_got = after((own, send), in_got)
-    grads = split_sum(own, x_partner(send, (2, 2)))
     got = fold_phase2((out_sum, total(in_got).astype(HALF)))
-    got = after(grads, got)
     result = total([g[0] for g in got]).astype(HALF)
     grad_tokens = total([g[1] for g in got])
+    grads = split_sum(after((result, grad_tokens), own), x_partner(send, (2, 2)))
     return (
         result,
         grad_tokens,

time: 106 us -> 104 us (0.981)
  waiting for transfers between devices: 35.6 us -> 30.8 us
  starting transfers between devices: 45.8 us -> 49 us
    ppermute x4, waiting for transfers between devices: 23.8 us -> 14.5 us  [x_partner(): return lax.ppermute(a, SEQ, pairs)]
    ppermute x21, waiting for transfers between devices: 8.9 us -> 14.9 us  [plane_shift(): return lax.ppermute(a, PLANE, plane_pairs(phase, shift))]
    ppermute x21, starting transfers between devices: 37.1 us -> 39.8 us  [plane_shift(): return lax.ppermute(a, PLANE, plane_pairs(phase, shift))]
    ppermute x6, waiting for transfers between devices: 2.85 us -> 1.33 us  [core_swap(): return lax.ppermute(a, 'core', [(0, 1), (1, 0)])]
  transfers between devices with their start and end apart: 33 -> 33, of which waited for: 12 -> 12; matrix products, arithmetic and copies ran while one was open for 8% -> 9% of each run, Pallas kernels for 5% -> 4%
where the time goes in v5:
time: 104 us
  starting transfers between devices  49 us (47%)
  waiting for transfers between devices  30.8 us (30%)
  Pallas kernels  8.58 us (8%)
  matrix products  5.51 us (5%)
  local copies, waits for them, and re-layouts  4.88 us (5%)
  other arithmetic  3.77 us (4%)
  between operations  1.16 us (1%)
    ppermute x21, starting transfers between devices, plane_shift(): return lax.ppermute(a, PLANE, plane_pairs(phase, shift))  39.8 us
    ppermute x21, waiting for transfers between devices, plane_shift(): return lax.ppermute(a, PLANE, plane_pairs(phase, shift))  14.9 us
    ppermute x4, waiting for transfers between devices, x_partner(): return lax.ppermute(a, SEQ, pairs)  14.5 us
    dot_general x20, matrix products, mm(): return lax.dot_general(a, b, dims, preferred_element_type=WIDE)  5.51 us
    ppermute x4, starting transfers between devices, x_partner(): return lax.ppermute(a, SEQ, pairs)  4.73 us
    unnamed x12, local copies, waits for them, and re-layouts  4.61 us
    ppermute x1, starting transfers between devices, x_shift(): return lax.ppermute(a, 'x', [(i, (i + shift) % SIDE) for i in range(SIDE)])  3.1 us
    pallas_call x8, Pallas kernels, part_terms(): pl.pallas_call(part_terms_kernel, out_shape=jax.ShapeDtypeStruct((SIDE *...  3.08 us
  transfers between devices with their start and end apart: 33, of which 12 were waited for; matrix products, arithmetic and copies ran while one was open for 9% of the time, Pallas kernels for 4%

profile of v5, /device:TPU:0, one launch (start us, length us, event | category | flops | bytes accessed | tf_op | source)
XLA Modules:
  0.0 103.7 jit_solution(1566967858414358221)
XLA Ops:
  1.8 3.2 %collective-permute-start.2 = (bf16[256,256]{1,0:T(8,128)(2,1)S(1)}, bf16[256,256]{1,0:T(8,128)(2,1)S(1)}, u32[]{:S(2)}, u32[]{:S(2)}) collective-permute-start(bf16[256,256]{1,0:T(8,128)(2,1)S(1)} %bitcast.76), channel_id=1, source_target_pairs={{0,12},{1,13},{2,14},{3,15},{4,0},{5,1},{6,2},{7,3},{8,4},{9,5},{1... | collective-permute-start | bytes 393224 | tf_op jit(solution)/shard_map/ppermute | solution.py:43
  7.6 2.3 %collective-permute-start.12 = (bf16[256,256]{1,0:T(8,128)(2,1)S(1)}, bf16[256,256]{1,0:T(8,128)(2,1)S(1)}, u32[]{:S(2)}, u32[]{:S(2)}) collective-permute-start(bf16[256,256]{1,0:T(8,128)(2,1)S(1)} %bitcast.72), channel_id=1, source_target_pairs={{0,12},{1,13},{2,14},{3,15},{4,0},{5,1},{6,2},{7,3},{8,4},{9,5},{1... | collective-permute-start | bytes 393224 | tf_op jit(solution)/shard_map/ppermute | solution.py:43
  9.9 1.7 %collective-permute-start.11 = (bf16[256,256]{1,0:T(8,128)(2,1)S(1)}, bf16[256,256]{1,0:T(8,128)(2,1)S(1)}, u32[]{:S(2)}, u32[]{:S(2)}) collective-permute-start(bf16[256,256]{1,0:T(8,128)(2,1)S(1)} %bitcast.73), channel_id=1, source_target_pairs={{0,8},{1,9},{2,10},{3,11},{4,12},{5,13},{6,14},{7,15},{8,0},{9,1},... | collective-permute-start | bytes 393224 | tf_op jit(solution)/shard_map/ppermute | solution.py:43
  12.9 4.1 %collective-permute-start.5 = (bf16[1024,256]{1,0:T(8,128)(2,1)S(1)}, bf16[1024,256]{1,0:T(8,128)(2,1)S(1)}, u32[]{:S(2)}, u32[]{:S(2)}) collective-permute-start(bf16[1024,256]{1,0:T(8,128)(2,1)S(1)} %pad_maximum_fusion.a0), channel_id=1, source_target_pairs={{0,3},{1,0},{2,1},{3,2},{4,7},{5,4},{6,5},{7,6},{8,11},{9,8},{10,9... | collective-permute-start | bytes 1572872 | tf_op jit(solution)/shard_map/ppermute | solution.py:43
  19.4 9.9 %collective-permute-start.15 = (bf16[1024,256]{1,0:T(8,128)(2,1)S(1)}, bf16[1024,256]{1,0:T(8,128)(2,1)S(1)}, u32[]{:S(2)}, u32[]{:S(2)}) collective-permute-start(bf16[1024,256]{1,0:T(8,128)(2,1)S(1)} %pad_maximum_fusion.1.a0), channel_id=1, source_target_pairs={{0,3},{1,0},{2,1},{3,2},{4,7},{5,4},{6,5},{7,6},{8,11},{9,8},{10,9... | collective-permute-start | bytes 1572872 | tf_op jit(solution)/shard_map/ppermute | solution.py:43
  33.7 1.4 %collective-permute-start.13 = (bf16[1024,256]{1,0:T(8,128)(2,1)S(1)}, bf16[1024,256]{1,0:T(8,128)(2,1)S(1)}, u32[]{:S(2)}, u32[]{:S(2)}) collective-permute-start(bf16[1024,256]{1,0:T(8,128)(2,1)S(1)} %pad_maximum_fusion.1.a0), channel_id=1, source_target_pairs={{0,1},{1,2},{2,3},{3,0},{4,5},{5,6},{6,7},{7,4},{8,9},{9,10},{10,1... | collective-permute-start | bytes 1572872 | tf_op jit(solution)/shard_map/ppermute | solution.py:43
  38.0 3.1 %collective-permute-start.8 = (bf16[128,128]{1,0:T(8,128)(2,1)S(1)}, bf16[128,128]{1,0:T(8,128)(2,1)S(1)}, u32[]{:S(2)}, u32[]{:S(2)}) collective-permute-start(bf16[128,128]{1,0:T(8,128)(2,1)S(1)} %fusion.28), channel_id=1, source_target_pairs={{0,64},{32,96},{64,0},{96,32},{1,65},{33,97},{65,1},{97,33},{2,66}... | collective-permute-start | bytes 98312 | tf_op jit(solution)/shard_map/ppermute | solution.py:47
  41.8 3.8 %collective-permute-done.13.a1 = bf16[1024,256]{1,0:T(8,128)(2,1)S(1)} collective-permute-done((bf16[1024,256]{1,0:T(8,128)(2,1)S(1)}, bf16[1024,256]{1,0:T(8,128)(2,1)S(1)}, u32[]{:S(2)}, u32[]{:S(2)}) %collective-permute-start.13) | collective-permute-done | bytes 524320 | tf_op jit(solution)/shard_map/ppermute | solution.py:43
  50.3 1.9 %collective-permute-start.19 = (bf16[1024,256]{1,0:T(8,128)(2,1)S(1)}, bf16[1024,256]{1,0:T(8,128)(2,1)S(1)}, u32[]{:S(2)}, u32[]{:S(2)}) collective-permute-start(bf16[1024,256]{1,0:T(8,128)(2,1)S(1)} %part_terms.9), channel_id=1, source_target_pairs={{0,3},{1,0},{2,1},{3,2},{4,7},{5,4},{6,5},{7,6},{8,11},{9,8},{10,9... | collective-permute-start | bytes 1572872 | tf_op jit(solution)/shard_map/ppermute | solution.py:43
  52.2 2.1 %collective-permute-start.20 = (bf16[1024,256]{1,0:T(8,128)(2,1)S(1)}, bf16[1024,256]{1,0:T(8,128)(2,1)S(1)}, u32[]{:S(2)}, u32[]{:S(2)}) collective-permute-start(bf16[1024,256]{1,0:T(8,128)(2,1)S(1)} %part_terms.10), channel_id=1, source_target_pairs={{0,2},{1,3},{2,0},{3,1},{4,6},{5,7},{6,4},{7,5},{8,10},{9,11},{10,... | collective-permute-start | bytes 1572872 | tf_op jit(solution)/shard_map/ppermute | solution.py:43
  56.3 3.2 %collective-permute-done.17 = bf16[128,128]{1,0:T(8,128)(2,1)S(1)} collective-permute-done((bf16[128,128]{1,0:T(8,128)(2,1)S(1)}, bf16[128,128]{1,0:T(8,128)(2,1)S(1)}, u32[]{:S(2)}, u32[]{:S(2)}) %collective-permute-start.17) | collective-permute-done | bytes 32800 | tf_op jit(solution)/shard_map/ppermute | solution.py:60
  59.5 2.1 %collective-permute-start.18 = (bf16[128,128]{1,0:T(8,128)(2,1)S(1)}, bf16[128,128]{1,0:T(8,128)(2,1)S(1)}, u32[]{:S(2)}, u32[]{:S(2)}) collective-permute-start(bf16[128,128]{1,0:T(8,128)(2,1)S(1)} %fusion.33), channel_id=1, source_target_pairs={{0,64},{16,80},{32,96},{48,112},{64,0},{80,16},{96,32},{112,48},{1... | collective-permute-start | bytes 98312 | tf_op jit(solution)/shard_map/ppermute | solution.py:60
  62.0 3.1 %collective-permute-done.18 = bf16[128,128]{1,0:T(8,128)(2,1)S(1)} collective-permute-done((bf16[128,128]{1,0:T(8,128)(2,1)S(1)}, bf16[128,128]{1,0:T(8,128)(2,1)S(1)}, u32[]{:S(2)}, u32[]{:S(2)}) %collective-permute-start.18) | collective-permute-done | bytes 32800 | tf_op jit(solution)/shard_map/ppermute | solution.py:60
  66.7 1.9 %collective-permute-done.21 = bf16[1024,256]{1,0:T(8,128)(2,1)S(1)} collective-permute-done((bf16[1024,256]{1,0:T(8,128)(2,1)S(1)}, bf16[1024,256]{1,0:T(8,128)(2,1)S(1)}, u32[]{:S(2)}, u32[]{:S(2)}) %collective-permute-start.21) | collective-permute-done | bytes 524320 | tf_op jit(solution)/shard_map/ppermute | solution.py:43
  68.9 1.8 %weight_grads.1 = (bf16[4,256,512]{2,1,0:T(8,128)(2,1)S(1)}, bf16[4,256,512]{2,1,0:T(8,128)(2,1)S(1)}) custom-call(bf16[16,256,256]{2,1,0:T(8,128)(2,1)S(1)} %sort_blocks.2.t_own, bf16[8,256,256]{2,1,0:T(8,128)(2,1)S(1)} %collective-permute-done.22.t_other, bf16[16,256,256]{2,1,0:T(8,128)(2,1)S(1)} %sort_blocks.3.g_own, ...), custom_call_target="tpu_custom_call" | custom-call | flops 1073741824 | bytes 6291456 | tf_op jit(solution)/shard_map/weight_grads/pallas_call | solution.py:157
  71.4 2.4 %collective-permute-start.26 = (bf16[1024,256]{1,0:T(8,128)(2,1)S(1)}, bf16[1024,256]{1,0:T(8,128)(2,1)S(1)}, u32[]{:S(2)}, u32[]{:S(2)}) collective-permute-start(bf16[1024,256]{1,0:T(8,128)(2,1)S(1)} %part_terms.13), channel_id=1, source_target_pairs={{0,3},{1,0},{2,1},{3,2},{4,7},{5,4},{6,5},{7,6},{8,11},{9,8},{10,9... | collective-permute-start | bytes 1572872 | tf_op jit(solution)/shard_map/ppermute | solution.py:43
  75.3 1.5 %collective-permute-start.28 = (bf16[1024,256]{1,0:T(8,128)(2,1)S(1)}, bf16[1024,256]{1,0:T(8,128)(2,1)S(1)}, u32[]{:S(2)}, u32[]{:S(2)}) collective-permute-start(bf16[1024,256]{1,0:T(8,128)(2,1)S(1)} %part_terms.15), channel_id=1, source_target_pairs={{0,1},{1,2},{2,3},{3,0},{4,5},{5,6},{6,7},{7,4},{8,9},{9,10},{10,1... | collective-permute-start | bytes 1572872 | tf_op jit(solution)/shard_map/ppermute | solution.py:43
  77.3 8.3 %collective-permute-done.25 = bf16[4,256,512]{2,1,0:T(8,128)(2,1)S(1)} collective-permute-done((bf16[4,256,512]{2,1,0:T(8,128)(2,1)S(1)}, bf16[4,256,512]{2,1,0:T(8,128)(2,1)S(1)}, u32[]{:S(2)}, u32[]{:S(2)}) %collective-permute-start.25) | collective-permute-done | bytes 1048608 | tf_op jit(solution)/shard_map/ppermute | solution.py:60
  85.9 1.8 %collective-permute-start.32 = (bf16[512,512]{1,0:T(8,128)(2,1)S(1)}, bf16[512,512]{1,0:T(8,128)(2,1)S(1)}, u32[]{:S(2)}, u32[]{:S(2)}) collective-permute-start(bf16[512,512]{1,0:T(8,128)(2,1)S(1)} %bitcast.71), channel_id=1, source_target_pairs={{0,64},{16,80},{32,96},{48,112},{64,0},{80,16},{96,32},{112,48},{1... | collective-permute-start | bytes 1572872 | tf_op jit(solution)/shard_map/ppermute | solution.py:60
  87.7 2.9 %collective-permute-done.28 = bf16[1024,256]{1,0:T(8,128)(2,1)S(1)} collective-permute-done((bf16[1024,256]{1,0:T(8,128)(2,1)S(1)}, bf16[1024,256]{1,0:T(8,128)(2,1)S(1)}, u32[]{:S(2)}, u32[]{:S(2)}) %collective-permute-start.28) | collective-permute-done | bytes 524320 | tf_op jit(solution)/shard_map/ppermute | solution.py:43
  91.0 2.3 %collective-permute-start.30 = (bf16[2,256,256]{2,1,0:T(8,128)(2,1)S(1)}, bf16[2,256,256]{2,1,0:T(8,128)(2,1)S(1)}, u32[]{:S(2)}, u32[]{:S(2)}) collective-permute-start(bf16[2,256,256]{2,1,0:T(8,128)(2,1)S(1)} %pad_maximum_fusion.4), channel_id=1, source_target_pairs={{0,8},{1,9},{2,10},{3,11},{4,12},{5,13},{6,14},{7,15},{8,0},{9,1},... | collective-permute-start | bytes 786440 | tf_op jit(solution)/shard_map/ppermute | solution.py:43
  93.4 3.3 %collective-permute-start.29 = (bf16[2,256,256]{2,1,0:T(8,128)(2,1)S(1)}, bf16[2,256,256]{2,1,0:T(8,128)(2,1)S(1)}, u32[]{:S(2)}, u32[]{:S(2)}) collective-permute-start(bf16[2,256,256]{2,1,0:T(8,128)(2,1)S(1)} %pad_maximum_fusion.3), channel_id=1, source_target_pairs={{0,12},{1,13},{2,14},{3,15},{4,0},{5,1},{6,2},{7,3},{8,4},{9,5},{1... | collective-permute-start | bytes 786440 | tf_op jit(solution)/shard_map/ppermute | solution.py:43
  96.7 2.3 %collective-permute-done.30 = bf16[2,256,256]{2,1,0:T(8,128)(2,1)S(1)} collective-permute-done((bf16[2,256,256]{2,1,0:T(8,128)(2,1)S(1)}, bf16[2,256,256]{2,1,0:T(8,128)(2,1)S(1)}, u32[]{:S(2)}, u32[]{:S(2)}) %collective-permute-start.30) | collective-permute-done | bytes 262176 | tf_op jit(solution)/shard_map/ppermute | solution.py:43
  99.0 2.7 %collective-permute-done.31 = bf16[2,256,256]{2,1,0:T(8,128)(2,1)S(1)} collective-permute-done((bf16[2,256,256]{2,1,0:T(8,128)(2,1)S(1)}, bf16[2,256,256]{2,1,0:T(8,128)(2,1)S(1)}, u32[]{:S(2)}, u32[]{:S(2)}) %collective-permute-start.31) | collective-permute-done | bytes 262176 | tf_op jit(solution)/shard_map/ppermute | solution.py:43
  (111 shorter events, 29.7 us)
Async XLA Ops:
  1.8 9.8 %collective-permute-start.2 = (bf16[256,256]{1,0:T(8,128)(2,1)S(1)}, bf16[256,256]{1,0:T(8,128)(2,1)S(1)}, u32[]{:S(2)}, u32[]{:S(2)}) collective-permute-start(bf16[256,256]{1,0:T(8,128)(2,1)S(1)} %bitcast.76), channel_id=1, source_target_pairs={{0,12},{1,13},{2,14},{3,15},{4,0},{5,1},{6,2},{7,3},{8,4},{9,5},{1... | collective-permute-start | bytes 393224 | tf_op jit(solution)/shard_map/ppermute | solution.py:43
  5.6 7.2 %collective-permute-start = (bf16[256,256]{1,0:T(8,128)(2,1)S(1)}, bf16[256,256]{1,0:T(8,128)(2,1)S(1)}, u32[]{:S(2)}, u32[]{:S(2)}) collective-permute-start(bf16[256,256]{1,0:T(8,128)(2,1)S(1)} %bitcast.78), channel_id=1, source_target_pairs={{0,4},{1,5},{2,6},{3,7},{4,8},{5,9},{6,10},{7,11},{8,12},{9,13},{1... | collective-permute-start | bytes 393224 | tf_op jit(solution)/shard_map/ppermute | solution.py:43
  7.6 9.6 %collective-permute-start.12 = (bf16[256,256]{1,0:T(8,128)(2,1)S(1)}, bf16[256,256]{1,0:T(8,128)(2,1)S(1)}, u32[]{:S(2)}, u32[]{:S(2)}) collective-permute-start(bf16[256,256]{1,0:T(8,128)(2,1)S(1)} %bitcast.72), channel_id=1, source_target_pairs={{0,12},{1,13},{2,14},{3,15},{4,0},{5,1},{6,2},{7,3},{8,4},{9,5},{1... | collective-permute-start | bytes 393224 | tf_op jit(solution)/shard_map/ppermute | solution.py:43
  9.9 8.5 %collective-permute-start.11 = (bf16[256,256]{1,0:T(8,128)(2,1)S(1)}, bf16[256,256]{1,0:T(8,128)(2,1)S(1)}, u32[]{:S(2)}, u32[]{:S(2)}) collective-permute-start(bf16[256,256]{1,0:T(8,128)(2,1)S(1)} %bitcast.73), channel_id=1, source_target_pairs={{0,8},{1,9},{2,10},{3,11},{4,12},{5,13},{6,14},{7,15},{8,0},{9,1},... | collective-permute-start | bytes 393224 | tf_op jit(solution)/shard_map/ppermute | solution.py:43
  11.6 6.8 %collective-permute-start.10 = (bf16[256,256]{1,0:T(8,128)(2,1)S(1)}, bf16[256,256]{1,0:T(8,128)(2,1)}, u32[]{:S(2)}, u32[]{:S(2)}) collective-permute-start(bf16[256,256]{1,0:T(8,128)(2,1)S(1)} %bitcast.74), channel_id=1, source_target_pairs={{0,4},{1,5},{2,6},{3,7},{4,8},{5,9},{6,10},{7,11},{8,12},{9,13},{1... | collective-permute-start | bytes 393224 | tf_op jit(solution)/shard_map/ppermute | solution.py:43
  12.9 20.8 %collective-permute-start.5 = (bf16[1024,256]{1,0:T(8,128)(2,1)S(1)}, bf16[1024,256]{1,0:T(8,128)(2,1)S(1)}, u32[]{:S(2)}, u32[]{:S(2)}) collective-permute-start(bf16[1024,256]{1,0:T(8,128)(2,1)S(1)} %pad_maximum_fusion.a0), channel_id=1, source_target_pairs={{0,3},{1,0},{2,1},{3,2},{4,7},{5,4},{6,5},{7,6},{8,11},{9,8},{10,9... | collective-permute-start | bytes 1572872 | tf_op jit(solution)/shard_map/ppermute | solution.py:43
  17.1 19.0 %collective-permute-start.4 = (bf16[1024,256]{1,0:T(8,128)(2,1)S(1)}, bf16[1024,256]{1,0:T(8,128)(2,1)S(1)}, u32[]{:S(2)}, u32[]{:S(2)}) collective-permute-start(bf16[1024,256]{1,0:T(8,128)(2,1)S(1)} %pad_maximum_fusion.a0), channel_id=1, source_target_pairs={{0,2},{1,3},{2,0},{3,1},{4,6},{5,7},{6,4},{7,5},{8,10},{9,11},{10,... | collective-permute-start | bytes 1572872 | tf_op jit(solution)/shard_map/ppermute | solution.py:43
  17.2 18.4 %collective-permute-start.3 = (bf16[1024,256]{1,0:T(8,128)(2,1)S(1)}, bf16[1024,256]{1,0:T(8,128)(2,1)S(1)}, u32[]{:S(2)}, u32[]{:S(2)}) collective-permute-start(bf16[1024,256]{1,0:T(8,128)(2,1)S(1)} %pad_maximum_fusion.a0), channel_id=1, source_target_pairs={{0,1},{1,2},{2,3},{3,0},{4,5},{5,6},{6,7},{7,4},{8,9},{9,10},{10,1... | collective-permute-start | bytes 1572872 | tf_op jit(solution)/shard_map/ppermute | solution.py:43
  19.4 22.4 %collective-permute-start.15 = (bf16[1024,256]{1,0:T(8,128)(2,1)S(1)}, bf16[1024,256]{1,0:T(8,128)(2,1)S(1)}, u32[]{:S(2)}, u32[]{:S(2)}) collective-permute-start(bf16[1024,256]{1,0:T(8,128)(2,1)S(1)} %pad_maximum_fusion.1.a0), channel_id=1, source_target_pairs={{0,3},{1,0},{2,1},{3,2},{4,7},{5,4},{6,5},{7,6},{8,11},{9,8},{10,9... | collective-permute-start | bytes 1572872 | tf_op jit(solution)/shard_map/ppermute | solution.py:43
  29.2 12.5 %collective-permute-start.14 = (bf16[1024,256]{1,0:T(8,128)(2,1)S(1)}, bf16[1024,256]{1,0:T(8,128)(2,1)S(1)}, u32[]{:S(2)}, u32[]{:S(2)}) collective-permute-start(bf16[1024,256]{1,0:T(8,128)(2,1)S(1)} %pad_maximum_fusion.1.a0), channel_id=1, source_target_pairs={{0,2},{1,3},{2,0},{3,1},{4,6},{5,7},{6,4},{7,5},{8,10},{9,11},{10,... | collective-permute-start | bytes 1572872 | tf_op jit(solution)/shard_map/ppermute | solution.py:43
  33.7 11.8 %collective-permute-start.13 = (bf16[1024,256]{1,0:T(8,128)(2,1)S(1)}, bf16[1024,256]{1,0:T(8,128)(2,1)S(1)}, u32[]{:S(2)}, u32[]{:S(2)}) collective-permute-start(bf16[1024,256]{1,0:T(8,128)(2,1)S(1)} %pad_maximum_fusion.1.a0), channel_id=1, source_target_pairs={{0,1},{1,2},{2,3},{3,0},{4,5},{5,6},{6,7},{7,4},{8,9},{9,10},{10,1... | collective-permute-start | bytes 1572872 | tf_op jit(solution)/shard_map/ppermute | solution.py:43
  38.0 8.2 %collective-permute-start.8 = (bf16[128,128]{1,0:T(8,128)(2,1)S(1)}, bf16[128,128]{1,0:T(8,128)(2,1)S(1)}, u32[]{:S(2)}, u32[]{:S(2)}) collective-permute-start(bf16[128,128]{1,0:T(8,128)(2,1)S(1)} %fusion.28), channel_id=1, source_target_pairs={{0,64},{32,96},{64,0},{96,32},{1,65},{33,97},{65,1},{97,33},{2,66}... | collective-permute-start | bytes 98312 | tf_op jit(solution)/shard_map/ppermute | solution.py:47
  50.3 15.8 %collective-permute-start.19 = (bf16[1024,256]{1,0:T(8,128)(2,1)S(1)}, bf16[1024,256]{1,0:T(8,128)(2,1)S(1)}, u32[]{:S(2)}, u32[]{:S(2)}) collective-permute-start(bf16[1024,256]{1,0:T(8,128)(2,1)S(1)} %part_terms.9), channel_id=1, source_target_pairs={{0,3},{1,0},{2,1},{3,2},{4,7},{5,4},{6,5},{7,6},{8,11},{9,8},{10,9... | collective-permute-start | bytes 1572872 | tf_op jit(solution)/shard_map/ppermute | solution.py:43
  52.2 14.4 %collective-permute-start.20 = (bf16[1024,256]{1,0:T(8,128)(2,1)S(1)}, bf16[1024,256]{1,0:T(8,128)(2,1)S(1)}, u32[]{:S(2)}, u32[]{:S(2)}) collective-permute-start(bf16[1024,256]{1,0:T(8,128)(2,1)S(1)} %part_terms.10), channel_id=1, source_target_pairs={{0,2},{1,3},{2,0},{3,1},{4,6},{5,7},{6,4},{7,5},{8,10},{9,11},{10,... | collective-permute-start | bytes 1572872 | tf_op jit(solution)/shard_map/ppermute | solution.py:43
  54.3 14.2 %collective-permute-start.21 = (bf16[1024,256]{1,0:T(8,128)(2,1)S(1)}, bf16[1024,256]{1,0:T(8,128)(2,1)S(1)}, u32[]{:S(2)}, u32[]{:S(2)}) collective-permute-start(bf16[1024,256]{1,0:T(8,128)(2,1)S(1)} %part_terms.11), channel_id=1, source_target_pairs={{0,1},{1,2},{2,3},{3,0},{4,5},{5,6},{6,7},{7,4},{8,9},{9,10},{10,1... | collective-permute-start | bytes 1572872 | tf_op jit(solution)/shard_map/ppermute | solution.py:43
  61.9 7.0 %collective-permute-start.23 = (bf16[8,256,256]{2,1,0:T(8,128)(2,1)S(1)}, bf16[8,256,256]{2,1,0:T(8,128)(2,1)S(1)}, u32[]{:S(2)}, u32[]{:S(2)}) collective-permute-start(bf16[8,256,256]{2,1,0:T(8,128)(2,1)S(1)} %slice.122), channel_id=1, source_target_pairs={{0,16},{16,0},{1,17},{17,1},{2,18},{18,2},{3,19},{19,3},{4,20},{20... | collective-permute-start | bytes 3145736 | tf_op jit(solution)/shard_map/ppermute | solution.py:64
  70.7 14.9 %collective-permute-start.25 = (bf16[4,256,512]{2,1,0:T(8,128)(2,1)S(1)}, bf16[4,256,512]{2,1,0:T(8,128)(2,1)S(1)}, u32[]{:S(2)}, u32[]{:S(2)}) collective-permute-start(bf16[4,256,512]{2,1,0:T(8,128)(2,1)S(1)} %get-tuple-element.55), channel_id=1, source_target_pairs={{0,32},{16,112},{32,0},{48,80},{64,96},{80,48},{96,64},{112,16},{1... | collective-permute-start | bytes 3145736 | tf_op jit(solution)/shard_map/ppermute | solution.py:60
  71.4 16.3 %collective-permute-start.26 = (bf16[1024,256]{1,0:T(8,128)(2,1)S(1)}, bf16[1024,256]{1,0:T(8,128)(2,1)S(1)}, u32[]{:S(2)}, u32[]{:S(2)}) collective-permute-start(bf16[1024,256]{1,0:T(8,128)(2,1)S(1)} %part_terms.13), channel_id=1, source_target_pairs={{0,3},{1,0},{2,1},{3,2},{4,7},{5,4},{6,5},{7,6},{8,11},{9,8},{10,9... | collective-permute-start | bytes 1572872 | tf_op jit(solution)/shard_map/ppermute | solution.py:43
  74.3 13.5 %collective-permute-start.27 = (bf16[1024,256]{1,0:T(8,128)(2,1)S(1)}, bf16[1024,256]{1,0:T(8,128)(2,1)S(1)}, u32[]{:S(2)}, u32[]{:S(2)}) collective-permute-start(bf16[1024,256]{1,0:T(8,128)(2,1)S(1)} %part_terms.14), channel_id=1, source_target_pairs={{0,2},{1,3},{2,0},{3,1},{4,6},{5,7},{6,4},{7,5},{8,10},{9,11},{10,... | collective-permute-start | bytes 1572872 | tf_op jit(solution)/shard_map/ppermute | solution.py:43
  75.3 15.3 %collective-permute-start.28 = (bf16[1024,256]{1,0:T(8,128)(2,1)S(1)}, bf16[1024,256]{1,0:T(8,128)(2,1)S(1)}, u32[]{:S(2)}, u32[]{:S(2)}) collective-permute-start(bf16[1024,256]{1,0:T(8,128)(2,1)S(1)} %part_terms.15), channel_id=1, source_target_pairs={{0,1},{1,2},{2,3},{3,0},{4,5},{5,6},{6,7},{7,4},{8,9},{9,10},{10,1... | collective-permute-start | bytes 1572872 | tf_op jit(solution)/shard_map/ppermute | solution.py:43
  85.9 16.7 %collective-permute-start.32 = (bf16[512,512]{1,0:T(8,128)(2,1)S(1)}, bf16[512,512]{1,0:T(8,128)(2,1)S(1)}, u32[]{:S(2)}, u32[]{:S(2)}) collective-permute-start(bf16[512,512]{1,0:T(8,128)(2,1)S(1)} %bitcast.71), channel_id=1, source_target_pairs={{0,64},{16,80},{32,96},{48,112},{64,0},{80,16},{96,32},{112,48},{1... | collective-permute-start | bytes 1572872 | tf_op jit(solution)/shard_map/ppermute | solution.py:60
  91.0 8.0 %collective-permute-start.30 = (bf16[2,256,256]{2,1,0:T(8,128)(2,1)S(1)}, bf16[2,256,256]{2,1,0:T(8,128)(2,1)S(1)}, u32[]{:S(2)}, u32[]{:S(2)}) collective-permute-start(bf16[2,256,256]{2,1,0:T(8,128)(2,1)S(1)} %pad_maximum_fusion.4), channel_id=1, source_target_pairs={{0,8},{1,9},{2,10},{3,11},{4,12},{5,13},{6,14},{7,15},{8,0},{9,1},... | collective-permute-start | bytes 786440 | tf_op jit(solution)/shard_map/ppermute | solution.py:43
  93.3 8.4 %collective-permute-start.31 = (bf16[2,256,256]{2,1,0:T(8,128)(2,1)S(1)}, bf16[2,256,256]{2,1,0:T(8,128)(2,1)S(1)}, u32[]{:S(2)}, u32[]{:S(2)}) collective-permute-start(bf16[2,256,256]{2,1,0:T(8,128)(2,1)S(1)} %pad_maximum_fusion.5), channel_id=1, source_target_pairs={{0,4},{1,5},{2,6},{3,7},{4,8},{5,9},{6,10},{7,11},{8,12},{9,13},{1... | collective-permute-start | bytes 786440 | tf_op jit(solution)/shard_map/ppermute | solution.py:43
  93.4 8.3 %collective-permute-start.29 = (bf16[2,256,256]{2,1,0:T(8,128)(2,1)S(1)}, bf16[2,256,256]{2,1,0:T(8,128)(2,1)S(1)}, u32[]{:S(2)}, u32[]{:S(2)}) collective-permute-start(bf16[2,256,256]{2,1,0:T(8,128)(2,1)S(1)} %pad_maximum_fusion.3), channel_id=1, source_target_pairs={{0,12},{1,13},{2,14},{3,15},{4,0},{5,1},{6,2},{7,3},{8,4},{9,5},{1... | collective-permute-start | bytes 786440 | tf_op jit(solution)/shard_map/ppermute | solution.py:43
  (14 other events, 92.6 us)

commit v6 on v5

--- a/solution.py
+++ b/solution.py
@@ -274,10 +274,10 @@
     return (a.astype(WIDE) + b.astype(WIDE)).astype(HALF)
 
 
-def seq_exchange(own, earlier):
+def seq_exchange(own, earlier, first):
     x, core = lax.axis_index("x"), lax.axis_index("core")
     other = core_swap(own)
-    pair = rounded_sum(own, other)
+    pair = after(first, rounded_sum(own, other))
     near = x_partner(pair, (1, 1))
     four = rounded_sum(pair, near)
     far = x_partner(four, (2, 2))
@@ -321,8 +321,6 @@
     mixed = mm(scores, values, NN) + mm(query, prior, NN)
     inv_norm = lax.rsqrt(jnp.mean(mixed * mixed, axis=-1, keepdims=True) + EPSILON)
     normed = (mixed * inv_norm).astype(HALF)
-    out_terms = [part_terms(w_o, d, normed) for d in range(SIDE)]
-    out_got = fold_phase1(out_terms)
 
     grad_normed = sum(mm(g, w, TN) for g, w in zip(g_parts, wo_parts))
     grad_mixed = inv_norm * (
@@ -331,10 +329,11 @@
     )
     grad_mixed = grad_mixed.astype(HALF)
     own_back = mm(query, grad_mixed, TN).astype(HALF)
+    out_terms = [part_terms(w_o, d, after(own_back, normed)) for d in range(SIDE)]
+    out_got = fold_phase1(out_terms)
     half = SIDE * SIDE // 2
     t_sorted, g_sorted = sort_blocks(slots, t_parts), sort_blocks(slots, g_parts)
-    own_back = after(out_terms, own_back)
-    behind, halves, _ = seq_exchange(own_back, False)
+    behind, halves, _ = seq_exchange(own_back, False, out_terms)
     t_other, g_other = (core_swap(after(halves[0], a[half:])) for a in (t_sorted, g_sorted))
 
     grad_scores = jnp.where(allowed, mm(grad_mixed, values, NT), 0.0).astype(HALF)
@@ -358,9 +357,10 @@
     own, send = mine[0], mine[1]
     in_got = after((own, send), in_got)
     got = fold_phase2((out_sum, total(in_got).astype(HALF)))
+    grads = split_sum(after(got[1], own), x_partner(send, (2, 2)))
+    got[3] = after(grads, got[3])
     result = total([g[0] for g in got]).astype(HALF)
     grad_tokens = total([g[1] for g in got])
-    grads = split_sum(after((result, grad_tokens), own), x_partner(send, (2, 2)))
     return (
         result,
         grad_tokens,

time: 104 us -> 103 us (level)
  starting transfers between devices: 49 us -> 47.2 us
    ppermute x4, waiting for transfers between devices: 14.5 us -> 19.3 us  [x_partner(): return lax.ppermute(a, SEQ, pairs)]
    ppermute x21, waiting for transfers between devices: 14.9 us -> 11.9 us  [plane_shift(): return lax.ppermute(a, PLANE, plane_pairs(phase, shift))]
    ppermute x21, starting transfers between devices: 39.8 us -> 37.5 us  [plane_shift(): return lax.ppermute(a, PLANE, plane_pairs(phase, shift))]
  transfers between devices with their start and end apart: 33 -> 33, of which waited for: 12 -> 12; matrix products, arithmetic and copies ran while one was open for 9% -> 8% of each run, Pallas kernels for 4% -> 7%
where the time goes in v6:
time: 103 us
  starting transfers between devices  47.2 us (46%)
  waiting for transfers between devices  31.5 us (31%)
  Pallas kernels  8.59 us (8%)
  matrix products  5.51 us (5%)
  local copies, waits for them, and re-layouts  4.88 us (5%)
  other arithmetic  3.76 us (4%)
  between operations  1.17 us (1%)
    ppermute x21, starting transfers between devices, plane_shift(): return lax.ppermute(a, PLANE, plane_pairs(phase, shift))  37.5 us
    ppermute x4, waiting for transfers between devices, x_partner(): return lax.ppermute(a, SEQ, pairs)  19.3 us
    ppermute x21, waiting for transfers between devices, plane_shift(): return lax.ppermute(a, PLANE, plane_pairs(phase, shift))  11.9 us
    dot_general x20, matrix products, mm(): return lax.dot_general(a, b, dims, preferred_element_type=WIDE)  5.51 us
    unnamed x12, local copies, waits for them, and re-layouts  4.61 us
    ppermute x4, starting transfers between devices, x_partner(): return lax.ppermute(a, SEQ, pairs)  4.59 us
    ppermute x1, starting transfers between devices, x_shift(): return lax.ppermute(a, 'x', [(i, (i + shift) % SIDE) for i in range(SIDE)])  3.1 us
    pallas_call x8, Pallas kernels, part_terms(): pl.pallas_call(part_terms_kernel, out_shape=jax.ShapeDtypeStruct((SIDE *...  3.08 us
  transfers between devices with their start and end apart: 33, of which 12 were waited for; matrix products, arithmetic and copies ran while one was open for 8% of the time, Pallas kernels for 7%

profile of v6, /device:TPU:0, one launch (start us, length us, event | category | flops | bytes accessed | tf_op | source)
XLA Modules:
  0.0 102.6 jit_solution(3336851174677838986)
XLA Ops:
  1.8 3.2 %collective-permute-start.2 = (bf16[256,256]{1,0:T(8,128)(2,1)S(1)}, bf16[256,256]{1,0:T(8,128)(2,1)S(1)}, u32[]{:S(2)}, u32[]{:S(2)}) collective-permute-start(bf16[256,256]{1,0:T(8,128)(2,1)S(1)} %bitcast.72), channel_id=1, source_target_pairs={{0,12},{1,13},{2,14},{3,15},{4,0},{5,1},{6,2},{7,3},{8,4},{9,5},{1... | collective-permute-start | bytes 393224 | tf_op jit(solution)/shard_map/ppermute | solution.py:43
  7.6 2.3 %collective-permute-start.12 = (bf16[256,256]{1,0:T(8,128)(2,1)S(1)}, bf16[256,256]{1,0:T(8,128)(2,1)S(1)}, u32[]{:S(2)}, u32[]{:S(2)}) collective-permute-start(bf16[256,256]{1,0:T(8,128)(2,1)S(1)} %bitcast.68), channel_id=1, source_target_pairs={{0,12},{1,13},{2,14},{3,15},{4,0},{5,1},{6,2},{7,3},{8,4},{9,5},{1... | collective-permute-start | bytes 393224 | tf_op jit(solution)/shard_map/ppermute | solution.py:43
  9.9 1.7 %collective-permute-start.11 = (bf16[256,256]{1,0:T(8,128)(2,1)S(1)}, bf16[256,256]{1,0:T(8,128)(2,1)S(1)}, u32[]{:S(2)}, u32[]{:S(2)}) collective-permute-start(bf16[256,256]{1,0:T(8,128)(2,1)S(1)} %bitcast.69), channel_id=1, source_target_pairs={{0,8},{1,9},{2,10},{3,11},{4,12},{5,13},{6,14},{7,15},{8,0},{9,1},... | collective-permute-start | bytes 393224 | tf_op jit(solution)/shard_map/ppermute | solution.py:43
  12.9 4.1 %collective-permute-start.5 = (bf16[1024,256]{1,0:T(8,128)(2,1)S(1)}, bf16[1024,256]{1,0:T(8,128)(2,1)S(1)}, u32[]{:S(2)}, u32[]{:S(2)}) collective-permute-start(bf16[1024,256]{1,0:T(8,128)(2,1)S(1)} %pad_maximum_fusion.a0), channel_id=1, source_target_pairs={{0,3},{1,0},{2,1},{3,2},{4,7},{5,4},{6,5},{7,6},{8,11},{9,8},{10,9... | collective-permute-start | bytes 1572872 | tf_op jit(solution)/shard_map/ppermute | solution.py:43
  19.4 9.9 %collective-permute-start.15 = (bf16[1024,256]{1,0:T(8,128)(2,1)S(1)}, bf16[1024,256]{1,0:T(8,128)(2,1)S(1)}, u32[]{:S(2)}, u32[]{:S(2)}) collective-permute-start(bf16[1024,256]{1,0:T(8,128)(2,1)S(1)} %pad_maximum_fusion.1.a0), channel_id=1, source_target_pairs={{0,3},{1,0},{2,1},{3,2},{4,7},{5,4},{6,5},{7,6},{8,11},{9,8},{10,9... | collective-permute-start | bytes 1572872 | tf_op jit(solution)/shard_map/ppermute | solution.py:43
  33.7 1.4 %collective-permute-start.13 = (bf16[1024,256]{1,0:T(8,128)(2,1)S(1)}, bf16[1024,256]{1,0:T(8,128)(2,1)S(1)}, u32[]{:S(2)}, u32[]{:S(2)}) collective-permute-start(bf16[1024,256]{1,0:T(8,128)(2,1)S(1)} %pad_maximum_fusion.1.a0), channel_id=1, source_target_pairs={{0,1},{1,2},{2,3},{3,0},{4,5},{5,6},{6,7},{7,4},{8,9},{9,10},{10,1... | collective-permute-start | bytes 1572872 | tf_op jit(solution)/shard_map/ppermute | solution.py:43
  38.0 3.1 %collective-permute-start.8 = (bf16[128,128]{1,0:T(8,128)(2,1)S(1)}, bf16[128,128]{1,0:T(8,128)(2,1)S(1)}, u32[]{:S(2)}, u32[]{:S(2)}) collective-permute-start(bf16[128,128]{1,0:T(8,128)(2,1)S(1)} %fusion.28), channel_id=1, source_target_pairs={{0,64},{32,96},{64,0},{96,32},{1,65},{33,97},{65,1},{97,33},{2,66}... | collective-permute-start | bytes 98312 | tf_op jit(solution)/shard_map/ppermute | solution.py:47
  41.8 3.8 %collective-permute-done.13.a1 = bf16[1024,256]{1,0:T(8,128)(2,1)S(1)} collective-permute-done((bf16[1024,256]{1,0:T(8,128)(2,1)S(1)}, bf16[1024,256]{1,0:T(8,128)(2,1)S(1)}, u32[]{:S(2)}, u32[]{:S(2)}) %collective-permute-start.13) | collective-permute-done | bytes 524320 | tf_op jit(solution)/shard_map/ppermute | solution.py:43
  50.6 1.6 %collective-permute-start.19 = (bf16[1024,256]{1,0:T(8,128)(2,1)S(1)}, bf16[1024,256]{1,0:T(8,128)(2,1)S(1)}, u32[]{:S(2)}, u32[]{:S(2)}) collective-permute-start(bf16[1024,256]{1,0:T(8,128)(2,1)S(1)} %part_terms.9), channel_id=1, source_target_pairs={{0,3},{1,0},{2,1},{3,2},{4,7},{5,4},{6,5},{7,6},{8,11},{9,8},{10,9... | collective-permute-start | bytes 1572872 | tf_op jit(solution)/shard_map/ppermute | solution.py:43
  52.1 2.1 %collective-permute-start.20 = (bf16[1024,256]{1,0:T(8,128)(2,1)S(1)}, bf16[1024,256]{1,0:T(8,128)(2,1)S(1)}, u32[]{:S(2)}, u32[]{:S(2)}) collective-permute-start(bf16[1024,256]{1,0:T(8,128)(2,1)S(1)} %part_terms.10), channel_id=1, source_target_pairs={{0,2},{1,3},{2,0},{3,1},{4,6},{5,7},{6,4},{7,5},{8,10},{9,11},{10,... | collective-permute-start | bytes 1572872 | tf_op jit(solution)/shard_map/ppermute | solution.py:43
  55.1 3.7 %collective-permute-done.17 = bf16[128,128]{1,0:T(8,128)(2,1)S(1)} collective-permute-done((bf16[128,128]{1,0:T(8,128)(2,1)S(1)}, bf16[128,128]{1,0:T(8,128)(2,1)S(1)}, u32[]{:S(2)}, u32[]{:S(2)}) %collective-permute-start.17) | collective-permute-done | bytes 32800 | tf_op jit(solution)/shard_map/ppermute | solution.py:60
  58.7 1.7 %collective-permute-start.18 = (bf16[128,128]{1,0:T(8,128)(2,1)S(1)}, bf16[128,128]{1,0:T(8,128)(2,1)S(1)}, u32[]{:S(2)}, u32[]{:S(2)}) collective-permute-start(bf16[128,128]{1,0:T(8,128)(2,1)S(1)} %fusion.33), channel_id=1, source_target_pairs={{0,64},{16,80},{32,96},{48,112},{64,0},{80,16},{96,32},{112,48},{1... | collective-permute-start | bytes 98312 | tf_op jit(solution)/shard_map/ppermute | solution.py:60
  60.8 3.4 %collective-permute-done.18 = bf16[128,128]{1,0:T(8,128)(2,1)S(1)} collective-permute-done((bf16[128,128]{1,0:T(8,128)(2,1)S(1)}, bf16[128,128]{1,0:T(8,128)(2,1)S(1)}, u32[]{:S(2)}, u32[]{:S(2)}) %collective-permute-start.18) | collective-permute-done | bytes 32800 | tf_op jit(solution)/shard_map/ppermute | solution.py:60
  65.9 2.6 %collective-permute-done.21 = bf16[1024,256]{1,0:T(8,128)(2,1)S(1)} collective-permute-done((bf16[1024,256]{1,0:T(8,128)(2,1)S(1)}, bf16[1024,256]{1,0:T(8,128)(2,1)S(1)}, u32[]{:S(2)}, u32[]{:S(2)}) %collective-permute-start.21) | collective-permute-done | bytes 524320 | tf_op jit(solution)/shard_map/ppermute | solution.py:43
  68.8 1.8 %weight_grads.1 = (bf16[4,256,512]{2,1,0:T(8,128)(2,1)S(1)}, bf16[4,256,512]{2,1,0:T(8,128)(2,1)S(1)}) custom-call(bf16[16,256,256]{2,1,0:T(8,128)(2,1)S(1)} %sort_blocks.2.t_own, bf16[8,256,256]{2,1,0:T(8,128)(2,1)S(1)} %collective-permute-done.22.t_other, bf16[16,256,256]{2,1,0:T(8,128)(2,1)S(1)} %sort_blocks.3.g_own, ...), custom_call_target="tpu_custom_call" | custom-call | flops 1073741824 | bytes 6291456 | tf_op jit(solution)/shard_map/weight_grads/pallas_call | solution.py:157
  71.7 1.3 %collective-permute-start.26 = (bf16[1024,256]{1,0:T(8,128)(2,1)S(1)}, bf16[1024,256]{1,0:T(8,128)(2,1)S(1)}, u32[]{:S(2)}, u32[]{:S(2)}) collective-permute-start(bf16[1024,256]{1,0:T(8,128)(2,1)S(1)} %part_terms.13), channel_id=1, source_target_pairs={{0,3},{1,0},{2,1},{3,2},{4,7},{5,4},{6,5},{7,6},{8,11},{9,8},{10,9... | collective-permute-start | bytes 1572872 | tf_op jit(solution)/shard_map/ppermute | solution.py:43
  74.9 1.4 %collective-permute-start.28 = (bf16[1024,256]{1,0:T(8,128)(2,1)S(1)}, bf16[1024,256]{1,0:T(8,128)(2,1)S(1)}, u32[]{:S(2)}, u32[]{:S(2)}) collective-permute-start(bf16[1024,256]{1,0:T(8,128)(2,1)S(1)} %part_terms.15), channel_id=1, source_target_pairs={{0,1},{1,2},{2,3},{3,0},{4,5},{5,6},{6,7},{7,4},{8,9},{9,10},{10,1... | collective-permute-start | bytes 1572872 | tf_op jit(solution)/shard_map/ppermute | solution.py:43
  76.8 8.6 %collective-permute-done.25 = bf16[4,256,512]{2,1,0:T(8,128)(2,1)S(1)} collective-permute-done((bf16[4,256,512]{2,1,0:T(8,128)(2,1)S(1)}, bf16[4,256,512]{2,1,0:T(8,128)(2,1)S(1)}, u32[]{:S(2)}, u32[]{:S(2)}) %collective-permute-start.25) | collective-permute-done | bytes 1048608 | tf_op jit(solution)/shard_map/ppermute | solution.py:60
  85.8 2.1 %collective-permute-start.31 = (bf16[512,512]{1,0:T(8,128)(2,1)S(1)}, bf16[512,512]{1,0:T(8,128)(2,1)S(1)}, u32[]{:S(2)}, u32[]{:S(2)}) collective-permute-start(bf16[512,512]{1,0:T(8,128)(2,1)S(1)} %bitcast.67), channel_id=1, source_target_pairs={{0,64},{16,80},{32,96},{48,112},{64,0},{80,16},{96,32},{112,48},{1... | collective-permute-start | bytes 1572872 | tf_op jit(solution)/shard_map/ppermute | solution.py:60
  88.0 1.9 %collective-permute-done.28 = bf16[1024,256]{1,0:T(8,128)(2,1)S(1)} collective-permute-done((bf16[1024,256]{1,0:T(8,128)(2,1)S(1)}, bf16[1024,256]{1,0:T(8,128)(2,1)S(1)}, u32[]{:S(2)}, u32[]{:S(2)}) %collective-permute-start.28) | collective-permute-done | bytes 524320 | tf_op jit(solution)/shard_map/ppermute | solution.py:43
  90.9 1.5 %collective-permute-start.32 = (bf16[2,256,256]{2,1,0:T(8,128)(2,1)S(1)}, bf16[2,256,256]{2,1,0:T(8,128)(2,1)S(1)}, u32[]{:S(2)}, u32[]{:S(2)}) collective-permute-start(bf16[2,256,256]{2,1,0:T(8,128)(2,1)S(1)} %pad_maximum_fusion.5), channel_id=1, source_target_pairs={{0,4},{1,5},{2,6},{3,7},{4,8},{5,9},{6,10},{7,11},{8,12},{9,13},{1... | collective-permute-start | bytes 786440 | tf_op jit(solution)/shard_map/ppermute | solution.py:43
  92.4 2.3 %collective-permute-start.30 = (bf16[2,256,256]{2,1,0:T(8,128)(2,1)S(1)}, bf16[2,256,256]{2,1,0:T(8,128)(2,1)S(1)}, u32[]{:S(2)}, u32[]{:S(2)}) collective-permute-start(bf16[2,256,256]{2,1,0:T(8,128)(2,1)S(1)} %pad_maximum_fusion.4), channel_id=1, source_target_pairs={{0,8},{1,9},{2,10},{3,11},{4,12},{5,13},{6,14},{7,15},{8,0},{9,1},... | collective-permute-start | bytes 786440 | tf_op jit(solution)/shard_map/ppermute | solution.py:43
  94.7 1.9 %collective-permute-done.29 = bf16[2,256,256]{2,1,0:T(8,128)(2,1)S(1)} collective-permute-done((bf16[2,256,256]{2,1,0:T(8,128)(2,1)S(1)}, bf16[2,256,256]{2,1,0:T(8,128)(2,1)S(1)}, u32[]{:S(2)}, u32[]{:S(2)}) %collective-permute-start.29) | collective-permute-done | bytes 262176 | tf_op jit(solution)/shard_map/ppermute | solution.py:43
  96.6 3.6 %collective-permute-done.31.got = bf16[512,512]{1,0:T(8,128)(2,1)S(1)} collective-permute-done((bf16[512,512]{1,0:T(8,128)(2,1)S(1)}, bf16[512,512]{1,0:T(8,128)(2,1)S(1)}, u32[]{:S(2)}, u32[]{:S(2)}) %collective-permute-start.31) | collective-permute-done | bytes 524320 | tf_op jit(solution)/shard_map/ppermute | solution.py:60
  (111 shorter events, 30.6 us)
Async XLA Ops:
  1.8 9.8 %collective-permute-start.2 = (bf16[256,256]{1,0:T(8,128)(2,1)S(1)}, bf16[256,256]{1,0:T(8,128)(2,1)S(1)}, u32[]{:S(2)}, u32[]{:S(2)}) collective-permute-start(bf16[256,256]{1,0:T(8,128)(2,1)S(1)} %bitcast.72), channel_id=1, source_target_pairs={{0,12},{1,13},{2,14},{3,15},{4,0},{5,1},{6,2},{7,3},{8,4},{9,5},{1... | collective-permute-start | bytes 393224 | tf_op jit(solution)/shard_map/ppermute | solution.py:43
  5.0 6.6 %collective-permute-start.1 = (bf16[256,256]{1,0:T(8,128)(2,1)S(1)}, bf16[256,256]{1,0:T(8,128)(2,1)S(1)}, u32[]{:S(2)}, u32[]{:S(2)}) collective-permute-start(bf16[256,256]{1,0:T(8,128)(2,1)S(1)} %bitcast.73), channel_id=1, source_target_pairs={{0,8},{1,9},{2,10},{3,11},{4,12},{5,13},{6,14},{7,15},{8,0},{9,1},... | collective-permute-start | bytes 393224 | tf_op jit(solution)/shard_map/ppermute | solution.py:43
  5.6 7.2 %collective-permute-start = (bf16[256,256]{1,0:T(8,128)(2,1)S(1)}, bf16[256,256]{1,0:T(8,128)(2,1)S(1)}, u32[]{:S(2)}, u32[]{:S(2)}) collective-permute-start(bf16[256,256]{1,0:T(8,128)(2,1)S(1)} %bitcast.74), channel_id=1, source_target_pairs={{0,4},{1,5},{2,6},{3,7},{4,8},{5,9},{6,10},{7,11},{8,12},{9,13},{1... | collective-permute-start | bytes 393224 | tf_op jit(solution)/shard_map/ppermute | solution.py:43
  7.6 9.6 %collective-permute-start.12 = (bf16[256,256]{1,0:T(8,128)(2,1)S(1)}, bf16[256,256]{1,0:T(8,128)(2,1)S(1)}, u32[]{:S(2)}, u32[]{:S(2)}) collective-permute-start(bf16[256,256]{1,0:T(8,128)(2,1)S(1)} %bitcast.68), channel_id=1, source_target_pairs={{0,12},{1,13},{2,14},{3,15},{4,0},{5,1},{6,2},{7,3},{8,4},{9,5},{1... | collective-permute-start | bytes 393224 | tf_op jit(solution)/shard_map/ppermute | solution.py:43
  9.9 8.5 %collective-permute-start.11 = (bf16[256,256]{1,0:T(8,128)(2,1)S(1)}, bf16[256,256]{1,0:T(8,128)(2,1)S(1)}, u32[]{:S(2)}, u32[]{:S(2)}) collective-permute-start(bf16[256,256]{1,0:T(8,128)(2,1)S(1)} %bitcast.69), channel_id=1, source_target_pairs={{0,8},{1,9},{2,10},{3,11},{4,12},{5,13},{6,14},{7,15},{8,0},{9,1},... | collective-permute-start | bytes 393224 | tf_op jit(solution)/shard_map/ppermute | solution.py:43
  11.6 6.8 %collective-permute-start.10 = (bf16[256,256]{1,0:T(8,128)(2,1)S(1)}, bf16[256,256]{1,0:T(8,128)(2,1)}, u32[]{:S(2)}, u32[]{:S(2)}) collective-permute-start(bf16[256,256]{1,0:T(8,128)(2,1)S(1)} %bitcast.70), channel_id=1, source_target_pairs={{0,4},{1,5},{2,6},{3,7},{4,8},{5,9},{6,10},{7,11},{8,12},{9,13},{1... | collective-permute-start | bytes 393224 | tf_op jit(solution)/shard_map/ppermute | solution.py:43
  12.9 20.8 %collective-permute-start.5 = (bf16[1024,256]{1,0:T(8,128)(2,1)S(1)}, bf16[1024,256]{1,0:T(8,128)(2,1)S(1)}, u32[]{:S(2)}, u32[]{:S(2)}) collective-permute-start(bf16[1024,256]{1,0:T(8,128)(2,1)S(1)} %pad_maximum_fusion.a0), channel_id=1, source_target_pairs={{0,3},{1,0},{2,1},{3,2},{4,7},{5,4},{6,5},{7,6},{8,11},{9,8},{10,9... | collective-permute-start | bytes 1572872 | tf_op jit(solution)/shard_map/ppermute | solution.py:43
  17.1 19.0 %collective-permute-start.4 = (bf16[1024,256]{1,0:T(8,128)(2,1)S(1)}, bf16[1024,256]{1,0:T(8,128)(2,1)S(1)}, u32[]{:S(2)}, u32[]{:S(2)}) collective-permute-start(bf16[1024,256]{1,0:T(8,128)(2,1)S(1)} %pad_maximum_fusion.a0), channel_id=1, source_target_pairs={{0,2},{1,3},{2,0},{3,1},{4,6},{5,7},{6,4},{7,5},{8,10},{9,11},{10,... | collective-permute-start | bytes 1572872 | tf_op jit(solution)/shard_map/ppermute | solution.py:43
  17.2 18.4 %collective-permute-start.3 = (bf16[1024,256]{1,0:T(8,128)(2,1)S(1)}, bf16[1024,256]{1,0:T(8,128)(2,1)S(1)}, u32[]{:S(2)}, u32[]{:S(2)}) collective-permute-start(bf16[1024,256]{1,0:T(8,128)(2,1)S(1)} %pad_maximum_fusion.a0), channel_id=1, source_target_pairs={{0,1},{1,2},{2,3},{3,0},{4,5},{5,6},{6,7},{7,4},{8,9},{9,10},{10,1... | collective-permute-start | bytes 1572872 | tf_op jit(solution)/shard_map/ppermute | solution.py:43
  19.4 22.4 %collective-permute-start.15 = (bf16[1024,256]{1,0:T(8,128)(2,1)S(1)}, bf16[1024,256]{1,0:T(8,128)(2,1)S(1)}, u32[]{:S(2)}, u32[]{:S(2)}) collective-permute-start(bf16[1024,256]{1,0:T(8,128)(2,1)S(1)} %pad_maximum_fusion.1.a0), channel_id=1, source_target_pairs={{0,3},{1,0},{2,1},{3,2},{4,7},{5,4},{6,5},{7,6},{8,11},{9,8},{10,9... | collective-permute-start | bytes 1572872 | tf_op jit(solution)/shard_map/ppermute | solution.py:43
  29.2 12.5 %collective-permute-start.14 = (bf16[1024,256]{1,0:T(8,128)(2,1)S(1)}, bf16[1024,256]{1,0:T(8,128)(2,1)S(1)}, u32[]{:S(2)}, u32[]{:S(2)}) collective-permute-start(bf16[1024,256]{1,0:T(8,128)(2,1)S(1)} %pad_maximum_fusion.1.a0), channel_id=1, source_target_pairs={{0,2},{1,3},{2,0},{3,1},{4,6},{5,7},{6,4},{7,5},{8,10},{9,11},{10,... | collective-permute-start | bytes 1572872 | tf_op jit(solution)/shard_map/ppermute | solution.py:43
  33.7 11.8 %collective-permute-start.13 = (bf16[1024,256]{1,0:T(8,128)(2,1)S(1)}, bf16[1024,256]{1,0:T(8,128)(2,1)S(1)}, u32[]{:S(2)}, u32[]{:S(2)}) collective-permute-start(bf16[1024,256]{1,0:T(8,128)(2,1)S(1)} %pad_maximum_fusion.1.a0), channel_id=1, source_target_pairs={{0,1},{1,2},{2,3},{3,0},{4,5},{5,6},{6,7},{7,4},{8,9},{9,10},{10,1... | collective-permute-start | bytes 1572872 | tf_op jit(solution)/shard_map/ppermute | solution.py:43
  38.0 8.5 %collective-permute-start.8 = (bf16[128,128]{1,0:T(8,128)(2,1)S(1)}, bf16[128,128]{1,0:T(8,128)(2,1)S(1)}, u32[]{:S(2)}, u32[]{:S(2)}) collective-permute-start(bf16[128,128]{1,0:T(8,128)(2,1)S(1)} %fusion.28), channel_id=1, source_target_pairs={{0,64},{32,96},{64,0},{96,32},{1,65},{33,97},{65,1},{97,33},{2,66}... | collective-permute-start | bytes 98312 | tf_op jit(solution)/shard_map/ppermute | solution.py:47
  50.6 14.7 %collective-permute-start.19 = (bf16[1024,256]{1,0:T(8,128)(2,1)S(1)}, bf16[1024,256]{1,0:T(8,128)(2,1)S(1)}, u32[]{:S(2)}, u32[]{:S(2)}) collective-permute-start(bf16[1024,256]{1,0:T(8,128)(2,1)S(1)} %part_terms.9), channel_id=1, source_target_pairs={{0,3},{1,0},{2,1},{3,2},{4,7},{5,4},{6,5},{7,6},{8,11},{9,8},{10,9... | collective-permute-start | bytes 1572872 | tf_op jit(solution)/shard_map/ppermute | solution.py:43
  52.1 13.7 %collective-permute-start.20 = (bf16[1024,256]{1,0:T(8,128)(2,1)S(1)}, bf16[1024,256]{1,0:T(8,128)(2,1)S(1)}, u32[]{:S(2)}, u32[]{:S(2)}) collective-permute-start(bf16[1024,256]{1,0:T(8,128)(2,1)S(1)} %part_terms.10), channel_id=1, source_target_pairs={{0,2},{1,3},{2,0},{3,1},{4,6},{5,7},{6,4},{7,5},{8,10},{9,11},{10,... | collective-permute-start | bytes 1572872 | tf_op jit(solution)/shard_map/ppermute | solution.py:43
  54.2 14.2 %collective-permute-start.21 = (bf16[1024,256]{1,0:T(8,128)(2,1)S(1)}, bf16[1024,256]{1,0:T(8,128)(2,1)S(1)}, u32[]{:S(2)}, u32[]{:S(2)}) collective-permute-start(bf16[1024,256]{1,0:T(8,128)(2,1)S(1)} %part_terms.11), channel_id=1, source_target_pairs={{0,1},{1,2},{2,3},{3,0},{4,5},{5,6},{6,7},{7,4},{8,9},{9,10},{10,1... | collective-permute-start | bytes 1572872 | tf_op jit(solution)/shard_map/ppermute | solution.py:43
  60.7 8.0 %collective-permute-start.23 = (bf16[8,256,256]{2,1,0:T(8,128)(2,1)S(1)}, bf16[8,256,256]{2,1,0:T(8,128)(2,1)S(1)}, u32[]{:S(2)}, u32[]{:S(2)}) collective-permute-start(bf16[8,256,256]{2,1,0:T(8,128)(2,1)S(1)} %slice.122), channel_id=1, source_target_pairs={{0,16},{16,0},{1,17},{17,1},{2,18},{18,2},{3,19},{19,3},{4,20},{20... | collective-permute-start | bytes 3145736 | tf_op jit(solution)/shard_map/ppermute | solution.py:64
  70.6 14.9 %collective-permute-start.25 = (bf16[4,256,512]{2,1,0:T(8,128)(2,1)S(1)}, bf16[4,256,512]{2,1,0:T(8,128)(2,1)S(1)}, u32[]{:S(2)}, u32[]{:S(2)}) collective-permute-start(bf16[4,256,512]{2,1,0:T(8,128)(2,1)S(1)} %get-tuple-element.58), channel_id=1, source_target_pairs={{0,32},{16,112},{32,0},{48,80},{64,96},{80,48},{96,64},{112,16},{1... | collective-permute-start | bytes 3145736 | tf_op jit(solution)/shard_map/ppermute | solution.py:60
  71.7 16.3 %collective-permute-start.26 = (bf16[1024,256]{1,0:T(8,128)(2,1)S(1)}, bf16[1024,256]{1,0:T(8,128)(2,1)S(1)}, u32[]{:S(2)}, u32[]{:S(2)}) collective-permute-start(bf16[1024,256]{1,0:T(8,128)(2,1)S(1)} %part_terms.13), channel_id=1, source_target_pairs={{0,3},{1,0},{2,1},{3,2},{4,7},{5,4},{6,5},{7,6},{8,11},{9,8},{10,9... | collective-permute-start | bytes 1572872 | tf_op jit(solution)/shard_map/ppermute | solution.py:43
  73.4 14.5 %collective-permute-start.27 = (bf16[1024,256]{1,0:T(8,128)(2,1)S(1)}, bf16[1024,256]{1,0:T(8,128)(2,1)S(1)}, u32[]{:S(2)}, u32[]{:S(2)}) collective-permute-start(bf16[1024,256]{1,0:T(8,128)(2,1)S(1)} %part_terms.14), channel_id=1, source_target_pairs={{0,2},{1,3},{2,0},{3,1},{4,6},{5,7},{6,4},{7,5},{8,10},{9,11},{10,... | collective-permute-start | bytes 1572872 | tf_op jit(solution)/shard_map/ppermute | solution.py:43
  74.9 14.9 %collective-permute-start.28 = (bf16[1024,256]{1,0:T(8,128)(2,1)S(1)}, bf16[1024,256]{1,0:T(8,128)(2,1)S(1)}, u32[]{:S(2)}, u32[]{:S(2)}) collective-permute-start(bf16[1024,256]{1,0:T(8,128)(2,1)S(1)} %part_terms.15), channel_id=1, source_target_pairs={{0,1},{1,2},{2,3},{3,0},{4,5},{5,6},{6,7},{7,4},{8,9},{9,10},{10,1... | collective-permute-start | bytes 1572872 | tf_op jit(solution)/shard_map/ppermute | solution.py:43
  85.8 14.4 %collective-permute-start.31 = (bf16[512,512]{1,0:T(8,128)(2,1)S(1)}, bf16[512,512]{1,0:T(8,128)(2,1)S(1)}, u32[]{:S(2)}, u32[]{:S(2)}) collective-permute-start(bf16[512,512]{1,0:T(8,128)(2,1)S(1)} %bitcast.67), channel_id=1, source_target_pairs={{0,64},{16,80},{32,96},{48,112},{64,0},{80,16},{96,32},{112,48},{1... | collective-permute-start | bytes 1572872 | tf_op jit(solution)/shard_map/ppermute | solution.py:60
  90.9 10.4 %collective-permute-start.32 = (bf16[2,256,256]{2,1,0:T(8,128)(2,1)S(1)}, bf16[2,256,256]{2,1,0:T(8,128)(2,1)S(1)}, u32[]{:S(2)}, u32[]{:S(2)}) collective-permute-start(bf16[2,256,256]{2,1,0:T(8,128)(2,1)S(1)} %pad_maximum_fusion.5), channel_id=1, source_target_pairs={{0,4},{1,5},{2,6},{3,7},{4,8},{5,9},{6,10},{7,11},{8,12},{9,13},{1... | collective-permute-start | bytes 786440 | tf_op jit(solution)/shard_map/ppermute | solution.py:43
  92.4 9.4 %collective-permute-start.30 = (bf16[2,256,256]{2,1,0:T(8,128)(2,1)S(1)}, bf16[2,256,256]{2,1,0:T(8,128)(2,1)S(1)}, u32[]{:S(2)}, u32[]{:S(2)}) collective-permute-start(bf16[2,256,256]{2,1,0:T(8,128)(2,1)S(1)} %pad_maximum_fusion.4), channel_id=1, source_target_pairs={{0,8},{1,9},{2,10},{3,11},{4,12},{5,13},{6,14},{7,15},{8,0},{9,1},... | collective-permute-start | bytes 786440 | tf_op jit(solution)/shard_map/ppermute | solution.py:43
  (14 other events, 98.5 us)
